TPU v7x, 32 devices: a whole 2x2x4 slice. The times are simulated.
32 devices in a mesh: batch: 2 (over y), seq: 16 (over z, x, core).
Axes of the slice: x: 2, y: 2, z: 4, core: 2. Of those that a mesh axis runs over, the one named last changes fastest.
Arguments:
- block_input: bfloat16 [2, 2048, 1536], P('batch', 'seq'), may hold values from -6 to 6
- positions: int32 [2, 2048], P('batch', 'seq'), may hold values from 0 to 3070, as said below
- needle: int32 [2, 2048], P('batch', 'seq'), may hold values 0 or 1
- cotangent: bfloat16 [2, 2048, 1536], P('batch', 'seq'), may hold values from -6 to 6
- norm_gain1: float32 [1536], replicated, may hold values from 0.25 to 1.75
- w_query: bfloat16 [1536, 1536], P('seq'), may hold values from -0.21875 to 0.21875
- w_key: bfloat16 [1536, 1536], P('seq'), may hold values from -0.21875 to 0.21875
- w_value: bfloat16 [1536, 1536], P('seq'), may hold values from -0.15625 to 0.15625
- lam_q1: float32 [12, 64], replicated, may hold values from -0.6 to 0.6
- lam_k1: float32 [12, 64], replicated, may hold values from -0.6 to 0.6
- lam_q2: float32 [12, 64], replicated, may hold values from -0.6 to 0.6
- lam_k2: float32 [12, 64], replicated, may hold values from -0.6 to 0.6
- sub_gain: float32 [128], replicated, may hold values from 0.25 to 1.75
- w_out: bfloat16 [1536, 1536], P('seq'), may hold values from -0.375 to 0.375
- norm_gain2: float32 [1536], replicated, may hold values from 0.25 to 1.75
- w_gate: bfloat16 [1536, 4096], P('seq'), may hold values from -0.15625 to 0.15625
- w_up: bfloat16 [1536, 4096], P('seq'), may hold values from -0.15625 to 0.15625
- w_down: bfloat16 [1536, 4096], P('seq'), may hold values from -0.125 to 0.125
Outputs:
- output: bfloat16 [2, 2048, 1536], P('batch', 'seq')
- input_grad: float32 [2, 2048, 1536], P('batch', 'seq')
- gain1_grad: float32 [1536], replicated
- query_grad: float32 [1536, 1536], P('seq')
- key_grad: float32 [1536, 1536], P('seq')
- value_grad: float32 [1536, 1536], P('seq')
- lam_q1_grad: float32 [12, 64], replicated
- lam_k1_grad: float32 [12, 64], replicated
- lam_q2_grad: float32 [12, 64], replicated
- lam_k2_grad: float32 [12, 64], replicated
- sub_gain_grad: float32 [128], replicated
- out_grad: float32 [1536, 1536], P('seq')
- gain2_grad: float32 [1536], replicated
- gate_grad: float32 [1536, 4096], P('seq')
- up_grad: float32 [1536, 4096], P('seq')
- down_grad: float32 [1536, 4096], P('seq')
- lam_mean: float32 [], replicated
- lam_grad_norm: float32 [], replicated
Inputs may be any that keep to these rules, and one draw needn't show every extreme that they name: Along each sequence the positions start at 0 and rise by 1 or 2 from token to token, by 2 at exactly (2047) // 2 of the steps, so that every sequence ends at the maximum.
All inputs are finite; a program needn't handle non-finite values. No bound on the sum of `needle` on one device may be relied on, other than what follows from the above.
Results may differ from a plain program's by a relative error of at most 0.02.
Values may be sent and summed in bfloat16 or wider, within the bound.
A program may use at most 448 MiB of HBM per device.

v0:
```python
import math

import jax
import jax.numpy as jnp
from jax import lax
from jax.sharding import PartitionSpec as P

lam_init = 0.619
norm_eps = 1e-05
neg_large = -1e30


def rms_norm(value, gain):
    factor = lax.rsqrt(jnp.mean(value * value, axis=-1, keepdims=True) + norm_eps)
    return value * factor * gain


def rotate(value, angles):
    middle = value.shape[-1] // 2
    first_half = value[..., :middle]
    second_half = value[..., middle:]
    cosine = jnp.cos(angles)[:, None, None, :]
    sine = jnp.sin(angles)[:, None, None, :]
    return jnp.concatenate(
        [first_half * cosine - second_half * sine, second_half * cosine + first_half * sine],
        axis=-1,
    )


def lambdas(lam_q1, lam_k1, lam_q2, lam_k2):
    return (
        jnp.exp(jnp.sum(lam_q1 * lam_k1, axis=-1))
        - jnp.exp(jnp.sum(lam_q2 * lam_k2, axis=-1))
        + lam_init
    )


def sub_block(total_rows):
    block_rows = total_rows
    while block_rows > 1024 and block_rows % 2 == 0:
        block_rows = block_rows // 2
    return block_rows


def contract_rows(left_side, right_side):
    return lax.dot_general(
        left_side, right_side, (((0,), (0,)), ((), ())), preferred_element_type=jnp.float32
    )


def contract_cols(left_side, right_side):
    return lax.dot_general(
        left_side, right_side, (((1,), (1,)), ((), ())), preferred_element_type=jnp.float32
    )


def body(
    block_input,
    positions,
    needle,
    cotangent,
    norm_gain1,
    w_query,
    w_key,
    w_value,
    lam_q1,
    lam_k1,
    lam_q2,
    lam_k2,
    sub_gain,
    w_out,
    norm_gain2,
    w_gate,
    w_up,
    w_down,
):
    row_count = block_input.shape[1]
    model_width = block_input.shape[2]
    head_count = lam_q1.shape[0]
    half_size = lam_q1.shape[1]
    value_size = sub_gain.shape[0]
    ffn_width = w_gate.shape[1]
    score_scale = half_size ** (-0.5)
    first_row = lax.axis_index("seq") * row_count
    last_row = first_row + row_count - 1
    own_ids = first_row + jnp.arange(row_count, dtype=jnp.int32)
    tokens = block_input[0].astype(jnp.float32)
    inv_freq = jnp.exp(
        -math.log(10000.0) * jnp.arange(half_size // 2, dtype=jnp.float32) / (half_size // 2)
    )
    angles = positions[0].astype(jnp.float32)[:, None] * inv_freq[None, :]
    w_q, w_k, w_v, w_o = (
        lax.all_gather(w_query, "seq", axis=0, tiled=True),
        lax.all_gather(w_key, "seq", axis=0, tiled=True),
        lax.all_gather(w_value, "seq", axis=0, tiled=True),
        lax.all_gather(w_out, "seq", axis=0, tiled=True),
    )
    normed, norm_one_pull = jax.vjp(rms_norm, tokens, norm_gain1)
    normed_low = normed.astype(jnp.bfloat16)
    query_raw = jnp.dot(normed_low, w_q, preferred_element_type=jnp.float32)
    key_raw = jnp.dot(normed_low, w_k, preferred_element_type=jnp.float32)
    value_low = jnp.dot(normed_low, w_v, preferred_element_type=jnp.float32).astype(jnp.bfloat16)
    query_rot = rotate(query_raw.reshape(row_count, head_count, 2, half_size), angles).astype(
        jnp.bfloat16
    )
    key_rot = rotate(key_raw.reshape(row_count, head_count, 2, half_size), angles).astype(
        jnp.bfloat16
    )
    key_flat = key_rot.reshape(row_count, model_width)
    value_mine = value_low.reshape(row_count, head_count, value_size)
    lam_vals, lam_pull = jax.vjp(lambdas, lam_q1, lam_k1, lam_q2, lam_k2)
    start_state = (
        jnp.full((2, head_count, row_count), neg_large, jnp.float32),
        jnp.zeros((2, head_count, row_count), jnp.float32),
        jnp.zeros((2, head_count, row_count, value_size), jnp.float32),
    )
    running = start_state
    key_piece = lax.all_gather(key_flat, "seq", axis=0, tiled=True)
    value_piece = lax.all_gather(value_low, "seq", axis=0, tiled=True)
    piece_rows = key_piece.shape[0]
    block_rows = sub_block(piece_rows)

    def forward_block_step(state_now, offset):
        block_start = offset

        def forward_compute(state_in):
            maxima, totals, accum = state_in
            key_blk = lax.dynamic_slice_in_dim(key_piece, offset, block_rows, 0).reshape(
                block_rows, head_count, 2, half_size
            )
            value_blk = lax.dynamic_slice_in_dim(value_piece, offset, block_rows, 0).reshape(
                block_rows, head_count, value_size
            )
            key_ids = block_start + jnp.arange(block_rows, dtype=jnp.int32)
            allowed = key_ids[None, :] <= own_ids[:, None]
            new_max, new_tot, new_acc = ([], [], [])
            for map_index in range(2):
                scores = (
                    jnp.einsum(
                        "qhd,khd->hqk",
                        query_rot[:, :, map_index],
                        key_blk[:, :, map_index],
                        preferred_element_type=jnp.float32,
                    )
                    * score_scale
                )
                scores = jnp.where(allowed[None], scores, neg_large)
                highest = jnp.maximum(maxima[map_index], jnp.max(scores, axis=-1))
                weights = jnp.where(allowed[None], jnp.exp(scores - highest[..., None]), 0.0)
                rescale = jnp.exp(maxima[map_index] - highest)
                new_tot.append(totals[map_index] * rescale + jnp.sum(weights, axis=-1))
                product = jnp.einsum(
                    "hqk,khe->hqe",
                    weights.astype(jnp.bfloat16),
                    value_blk,
                    preferred_element_type=jnp.float32,
                )
                new_acc.append(accum[map_index] * rescale[..., None] + product)
                new_max.append(highest)
            return (jnp.stack(new_max), jnp.stack(new_tot), jnp.stack(new_acc))

        state_now = lax.cond(
            block_start > last_row, lambda unchanged: unchanged, forward_compute, state_now
        )
        return (state_now, None)

    offsets = jnp.arange(piece_rows // block_rows, dtype=jnp.int32) * block_rows
    running, _ = lax.scan(forward_block_step, running, offsets)
    maxima, totals, accum = running
    map_outs = accum / totals[..., None]
    log_sums = maxima + jnp.log(totals)
    mixed = map_outs[0] - lam_vals[:, None, None] * map_outs[1]

    def sub_norm(mixed_in, gain_in):
        return rms_norm(mixed_in, gain_in) * (1.0 - lam_init)

    attended, sub_pull = jax.vjp(sub_norm, mixed, sub_gain)
    attended_low = attended.transpose(1, 0, 2).reshape(row_count, model_width).astype(jnp.bfloat16)
    resid = tokens + jnp.dot(attended_low, w_o, preferred_element_type=jnp.float32)
    w_g, w_u, w_d = (
        lax.all_gather(w_gate, "seq", axis=0, tiled=True),
        lax.all_gather(w_up, "seq", axis=0, tiled=True),
        lax.all_gather(w_down, "seq", axis=0, tiled=True),
    )
    normed_two, norm_two_pull = jax.vjp(rms_norm, resid, norm_gain2)
    normed_two_low = normed_two.astype(jnp.bfloat16)
    gate = jnp.dot(normed_two_low, w_g, preferred_element_type=jnp.float32)
    upper = jnp.dot(normed_two_low, w_u, preferred_element_type=jnp.float32)
    activation, act_pull = jax.vjp(
        lambda gate_in, upper_in: jax.nn.silu(gate_in) * upper_in, gate, upper
    )
    inner = activation.astype(jnp.bfloat16)
    result = resid + contract_cols(inner, w_d)
    output = result.astype(jnp.bfloat16)[None]
    grad_out = cotangent[0].astype(jnp.float32) * needle[0].astype(jnp.float32)[:, None]
    grad_low = grad_out.astype(jnp.bfloat16)
    w_g, w_u, w_d = (
        lax.all_gather(w_gate, "seq", axis=0, tiled=True),
        lax.all_gather(w_up, "seq", axis=0, tiled=True),
        lax.all_gather(w_down, "seq", axis=0, tiled=True),
    )
    grad_inner = jnp.dot(grad_low, w_d, preferred_element_type=jnp.float32)
    grad_gate, grad_upper = act_pull(grad_inner)
    gate_low = grad_gate.astype(jnp.bfloat16)
    upper_low = grad_upper.astype(jnp.bfloat16)
    grad_normed_two = contract_cols(gate_low, w_g) + contract_cols(upper_low, w_u)
    grad_resid_two, grad_gain_two = norm_two_pull(grad_normed_two)
    grad_resid = grad_out + grad_resid_two
    resid_low = grad_resid.astype(jnp.bfloat16)
    w_q, w_k, w_v, w_o = (
        lax.all_gather(w_query, "seq", axis=0, tiled=True),
        lax.all_gather(w_key, "seq", axis=0, tiled=True),
        lax.all_gather(w_value, "seq", axis=0, tiled=True),
        lax.all_gather(w_out, "seq", axis=0, tiled=True),
    )
    grad_attended = contract_cols(resid_low, w_o)
    grad_mixed, grad_sub = sub_pull(
        grad_attended.reshape(row_count, head_count, value_size).transpose(1, 0, 2)
    )
    mixed_low = grad_mixed.astype(jnp.bfloat16)
    mixed_back = mixed_low.astype(jnp.float32)
    grad_lam = -jnp.sum(mixed_back * map_outs[1], axis=(1, 2))
    deltas = jnp.stack(
        [
            jnp.sum(mixed_back * map_outs[0], axis=-1),
            -lam_vals[:, None] * jnp.sum(mixed_back * map_outs[1], axis=-1),
        ]
    )
    mixed_rows = mixed_low.transpose(1, 0, 2)
    running = jnp.zeros((row_count, head_count, 2, half_size), jnp.float32)
    query_key_piece = lax.all_gather(key_flat, "seq", axis=0, tiled=True)
    query_value_piece = lax.all_gather(value_low, "seq", axis=0, tiled=True)
    piece_rows = query_key_piece.shape[0]
    query_block_rows = sub_block(piece_rows)

    def query_block_step(state_now, offset):
        block_start = offset

        def query_compute(state_in):
            key_blk = lax.dynamic_slice_in_dim(
                query_key_piece, offset, query_block_rows, 0
            ).reshape(query_block_rows, head_count, 2, half_size)
            value_blk = lax.dynamic_slice_in_dim(
                query_value_piece, offset, query_block_rows, 0
            ).reshape(query_block_rows, head_count, value_size)
            key_ids = block_start + jnp.arange(query_block_rows, dtype=jnp.int32)
            allowed = key_ids[None, :] <= own_ids[:, None]
            grad_dots = jnp.einsum(
                "qhe,khe->hqk", mixed_rows, value_blk, preferred_element_type=jnp.float32
            )
            updates = []
            for map_index in range(2):
                scores = (
                    jnp.einsum(
                        "qhd,khd->hqk",
                        query_rot[:, :, map_index],
                        key_blk[:, :, map_index],
                        preferred_element_type=jnp.float32,
                    )
                    * score_scale
                )
                weights = jnp.where(
                    allowed[None], jnp.exp(scores - log_sums[map_index][..., None]), 0.0
                )
                factor = 1.0 if map_index == 0 else -lam_vals[:, None, None]
                grad_scores = (
                    weights * (factor * grad_dots - deltas[map_index][..., None])
                ).astype(jnp.bfloat16)
                updates.append(
                    jnp.einsum(
                        "hqk,khd->qhd",
                        grad_scores,
                        key_blk[:, :, map_index],
                        preferred_element_type=jnp.float32,
                    )
                    * score_scale
                )
            return state_in + jnp.stack(updates, axis=2)

        state_now = lax.cond(
            block_start > last_row, lambda unchanged: unchanged, query_compute, state_now
        )
        return (state_now, None)

    offsets = jnp.arange(piece_rows // query_block_rows, dtype=jnp.int32) * query_block_rows
    running, _ = lax.scan(query_block_step, running, offsets)
    grad_query_rot = running
    log_all, delta_all = (
        lax.all_gather(log_sums, "seq", axis=2, tiled=True),
        lax.all_gather(deltas, "seq", axis=2, tiled=True),
    )
    key_start = (
        jnp.zeros((row_count, head_count, 2, half_size), jnp.float32),
        jnp.zeros((row_count, head_count, value_size), jnp.float32),
    )
    running = key_start
    query_piece = lax.all_gather(
        query_rot.reshape(row_count, model_width), "seq", axis=0, tiled=True
    )
    grad_piece = lax.all_gather(
        mixed_rows.reshape(row_count, model_width), "seq", axis=0, tiled=True
    )
    piece_rows = query_piece.shape[0]
    key_block_rows = sub_block(piece_rows)

    def key_block_step(state_now, offset):
        block_start = offset

        def key_compute(state_in):
            grad_keys, grad_values = state_in
            query_blk = lax.dynamic_slice_in_dim(query_piece, offset, key_block_rows, 0).reshape(
                key_block_rows, head_count, 2, half_size
            )
            grad_blk = lax.dynamic_slice_in_dim(grad_piece, offset, key_block_rows, 0).reshape(
                key_block_rows, head_count, value_size
            )
            query_ids = block_start + jnp.arange(key_block_rows, dtype=jnp.int32)
            allowed = own_ids[None, :] <= query_ids[:, None]
            log_blk = lax.dynamic_slice_in_dim(log_all, block_start, key_block_rows, 2)
            delta_blk = lax.dynamic_slice_in_dim(delta_all, block_start, key_block_rows, 2)
            grad_dots = jnp.einsum(
                "qhe,khe->hqk", grad_blk, value_mine, preferred_element_type=jnp.float32
            )
            key_terms = []
            for map_index in range(2):
                scores = (
                    jnp.einsum(
                        "qhd,khd->hqk",
                        query_blk[:, :, map_index],
                        key_rot[:, :, map_index],
                        preferred_element_type=jnp.float32,
                    )
                    * score_scale
                )
                weights = jnp.where(
                    allowed[None], jnp.exp(scores - log_blk[map_index][..., None]), 0.0
                )
                value_term = jnp.einsum(
                    "hqk,qhe->khe",
                    weights.astype(jnp.bfloat16),
                    grad_blk,
                    preferred_element_type=jnp.float32,
                )
                if map_index == 0:
                    grad_values = grad_values + value_term
                    factor = 1.0
                else:
                    grad_values = grad_values - lam_vals[None, :, None] * value_term
                    factor = -lam_vals[:, None, None]
                grad_scores = (
                    weights * (factor * grad_dots - delta_blk[map_index][..., None])
                ).astype(jnp.bfloat16)
                key_terms.append(
                    jnp.einsum(
                        "hqk,qhd->khd",
                        grad_scores,
                        query_blk[:, :, map_index],
                        preferred_element_type=jnp.float32,
                    )
                    * score_scale
                )
            return (grad_keys + jnp.stack(key_terms, axis=2), grad_values)

        state_now = lax.cond(
            block_start + key_block_rows - 1 < first_row,
            lambda unchanged: unchanged,
            key_compute,
            state_now,
        )
        return (state_now, None)

    offsets = jnp.arange(piece_rows // key_block_rows, dtype=jnp.int32) * key_block_rows
    running, _ = lax.scan(key_block_step, running, offsets)
    grad_key_rot, grad_values = running
    query_grad_low = (
        rotate(grad_query_rot, -angles).reshape(row_count, model_width).astype(jnp.bfloat16)
    )
    key_grad_low = (
        rotate(grad_key_rot, -angles).reshape(row_count, model_width).astype(jnp.bfloat16)
    )
    value_grad_low = grad_values.reshape(row_count, model_width).astype(jnp.bfloat16)
    grad_normed = (
        contract_cols(query_grad_low, w_q)
        + contract_cols(key_grad_low, w_k)
        + contract_cols(value_grad_low, w_v)
    )
    grad_tokens, grad_gain_one = norm_one_pull(grad_normed)
    input_grad = (grad_resid + grad_tokens)[None]
    lam_parts = lam_pull(grad_lam)
    small_totals = lax.psum(
        (
            grad_gain_one,
            grad_gain_two,
            grad_sub,
            lam_parts[0],
            lam_parts[1],
            lam_parts[2],
            lam_parts[3],
        ),
        ("batch", "seq"),
    )
    left_sides = (normed_low, attended_low, normed_two_low, grad_low)
    right_sides = (
        jnp.concatenate([query_grad_low, key_grad_low, value_grad_low], axis=1),
        resid_low,
        jnp.concatenate([gate_low, upper_low], axis=1),
        inner,
    )
    select = lambda matrix: matrix
    pieces = []
    for left_side, right_side in zip(left_sides, right_sides):
        pieces.append(contract_rows(select(left_side), right_side))
    grad_shard = lax.psum_scatter(
        jnp.concatenate(pieces, axis=1), "seq", scatter_dimension=0, tiled=True
    )
    grad_total = lax.psum(grad_shard, "batch")
    column_edges = [0]
    for column_width in (
        model_width,
        model_width,
        model_width,
        model_width,
        ffn_width,
        ffn_width,
        ffn_width,
    ):
        column_edges.append(column_edges[-1] + column_width)
    weight_grads = [
        grad_total[:, column_edges[index_pos] : column_edges[index_pos + 1]]
        for index_pos in range(7)
    ]
    squares = (
        jnp.sum(small_totals[3] ** 2)
        + jnp.sum(small_totals[4] ** 2)
        + jnp.sum(small_totals[5] ** 2)
        + jnp.sum(small_totals[6] ** 2)
    )
    return (
        output,
        input_grad,
        small_totals[0],
        weight_grads[0],
        weight_grads[1],
        weight_grads[2],
        small_totals[3],
        small_totals[4],
        small_totals[5],
        small_totals[6],
        small_totals[2],
        weight_grads[3],
        small_totals[1],
        weight_grads[4],
        weight_grads[5],
        weight_grads[6],
        jnp.mean(lam_vals),
        jnp.sqrt(squares),
    )


def solution(mesh):
    in_specs = (
        P("batch", "seq", None),
        P("batch", "seq"),
        P("batch", "seq"),
        P("batch", "seq", None),
        P(),
        P("seq", None),
        P("seq", None),
        P("seq", None),
        P(),
        P(),
        P(),
        P(),
        P(),
        P("seq", None),
        P(),
        P("seq", None),
        P("seq", None),
        P("seq", None),
    )
    out_specs = (
        P("batch", "seq", None),
        P("batch", "seq", None),
        P(),
        P("seq", None),
        P("seq", None),
        P("seq", None),
        P(),
        P(),
        P(),
        P(),
        P(),
        P("seq", None),
        P(),
        P("seq", None),
        P("seq", None),
        P("seq", None),
        P(),
        P(),
    )
    return jax.shard_map(body, mesh=mesh, in_specs=in_specs, out_specs=out_specs, check_vma=False)
```

profile of v0, /device:TPU:0, one launch (start us, length us, event | category | flops | bytes accessed | tf_op | source)
XLA Modules:
  0.0 2226.7 jit_solution(11921325850844272628)
XLA Ops:
  11.2 55.1 %all-gather.18.cloned.1.call-done = bf16[1536,1536]{1,0:T(8,128)(2,1)} async-done(((bf16[96,1536]{1,0:T(8,128)(2,1)}), bf16[1536,1536]{1,0:T(8,128)(2,1)}) %all-gather.18.cloned.1.call-update) | async-done | bytes 4718608 | tf_op jit(solution)/shard_map/all_gather | solution.py:95
  66.3 4.1 convolution_convert_fusion
  71.3 49.1 %all-gather.16.cloned.1.call-done = bf16[1536,1536]{1,0:T(8,128)(2,1)} async-done(((bf16[96,1536]{1,0:T(8,128)(2,1)}), bf16[1536,1536]{1,0:T(8,128)(2,1)}) %all-gather.16.cloned.1.call-update) | async-done | bytes 4718608 | tf_op jit(solution)/shard_map/all_gather | solution.py:93
  120.4 6.7 copy.69
  127.0 47.5 %all-gather.12.cloned.1.call-done = bf16[1536,1536]{1,0:T(8,128)(2,1)} async-done(((bf16[96,1536]{1,0:T(8,128)(2,1)}), bf16[1536,1536]{1,0:T(8,128)(2,1)}) %all-gather.12.cloned.1.call-update) | async-done | bytes 4718608 | tf_op jit(solution)/shard_map/all_gather | solution.py:94
  174.5 6.7 copy.68
  181.2 4.1 fusion.176
  194.5 43.0 %all-gather.20.cloned.1.call-done = bf16[2048,1536]{1,0:T(8,128)(2,1)} async-done(((bf16[128,1536]{1,0:T(8,128)(2,1)}), bf16[2048,1536]{1,0:T(8,128)(2,1)}) %all-gather.20.cloned.1.call-update) | async-done | bytes 6291472 | tf_op jit(solution)/shard_map/all_gather | solution.py:119
  237.6 8.7 copy.71
  246.3 58.2 %all-gather.14.cloned.1.call-done = bf16[2048,1536]{0,1:T(8,128)(2,1)} async-done(((bf16[128,1536]{0,1:T(8,128)(2,1)}), bf16[2048,1536]{0,1:T(8,128)(2,1)}) %all-gather.14.cloned.1.call-update) | async-done | bytes 6291472 | tf_op jit(solution)/shard_map/all_gather | solution.py:118
  304.6 24.8 %while.47 = (s32[]{:T(128)}, f32[2,12,128]{2,1,0:T(8,128)S(1)}, f32[2,12,128]{2,1,0:T(8,128)S(1)}, f32[2,12,128,128]{3,2,1,0:T(8,128)S(1)}, s32[2]{0:T(128)}, /*...) while((s32[]{:T(128)}, f32[2,12,128]{2,1,0:T(8,128)S(1)}, ...), condition=%wide.region_8.0_spmd.clone, body=%wide.region_1.8_spmd.clone.sunk | while | flops 1250184320 | bytes 67486016 | solution.py:168
  306.7 20.3 conditional.10
  309.6 7.0 constant_dynamic-slice_fusion
  318.0 2.9 fusion.9
  322.4 2.2 fusion.37
  334.5 23.5 %all-gather.22.cloned.1.call-done = bf16[1536,1536]{1,0:T(8,128)(2,1)} async-done(((bf16[96,1536]{1,0:T(8,128)(2,1)}), bf16[1536,1536]{1,0:T(8,128)(2,1)}) %all-gather.22.cloned.1.call-update) | async-done | bytes 4718608 | tf_op jit(solution)/shard_map/all_gather | solution.py:96
  358.0 3.2 multiply_reduce_fusion.2
  361.5 98.2 %all-gather.24.cloned.1.call-done = bf16[1536,4096]{1,0:T(8,128)(2,1)} async-done(((bf16[96,4096]{1,0:T(8,128)(2,1)}), bf16[1536,4096]{1,0:T(8,128)(2,1)}) %all-gather.24.cloned.1.call-update) | async-done | bytes 12582928 | tf_op jit(solution)/shard_map/all_gather | solution.py:181
  459.7 7.7 fusion.203
  467.4 93.5 %all-gather.26.cloned.1.call-done = bf16[1536,4096]{1,0:T(8,128)(2,1)} async-done(((bf16[96,4096]{1,0:T(8,128)(2,1)}), bf16[1536,4096]{1,0:T(8,128)(2,1)}) %all-gather.26.cloned.1.call-update) | async-done | bytes 12582928 | tf_op jit(solution)/shard_map/all_gather | solution.py:182
  560.9 7.7 fusion.204
  568.7 93.5 %all-gather.28.cloned.1.call-done = bf16[1536,4096]{1,0:T(8,128)(2,1)} async-done(((bf16[96,4096]{1,0:T(8,128)(2,1)}), bf16[1536,4096]{1,0:T(8,128)(2,1)}) %all-gather.28.cloned.1.call-update) | async-done | bytes 12582928 | tf_op jit(solution)/shard_map/all_gather | solution.py:183
  662.2 10.4 multiply_convert_fusion.12
  672.6 10.2 fusion.205
  682.8 7.4 multiply_reduce_fusion
  691.9 4.0 fusion.182
  700.6 21.5 all_gather.58
  725.0 35.3 %while.48 = (s32[]{:T(128)}, f32[128,12,2,64]{0,3,1,2:T(8,128)}, s32[2]{0:T(128)}, s32[]{:T(128)}, bf16[2048,1536]{0,1:T(8,128)(2,1)}, /*index=5*/bf16[128,12,2,...) while((s32[]{:T(128)}, f32[128,12,2,64]{0,3,1,2:T(8,128)}, ...), condition=%wide.region_20.21_spmd.clone, body=%wide.region_17.20_spmd.clone.sunk | while | flops 1229128832 | bytes 45290648 | solution.py:286
  727.5 30.4 %conditional.11 = (f32[128,12,2,64]{0,3,1,2:T(8,128)}) conditional(s32[]{:T(128)} %convert_element_type.324, (s32[]{:T(128)}, bf16[2048,1536]{0,1:T(8,128)(2,1)}, s32[]{:T(128)}, bf16[128,12,2,64]{0,3,2,1:T(8,128)(2,1)}, f32[2,12,128]{2,1,0:T(8,128)S(1)}, /*index=5*/bf16[2048,1536]{0,1:T(8,128)(2,1)}, bf16[128,12,128]{2,0,1:T(8,128)(2,1)S(1)}, ...), branch_computations={%region_18.18_spmd, %region_19.19_spmd} | conditional | flops 1229128832 | bytes 45289872 | solution.py:280
  729.4 6.9 constant_dynamic-slice_fusion.2
  736.3 3.7 fusion.201
  742.6 6.6 fusion.72
  749.2 6.3 fusion.66
  755.5 2.4 maximum_add_fusion
  761.8 51.0 %all_gather.60 = f32[2,12,2048]{2,1,0:T(8,128)} all-gather(f32[2,12,128]{2,1,0:T(8,128)S(1)} %pad_maximum_fusion.6), channel_id=1, replica_groups=mesh['batch'=2,'seq'=16] {'seq'}, dimensions={2}, use_global_device_ids=true | all-gather | bytes 208896 | tf_op jit(solution)/shard_map/all_gather | solution.py:290
  812.8 6.3 fusion.180
  819.1 10.2 fusion.184
  829.3 19.4 fusion.142
  850.7 82.4 %while.49 = (s32[]{:T(128)}, f32[128,12,2,64]{0,3,1,2:T(8,128)}, f32[128,12,128]{0,2,1:T(8,128)}, s32[2]{0:T(128)}, s32[]{:T(128)}, /*index=5*/bf16[2048,1536]{0...) while((s32[]{:T(128)}, f32[128,12,2,64]{0,3,1,2:T(8,128)}, ...), condition=%wide.region_24.25_spmd.clone.clone, body=%wide.region_21.24_spmd.clone.clone.sunk | while | flops 2047607936 | bytes 170503536 | solution.py:373
  853.3 38.7 %conditional.12 = ((f32[128,12,2,64]{0,3,1,2:T(8,128)}, f32[128,12,128]{0,2,1:T(8,128)})) conditional(s32[]{:T(128)} %convert_element_type.325, (s32[]{:T(128)}, bf16[2048,1536]{0,1:T(8,128)(2,1)}, s32[]{:T(128)}, bf16[128,12,2,64]{0,3,1,2:T(8,128)(2,1)}, f32[2,12,2048]{2,1,0:T(8,128)}, /*index=5*/bf16[2048,1536]{0,1:T(8,128)(2,1)}, ...), branch_computations={%region_22.22_spmd, %region_23.23_spmd} | conditional | flops 2047607936 | bytes 170502720 | solution.py:364
  855.2 6.9 constant_dynamic-slice_fusion.4
  862.2 3.8 fusion.202
  865.9 3.7 fusion.105
  872.6 8.3 fusion.124
  882.1 3.6 fusion.122
  889.0 3.0 fusion.118
  894.4 38.5 %conditional.12 = ((f32[128,12,2,64]{0,3,1,2:T(8,128)}, f32[128,12,128]{0,2,1:T(8,128)})) conditional(s32[]{:T(128)} %convert_element_type.325, (s32[]{:T(128)}, bf16[2048,1536]{0,1:T(8,128)(2,1)}, s32[]{:T(128)}, bf16[128,12,2,64]{0,3,1,2:T(8,128)(2,1)}, f32[2,12,2048]{2,1,0:T(8,128)}, /*index=5*/bf16[2048,1536]{0,1:T(8,128)(2,1)}, ...), branch_computations={%region_22.22_spmd, %region_23.23_spmd} | conditional | flops 2047607936 | bytes 170502720 | solution.py:364
  896.4 6.7 constant_dynamic-slice_fusion.4
  903.1 3.8 fusion.202
  906.9 3.7 fusion.105
  913.5 8.3 fusion.124
  923.0 3.6 fusion.122
  929.9 3.0 fusion.118
  936.1 12.8 fusion.147
  948.9 74.0 %pad_maximum_fusion.3 = f32[1536,18432]{1,0:T(8,128)} fusion(f32[1536,4096]{1,0:T(8,128)} %fusion.184, f32[1536,8192]{1,0:T(8,128)} %fusion.142, f32[1536,1536]{1,0:T(8,128)} %fusion.180, f32[1536,4608]{1,0:T(8,128)} %fusion.147), kind=kLoop, calls=%fused_computation.150 | loop fusion | flops 84934656 | bytes 226492416 | tf_op jit(solution)/shard_map/concatenate | solution.py:414
  1023.1 1013.5 %reduce-scatter.2.cloned.1.call-done = f32[96,18432]{1,0:T(8,128)} async-done(((f32[1536,18432]{1,0:T(8,128)}), f32[96,18432]{1,0:T(8,128)}) %reduce-scatter.2.cloned.1.call-update) | async-done | bytes 7077904 | tf_op jit(solution)/shard_map/reduce_scatter | solution.py:413
  2037.5 9.6 fusion.138
  2047.1 4.0 fusion.206
  2051.1 4.1 convolution_add_fusion.1
  2055.2 4.4 fusion.160
  2059.6 41.3 %all-reduce = (f32[1536]{0:T(1024)}, f32[12,64]{1,0:T(8,128)S(1)}, f32[12,64]{1,0:T(8,128)S(1)}, f32[12,64]{1,0:T(8,128)S(1)}, f32[12,64]{1,0:T(8,128)S(1)}, /*index=5*/f32[128]{0:T(128)}, f32[1536]{0:T(1024)}) all-reduce(f32[1536]{0:T(1024)S(1)} %get-tuple-element.724, ...), channel_id=1, replica_groups=mesh['batch'=2,'seq'=16] {'batch','seq'}, use_global_device_ids=true, to_apply=%region_27.28 | all-reduce | flops 6272 | bytes 50176 | tf_op jit(solution)/shard_map/psum | solution.py:390
  2107.2 102.8 %all-reduce.3.cloned.1.call-done = f32[96,18432]{1,0:T(8,128)} async-done(((f32[96,18432]{1,0:T(8,128)}), f32[96,18432]{1,0:T(8,128)}) %all-reduce.3.cloned.1.call-update) | async-done | bytes 7077904 | tf_op jit(solution)/shard_map/psum | solution.py:416
  2210.0 3.0 fusion.200
  2213.1 4.6 fusion.199
  (310 shorter events, 71.6 us)
Async XLA Ops:
  7.2 63.2 %copy-start.63 = (s32[1,128]{1,0:T(1,128)S(1)}, s32[1,128]{1,0:T(1,128)}, u32[]{:S(2)}) copy-start(s32[1,128]{1,0:T(1,128)} %param.31) | copy-start | bytes 1540
  7.2 59.1 %all-gather.18.cloned.1.call-start = ((), (), s32[]{:S(2)}) async-start(), calls=%async_computation.4 | async-start | bytes 5013504 | tf_op jit(solution)/shard_map/all_gather | solution.py:95
  7.9 112.5 %all-gather.16.cloned.1.call-start = ((), (), s32[]{:S(2)}) async-start(), calls=%async_computation.3 | async-start | bytes 5013504 | tf_op jit(solution)/shard_map/all_gather | solution.py:93
  8.7 165.8 %all-gather.12.cloned.1.call-start = ((), (), s32[]{:S(2)}) async-start(), calls=%async_computation.1 | async-start | bytes 5013504 | tf_op jit(solution)/shard_map/all_gather | solution.py:94
  9.4 228.2 %all-gather.20.cloned.1.call-start = ((), (), s32[]{:S(2)}) async-start(), calls=%async_computation.5 | async-start | bytes 6684672 | tf_op jit(solution)/shard_map/all_gather | solution.py:119
  11.2 174.1 %copy-start.41 = (f32[128]{0:T(128)}, f32[128]{0:T(128)S(1)}, u32[]{:S(2)}) copy-start(f32[128]{0:T(128)S(1)} %fusion.193) | copy-start | bytes 1540
  70.4 234.1 %all-gather.14.cloned.1.call-start = ((), (), s32[]{:S(2)}) async-start(), calls=%async_computation.2 | async-start | bytes 6684672 | tf_op jit(solution)/shard_map/all_gather | solution.py:118
  127.0 54.1 %copy-start.4 = (bf16[1,128,1536]{2,1,0:T(8,128)(2,1)S(1)}, bf16[1,128,1536]{2,1,0:T(8,128)(2,1)}, u32[]{:S(2)}) copy-start(bf16[1,128,1536]{2,1,0:T(8,128)(2,1)} %param.30) | copy-start | bytes 1179652
  127.0 54.1 %copy-start.28 = (f32[1536]{0:T(1024)S(1)}, f32[1536]{0:T(1024)}, u32[]{:S(2)}) copy-start(f32[1536]{0:T(1024)} %param.34) | copy-start | bytes 18436
  187.9 170.1 %all-gather.22.cloned.1.call-start = ((), (), s32[]{:S(2)}) async-start(), calls=%async_computation.6 | async-start | bytes 5013504 | tf_op jit(solution)/shard_map/all_gather | solution.py:96
  188.5 271.2 %all-gather.24.cloned.1.call-start = ((), (), s32[]{:S(2)}) async-start(), calls=%async_computation.7 | async-start | bytes 13369344 | tf_op jit(solution)/shard_map/all_gather | solution.py:181
  189.3 371.7 %all-gather.26.cloned.1.call-start = ((), (), s32[]{:S(2)}) async-start(), calls=%async_computation.8 | async-start | bytes 13369344 | tf_op jit(solution)/shard_map/all_gather | solution.py:182
  190.0 472.2 %all-gather.28.cloned.1.call-start = ((), (), s32[]{:S(2)}) async-start(), calls=%async_computation.9 | async-start | bytes 13369344 | tf_op jit(solution)/shard_map/all_gather | solution.py:183
  190.7 658.0 %all-gather.30.cloned.1.call-start = ((), (), s32[]{:S(2)}) async-start(), calls=%async_computation.10 | async-start | bytes 6684672 | tf_op jit(solution)/shard_map/all_gather | solution.py:297
  191.6 657.1 %all-gather.32.cloned.1.call-start = ((), (), s32[]{:S(2)}) async-start(), calls=%async_computation.11 | async-start | bytes 6684672 | tf_op jit(solution)/shard_map/all_gather | solution.py:300
  192.3 54.0 %copy-start.49 = (f32[12]{0:T(128)}, f32[12]{0:T(128)S(1)}, u32[]{:S(2)}) copy-start(f32[12]{0:T(128)S(1)} %get-tuple-element.871) | copy-start | bytes 148
  192.3 53.9 %copy-start.51 = (f32[12]{0:T(128)}, f32[12]{0:T(128)S(1)}, u32[]{:S(2)}) copy-start(f32[12]{0:T(128)S(1)} %get-tuple-element.872) | copy-start | bytes 148
  192.4 497.9 %copy-start.47 = (f32[128]{0:T(128)}, f32[128]{0:T(128)S(1)}, u32[]{:S(2)}) copy-start(f32[128]{0:T(128)S(1)} %convert_bitcast_fusion.1) | copy-start | bytes 1540
  193.5 505.1 %copy-start.57 = (f32[12]{0:T(128)}, f32[12]{0:T(128)S(1)}, u32[]{:S(2)}) copy-start(f32[12]{0:T(128)S(1)} %get-tuple-element.1192) | copy-start | bytes 148
  331.0 30.2 %copy-start.30 = (f32[1536]{0:T(1024)S(1)}, f32[1536]{0:T(1024)}, u32[]{:S(2)}) copy-start(f32[1536]{0:T(1024)} %param.44) | copy-start | bytes 18436
  334.5 132.9 %copy-start.17 = (bf16[12,128,128]{1,2,0:T(8,128)(2,1)}, bf16[12,128,128]{1,2,0:T(8,128)(2,1)S(1)}, u32[]{:S(2)}) copy-start(bf16[12,128,128]{1,2,0:T(8,128)(2,1)S(1)} %multiply_convert_fusion.15) | copy-start | bytes 1179652
  361.3 329.0 %copy-start.6 = (f32[128,1536]{1,0:T(8,128)}, f32[128,1536]{1,0:T(8,128)S(1)}, u32[]{:S(2)}) copy-start(f32[128,1536]{1,0:T(8,128)S(1)} %get-tuple-element.868) | copy-start | bytes 2359300
  361.4 199.5 %copy-start.15 = (bf16[128,1536]{1,0:T(8,128)(2,1)}, bf16[128,1536]{1,0:T(8,128)(2,1)S(1)}, u32[]{:S(2)}) copy-start(bf16[128,1536]{1,0:T(8,128)(2,1)S(1)} %multiply_convert_fusion.14) | copy-start | bytes 1179652
  467.4 194.8 %copy-start.26 = (bf16[1,128,1536]{2,1,0:T(8,128)(2,1)S(1)}, bf16[1,128,1536]{2,1,0:T(8,128)(2,1)}, u32[]{:S(2)}) copy-start(bf16[1,128,1536]{2,1,0:T(8,128)(2,1)} %param.33) | copy-start | bytes 1179652
  662.2 20.6 slice-start.4
  662.2 20.6 slice-start.5
  672.6 10.2 copy-start.21
  672.6 10.2 slice-start.6
  691.9 7.6 copy-start.23
  698.6 26.4 %copy-start.31 = (f32[12,128]{1,0:T(8,128)}, f32[12,128]{1,0:T(8,128)S(1)}, u32[]{:S(2)}) copy-start(f32[12,128]{1,0:T(8,128)S(1)} %get-tuple-element.719) | copy-start | bytes 18436
  698.6 1338.0 %reduce-scatter.2.cloned.1.call-start = ((), (), s32[]{:S(2)}) async-start(), calls=%async_computation.12 | async-start | bytes 120324096 | tf_op jit(solution)/shard_map/reduce_scatter | solution.py:413
  698.7 26.3 %copy-start.56 = (f32[12]{0:T(128)}, f32[12]{0:T(128)S(1)}, u32[]{:S(2)}) copy-start(f32[12]{0:T(128)S(1)} %neg.36) | copy-start | bytes 148
  819.1 10.3 copy-start.16
  819.1 10.3 copy-start.20
  819.1 10.2 copy-start.22
  829.3 21.3 copy-start.59
  850.7 85.4 %copy-start.5 = (bf16[1,128,1536]{2,1,0:T(8,128)(2,1)S(1)}, bf16[1,128,1536]{2,1,0:T(8,128)(2,1)}, u32[]{:S(2)}) copy-start(bf16[1,128,1536]{2,1,0:T(8,128)(2,1)} %param.30) | copy-start | bytes 1179652
  850.7 85.4 %copy-start.29 = (f32[1536]{0:T(1024)S(1)}, f32[1536]{0:T(1024)}, u32[]{:S(2)}) copy-start(f32[1536]{0:T(1024)} %param.34) | copy-start | bytes 18436
  850.7 85.4 %copy-start.42 = (f32[128]{0:T(128)S(1)}, f32[128]{0:T(128)}, u32[]{:S(2)}) copy-start(f32[128]{0:T(128)} %copy-done.41) | copy-start | bytes 1540
  862.1 7.5 copy-start
  869.7 12.3 slice-start
  872.6 8.3 copy-start.12
  872.6 9.4 slice-start.1
  910.6 12.3 slice-start
  913.5 8.3 copy-start.12
  913.5 9.4 slice-start.1
  1023.0 1014.3 %copy-start.50 = (f32[12]{0:T(128)S(1)}, f32[12]{0:T(128)}, u32[]{:S(2)}) copy-start(f32[12]{0:T(128)} %copy-done.49) | copy-start | bytes 148
  1023.0 1014.3 %copy-start.52 = (f32[12]{0:T(128)S(1)}, f32[12]{0:T(128)}, u32[]{:S(2)}) copy-start(f32[12]{0:T(128)} %copy-done.51) | copy-start | bytes 148
  1023.0 1014.3 %copy-start.55 = (f32[12]{0:T(128)S(1)}, f32[12]{0:T(128)}, u32[]{:S(2)}) copy-start(f32[12]{0:T(128)} %get-tuple-element.717) | copy-start | bytes 148
  1023.0 1014.3 %copy-start.34 = (f32[12,64]{1,0:T(8,128)S(1)}, f32[12,64]{1,0:T(8,128)}, u32[]{:S(2)}) copy-start(f32[12,64]{1,0:T(8,128)} %param.38) | copy-start | bytes 9220
  1023.0 1014.3 %copy-start.36 = (f32[12,64]{1,0:T(8,128)S(1)}, f32[12,64]{1,0:T(8,128)}, u32[]{:S(2)}) copy-start(f32[12,64]{1,0:T(8,128)} %param.39) | copy-start | bytes 9220
  1023.0 1014.4 %copy-start.38 = (f32[12,64]{1,0:T(8,128)S(1)}, f32[12,64]{1,0:T(8,128)}, u32[]{:S(2)}) copy-start(f32[12,64]{1,0:T(8,128)} %param.40) | copy-start | bytes 9220
  1023.0 1014.4 %copy-start.40 = (f32[12,64]{1,0:T(8,128)S(1)}, f32[12,64]{1,0:T(8,128)}, u32[]{:S(2)}) copy-start(f32[12,64]{1,0:T(8,128)} %param.41) | copy-start | bytes 9220
  1023.0 1014.5 %copy-start.7 = (f32[128,1536]{1,0:T(8,128)S(1)}, f32[128,1536]{1,0:T(8,128)}, u32[]{:S(2)}) copy-start(f32[128,1536]{1,0:T(8,128)} %copy-done.6) | copy-start | bytes 2359300
  1023.0 1014.5 %copy-start.19 = (bf16[128,4096]{1,0:T(8,128)(2,1)S(1)}, bf16[128,4096]{1,0:T(8,128)(2,1)}, u32[]{:S(2)}) copy-start(bf16[128,4096]{1,0:T(8,128)(2,1)} %get-tuple-element.844) | copy-start | bytes 3145732
  1023.1 1187.0 %all-reduce.3.cloned.1.call-start = ((), (), s32[]{:S(2)}) async-start(), calls=%async_computation.13 | async-start | bytes 14155776 | tf_op jit(solution)/shard_map/psum | solution.py:416
  2051.1 8.5 copy-start.32
  2051.1 8.5 copy-start.53
  2051.1 54.9 %copy-start.62 = (f32[128]{0:T(128)S(1)}, f32[128]{0:T(128)}, u32[]{:S(2)}) copy-start(f32[128]{0:T(128)} %copy-done.61) | copy-start | bytes 1540
  2051.1 54.9 %copy-start.14 = (f32[128,1536]{1,0:T(8,128)S(1)}, f32[128,1536]{1,0:T(8,128)}, u32[]{:S(2)}) copy-start(f32[128,1536]{1,0:T(8,128)} %copy-done.13) | copy-start | bytes 2359300
  2101.0 116.7 %copy-start.43 = (f32[12,64]{1,0:T(8,128)}, f32[12,64]{1,0:T(8,128)S(1)}, u32[]{:S(2)}) copy-start(f32[12,64]{1,0:T(8,128)S(1)} %get-tuple-element.797) | copy-start | bytes 9220
  2101.0 116.7 %copy-start.44 = (f32[12,64]{1,0:T(8,128)}, f32[12,64]{1,0:T(8,128)S(1)}, u32[]{:S(2)}) copy-start(f32[12,64]{1,0:T(8,128)S(1)} %get-tuple-element.798) | copy-start | bytes 9220
  2101.0 116.7 %copy-start.45 = (f32[12,64]{1,0:T(8,128)}, f32[12,64]{1,0:T(8,128)S(1)}, u32[]{:S(2)}) copy-start(f32[12,64]{1,0:T(8,128)S(1)} %get-tuple-element.799) | copy-start | bytes 9220
  2101.0 116.7 %copy-start.46 = (f32[12,64]{1,0:T(8,128)}, f32[12,64]{1,0:T(8,128)S(1)}, u32[]{:S(2)}) copy-start(f32[12,64]{1,0:T(8,128)S(1)} %get-tuple-element.800) | copy-start | bytes 9220
  (36 other events, 171.7 us)
Sparse Core Ops, SparseCore 0:
  10.3 55.9 all-gather.17
  68.6 51.7 all-gather.15
  122.7 51.7 all-gather.11
  177.2 60.3 all-gather.19
  240.1 64.2 all-gather.13
  306.6 51.3 all-gather.21
  360.3 99.3 all-gather.23
  461.9 98.9 all-gather.25
  563.2 98.9 all-gather.27
  664.7 65.9 all-gather.29
  733.5 64.0 all-gather.31
  1023.1 1013.5 reduce-scatter.1
  2039.2 170.7 all-reduce.2
where the time goes:
time: 2230 us
  waiting for transfers between devices  1680 us (75%)
  matrix products  207 us (9%)
  blocking collectives  114 us (5%)
  other arithmetic  105 us (5%)
  local copies, waits for them, and re-layouts  83.2 us (4%)
    reduce_scatter x1, waiting for transfers between devices, body(): lax.psum_scatter(jnp.concatenate(pieces, axis=1), 'seq', scatter_dimensio...  1010 us
    psum x1, waiting for transfers between devices, body(): grad_total = lax.psum(grad_shard, 'batch')  103 us
    all_gather x1, waiting for transfers between devices, body(): lax.all_gather(w_gate, 'seq', axis=0, tiled=True)  98.2 us
    all_gather x1, waiting for transfers between devices, body(): lax.all_gather(w_up, 'seq', axis=0, tiled=True)  93.5 us
    all_gather x1, waiting for transfers between devices, body(): lax.all_gather(w_down, 'seq', axis=0, tiled=True)  93.5 us
    concatenate x1, other arithmetic, body(): jnp.concatenate(pieces, axis=1)  74 us
    all_gather x1, waiting for transfers between devices, body(): key_piece = lax.all_gather(key_flat, 'seq', axis=0, tiled=True)  58.2 us
    all_gather x1, waiting for transfers between devices, body(): lax.all_gather(w_value, 'seq', axis=0, tiled=True)  55.1 us
  transfers between devices with their start and end apart: 13, of which 11 were waited for; matrix products, arithmetic and copies ran while one was open for 10% of the time, Pallas kernels for 0%

commit v1 on v0

v1 whole, which is shorter than its diff:
```python
import functools
import math

import jax
import jax.numpy as jnp
from jax import lax
from jax.experimental import pallas as pl
from jax.experimental.pallas import tpu as pltpu
from jax.sharding import PartitionSpec as P

lam_init = 0.619
norm_eps = 1e-05
log2e = math.log2(math.e)
neg_large = -1e30
f32 = jnp.float32
bf16 = jnp.bfloat16


def lambdas(lam_q1, lam_k1, lam_q2, lam_k2):
    return (
        jnp.exp(jnp.sum(lam_q1 * lam_k1, axis=-1))
        - jnp.exp(jnp.sum(lam_q2 * lam_k2, axis=-1))
        + lam_init
    )


def dims(left_axis, right_axis):
    return (((left_axis,), (right_axis,)), ((), ()))


def dot(left, right, left_axis=1, right_axis=0):
    return lax.dot_general(left, right, dims(left_axis, right_axis), preferred_element_type=f32)


def rotated(value, cosine, sine, inverse=False):
    parts = []
    step = cosine.shape[0]
    sign = -1.0 if inverse else 1.0
    for start in range(0, value.shape[0], 2 * step):
        first = value[start : start + step]
        second = value[start + step : start + 2 * step]
        parts.append(first * cosine - sign * (second * sine))
        parts.append(second * cosine + sign * (first * sine))
    return jnp.concatenate(parts, axis=0)


def forward_kernel(
    block, lam_ref, qkv_ref, cos_ref, sin_ref, gain_ref,
    q_ref, k_ref, v_ref, kt_ref, o1_ref, o2_ref, lse_ref, att_ref,
    qt_ref, vt_ref,
):
    step = pl.program_id(0)
    width = v_ref.shape[1]
    half = width // 2
    length = q_ref.shape[0]
    scale = half ** -0.5 * log2e

    @pl.when(step == 0)
    def _():
        def prepare(index, carry):
            cols = pl.ds(pl.multiple_of(index * block, block), block)
            cosine, sine = cos_ref[:, cols], sin_ref[:, cols]
            query = rotated(qkv_ref[0:width, cols], cosine, sine)
            key = rotated(qkv_ref[width : 2 * width, cols], cosine, sine)
            value = qkv_ref[2 * width : 3 * width, cols]
            qt_ref[:, cols] = query.astype(bf16)
            kt_ref[:, cols] = key.astype(bf16)
            vt_ref[:, cols] = value.astype(bf16)
            q_ref[cols, :] = query.T.astype(bf16)
            k_ref[cols, :] = key.T.astype(bf16)
            v_ref[cols, :] = value.T.astype(bf16)
            return carry

        lax.fori_loop(0, length // block, prepare, 0)

    own = pl.ds(pl.multiple_of(step * block, block), block)
    queries = qt_ref[:, own]
    key_ids = lax.broadcasted_iota(jnp.int32, (block, block), 0)
    query_ids = lax.broadcasted_iota(jnp.int32, (block, block), 1)

    def visit(index, state, diagonal):
        rows = pl.ds(pl.multiple_of(index * block, block), block)
        values = vt_ref[:, rows]
        out = []
        for part in range(2):
            top, total, acc = state[part]
            lo, hi = part * half, (part + 1) * half
            scores = dot(k_ref[rows, lo:hi], queries[lo:hi]) * scale
            if diagonal:
                scores = jnp.where(key_ids <= query_ids, scores, neg_large)
            new_top = jnp.maximum(top, jnp.max(scores, axis=0, keepdims=True))
            weights = jnp.exp2(scores - new_top)
            fade = jnp.exp2(top - new_top)
            total = total * fade + jnp.sum(weights, axis=0, keepdims=True)
            acc = acc * fade + dot(values, weights.astype(bf16))
            out.append((new_top, total, acc))
        return tuple(out)

    start = tuple(
        (
            jnp.full((1, block), neg_large, f32),
            jnp.zeros((1, block), f32),
            jnp.zeros((width, block), f32),
        )
        for _ in range(2)
    )
    state = lax.fori_loop(0, step, lambda index, now: visit(index, now, False), start)
    state = visit(step, state, True)
    outs = []
    for part, ref in ((0, o1_ref), (1, o2_ref)):
        top, total, acc = state[part]
        result = acc / total
        ref[:, own] = result
        lse_ref[pl.ds(part, 1), own] = top + jnp.log2(total)
        outs.append(result)
    mixed = outs[0] - lam_ref[0] * outs[1]
    factor = lax.rsqrt(jnp.mean(mixed * mixed, axis=0, keepdims=True) + norm_eps)
    attended = mixed * factor * gain_ref[...] * (1.0 - lam_init)
    att_ref[own, :] = attended.T.astype(bf16)


def forward_attention(lam, qkv, cosine, sine, gain, block):
    width = qkv.shape[0] // 3
    length = qkv.shape[1]
    full = lambda shape: pl.BlockSpec(shape, lambda i: (0,) * len(shape))
    outs = [
        ((length, width), bf16),
        ((length, width), bf16),
        ((length, width), bf16),
        ((width, length), bf16),
        ((width, length), f32),
        ((width, length), f32),
        ((8, length), f32),
        ((length, width), bf16),
    ]
    return pl.pallas_call(
        functools.partial(forward_kernel, block),
        grid=(length // block,),
        in_specs=[
            pl.BlockSpec(memory_space=pltpu.SMEM),
            full(qkv.shape),
            full(cosine.shape),
            full(sine.shape),
            full(gain.shape),
        ],
        out_specs=[full(shape) for shape, _ in outs],
        out_shape=[jax.ShapeDtypeStruct(shape, kind) for shape, kind in outs],
        scratch_shapes=[pltpu.VMEM((width, length), bf16), pltpu.VMEM((width, length), bf16)],
        compiler_params=pltpu.CompilerParams(
            dimension_semantics=("arbitrary",), vmem_limit_bytes=60 * 2**20
        ),
        name="attention_forward",
    )(lam, qkv, cosine, sine, gain)


def backward_kernel(
    block, lam_ref, q_ref, k_ref, v_ref, kt_ref, o1_ref, o2_ref, lse_ref, datt_ref,
    cos_ref, sin_ref, gain_ref,
    dqkv_ref, dgain_ref, dlam_ref,
    dmix_ref, dmixt_ref, delta_ref, dqt_ref,
):
    step = pl.program_id(0)
    blocks = pl.num_programs(0)
    width = v_ref.shape[1]
    half = width // 2
    length = q_ref.shape[0]
    scale = half ** -0.5
    lam = lam_ref[0]

    @pl.when(step == 0)
    def _():
        dgain_ref[...] = jnp.zeros_like(dgain_ref)
        dlam_ref[...] = jnp.zeros_like(dlam_ref)
        dqt_ref[...] = jnp.zeros_like(dqt_ref)

        def prepare(index, carry):
            cols = pl.ds(pl.multiple_of(index * block, block), block)
            first, second = o1_ref[:, cols], o2_ref[:, cols]
            mixed = first - lam * second
            factor = lax.rsqrt(jnp.mean(mixed * mixed, axis=0, keepdims=True) + norm_eps)
            upstream = datt_ref[cols, :].astype(f32).T * (1.0 - lam_init)
            dgain_ref[...] += jnp.sum(upstream * mixed * factor, axis=1, keepdims=True)
            scaled = upstream * gain_ref[...]
            dmixed = factor * scaled - mixed * (factor * factor * factor) * jnp.mean(
                scaled * mixed, axis=0, keepdims=True
            )
            low = dmixed.astype(bf16)
            back = low.astype(f32)
            dmixt_ref[:, cols] = low
            dmix_ref[cols, :] = back.T.astype(bf16)
            along_second = jnp.sum(back * second, axis=0, keepdims=True)
            delta_ref[0:1, cols] = jnp.sum(back * first, axis=0, keepdims=True)
            delta_ref[1:2, cols] = -lam * along_second
            dlam_ref[...] -= jnp.sum(along_second, axis=1, keepdims=True)
            return carry

        lax.fori_loop(0, length // block, prepare, 0)

    own = pl.ds(pl.multiple_of(step * block, block), block)
    key_ids = lax.broadcasted_iota(jnp.int32, (block, block), 0)
    query_ids = lax.broadcasted_iota(jnp.int32, (block, block), 1)
    keys = k_ref[own, :]
    keys_t = kt_ref[:, own]
    values = v_ref[own, :]

    def visit(index, state, diagonal):
        dkeys, dvalues = state
        cols = pl.ds(pl.multiple_of(index * block, block), block)
        queries = q_ref[cols, :]
        dmix = dmix_ref[cols, :]
        dprob = dot(values, dmixt_ref[:, cols])
        new_keys = []
        blend = None
        for part in range(2):
            lo, hi = part * half, (part + 1) * half
            scores = dot(keys[:, lo:hi], queries[:, lo:hi], 1, 1) * (scale * log2e)
            weights = jnp.exp2(scores - lse_ref[pl.ds(part, 1), cols])
            if diagonal:
                weights = jnp.where(key_ids <= query_ids, weights, 0.0)
            delta = delta_ref[part : part + 1, cols]
            if part == 0:
                blend = weights
                dscore = (weights * (dprob - delta)).astype(bf16)
            else:
                blend = blend - lam * weights
                dscore = (weights * (-lam * dprob - delta)).astype(bf16)
            new_keys.append(dkeys[part] + dot(dscore, queries[:, lo:hi]))
            dqt_ref[lo:hi, cols] += dot(keys_t[lo:hi], dscore)
        dvalues = dvalues + dot(blend.astype(bf16), dmix)
        return tuple(new_keys), dvalues

    start = (
        (jnp.zeros((block, half), f32), jnp.zeros((block, half), f32)),
        jnp.zeros((block, width), f32),
    )
    state = visit(step, start, True)
    dkeys, dvalues = lax.fori_loop(
        step + 1, blocks, lambda index, now: visit(index, now, False), state
    )
    both = jnp.concatenate(dkeys, axis=1).T * scale
    dqkv_ref[own, width : 2 * width] = (
        rotated(both, cos_ref[:, own], sin_ref[:, own], True).T.astype(bf16)
    )
    dqkv_ref[own, 2 * width : 3 * width] = dvalues.astype(bf16)

    dqkv_ref[own, 0:width] = (
        rotated(dqt_ref[:, own] * scale, cos_ref[:, own], sin_ref[:, own], True).T.astype(bf16)
    )


def backward_attention(lam, q, k, v, kt, o1, o2, lse, datt, cosine, sine, gain, block):
    length, width = q.shape
    full = lambda shape: pl.BlockSpec(shape, lambda i: (0,) * len(shape))
    arrays = (q, k, v, kt, o1, o2, lse, datt, cosine, sine, gain)
    outs = [((length, 3 * width), bf16), ((width, 1), f32), ((1, 1), f32)]
    return pl.pallas_call(
        functools.partial(backward_kernel, block),
        grid=(length // block,),
        in_specs=[pl.BlockSpec(memory_space=pltpu.SMEM)] + [full(a.shape) for a in arrays],
        out_specs=[full(shape) for shape, _ in outs],
        out_shape=[jax.ShapeDtypeStruct(shape, kind) for shape, kind in outs],
        scratch_shapes=[
            pltpu.VMEM((length, width), bf16),
            pltpu.VMEM((width, length), bf16),
            pltpu.VMEM((8, length), f32),
            pltpu.VMEM((width, length), f32),
        ],
        compiler_params=pltpu.CompilerParams(
            dimension_semantics=("arbitrary",), vmem_limit_bytes=60 * 2**20
        ),
        name="attention_backward",
    )(lam, *arrays)


def gather_rows(value):
    return lax.all_gather(value, "seq", axis=0, tiled=True)


def scatter_sum(value):
    return lax.psum_scatter(value, "seq", scatter_dimension=0, tiled=True)


def exchange(value):
    return lax.all_to_all(value, "seq", split_axis=0, concat_axis=0, tiled=True)


def rms_parts(value):
    return lax.rsqrt(jnp.mean(value * value, axis=-1, keepdims=True) + norm_eps)


def rms_back(value, factor, gain, upstream):
    scaled = upstream * gain
    mean = jnp.mean(scaled * value, axis=-1, keepdims=True)
    grad = factor * scaled - value * (factor * factor * factor) * mean
    return grad, jnp.sum(upstream * value * factor, axis=0)


def body(
    devices, block_input, positions, needle, cotangent, norm_gain1, w_query, w_key, w_value,
    lam_q1, lam_k1, lam_q2, lam_k2, sub_gain, w_out, norm_gain2, w_gate, w_up, w_down,
):
    rows, width = block_input.shape[1:]
    heads, half = lam_q1.shape
    head_width = sub_gain.shape[0]
    hidden = w_gate.shape[1]
    depth = w_query.shape[0]
    length = rows * devices
    columns = hidden // devices
    if heads > devices or hidden % devices:
        raise ValueError("unsupported mesh")
    head_of = [d * heads // devices for d in range(devices)]
    owner_of = [max(d for d in range(devices) if head_of[d] == h) for h in range(heads)]
    me = lax.axis_index("seq")
    my_head = me * heads // devices
    active = ((me + 1) * heads // devices > my_head).astype(f32)

    tokens = block_input[0].astype(f32)
    factor1 = rms_parts(tokens)
    normed = (tokens * factor1 * norm_gain1).astype(bf16)
    normed_all = gather_rows(normed)
    places = gather_rows(positions[0])

    by_head = jnp.stack([w.reshape(depth, heads, head_width) for w in (w_query, w_key, w_value)], 2)
    by_head = by_head.reshape(depth, heads, 3 * head_width).transpose(1, 0, 2)
    w_head = exchange(by_head[jnp.array(head_of)]).reshape(width, 3 * head_width)

    w_o = gather_rows(w_out)
    grad_out = cotangent[0].astype(f32) * needle[0].astype(f32)[:, None]
    grad_low = grad_out.astype(bf16)
    grad_all = gather_rows(grad_low)

    ffn = jnp.stack([w.reshape(depth, devices, columns) for w in (w_gate, w_up, w_down)], 2)
    ffn = ffn.reshape(depth, devices, 3 * columns).transpose(1, 0, 2)
    w_ffn = exchange(ffn).reshape(width, 3 * columns)

    inv_freq = jnp.exp(-math.log(10000.0) * jnp.arange(half // 2, dtype=f32) / (half // 2))
    angles = inv_freq[:, None] * places.astype(f32)[None, :]
    cosine, sine = jnp.cos(angles), jnp.sin(angles)
    lam_vals, lam_pull = jax.vjp(lambdas, lam_q1, lam_k1, lam_q2, lam_k2)
    lam_mine = lax.dynamic_slice_in_dim(lam_vals, my_head, 1, 0)
    gain_col = sub_gain[:, None]
    block = math.gcd(length, 512)

    qkv = dot(w_head, normed_all, 0, 1)
    q, k, v, kt, o1, o2, lse, att = forward_attention(
        lam_mine, qkv, cosine, sine, gain_col, block
    )
    att_rows = exchange(att.reshape(devices, rows, head_width))
    attended = jnp.concatenate([att_rows[d] for d in owner_of], axis=1)
    resid = tokens + dot(attended, w_o)
    factor2 = rms_parts(resid)
    normed_two = (resid * factor2 * norm_gain2).astype(bf16)
    two_all = gather_rows(normed_two)

    both = dot(two_all, w_ffn[:, : 2 * columns])
    gate, upper = both[:, :columns], both[:, columns:]
    grad_inner = dot(grad_all, w_ffn[:, 2 * columns :])
    sigma = jax.nn.sigmoid(gate)
    silu = gate * sigma
    inner = (silu * upper).astype(bf16)
    gate_low = (grad_inner * upper * sigma * (1.0 + gate * (1.0 - sigma))).astype(bf16)
    upper_low = (grad_inner * silu).astype(bf16)
    gates_low = jnp.concatenate([gate_low, upper_low], axis=1)
    grad_two = scatter_sum(dot(gates_low, w_ffn[:, : 2 * columns], 1, 1).astype(bf16)).astype(f32)
    ffn_out = scatter_sum(dot(inner, w_ffn[:, 2 * columns :], 1, 1).astype(bf16)).astype(f32)
    output = (resid + ffn_out).astype(bf16)[None]

    grad_resid_two, gain_two = rms_back(resid, factor2, norm_gain2, grad_two)
    grad_resid = grad_out + grad_resid_two
    resid_low = grad_resid.astype(bf16)
    grad_att = dot(resid_low, w_o, 1, 1).astype(bf16)
    pieces = jnp.stack(
        [grad_att[:, h * head_width : (h + 1) * head_width] for h in head_of], axis=0
    )
    datt = exchange(pieces).reshape(length, head_width)

    dqkv, dgain, dlam = backward_attention(
        lam_mine, q, k, v, kt, o1, o2, lse, datt, cosine, sine, gain_col, block
    )
    partial = (dot(dqkv, w_head, 1, 1) * active).astype(bf16)
    grad_normed = scatter_sum(partial).astype(f32)
    grad_tokens, gain_one = rms_back(tokens, factor1, norm_gain1, grad_normed)
    input_grad = (grad_resid + grad_tokens)[None]

    def settle(value):
        other = lax.ppermute(value, "batch", [(0, 1), (1, 0)])
        return value.astype(f32) + other.astype(f32)

    ffn_grads = jnp.concatenate(
        [dot(two_all, gates_low, 0, 0), dot(grad_all, inner, 0, 0)], axis=1
    ).astype(bf16)
    ffn_grads = settle(exchange(ffn_grads.reshape(devices, depth, 3 * columns)))
    ffn_grads = ffn_grads.reshape(devices, depth, 3, columns).transpose(2, 1, 0, 3)
    ffn_grads = ffn_grads.reshape(3, depth, hidden)

    head_grads = dot(normed_all, dqkv, 0, 0).astype(bf16)
    head_grads = settle(exchange(head_grads.reshape(devices, depth, 3 * head_width)))
    head_grads = jnp.stack([head_grads[d] for d in owner_of], axis=1)
    head_grads = head_grads.reshape(depth, heads, 3, head_width).transpose(2, 0, 1, 3)
    head_grads = head_grads.reshape(3, depth, width)

    out_grads = dot(attended, resid_low, 0, 0).astype(bf16)
    out_grads = settle(scatter_sum(out_grads))

    hot = jax.nn.one_hot(my_head, heads, dtype=f32) * active
    small = lax.psum(
        (gain_one, gain_two, dgain[:, 0] * active, hot * dlam[0, 0]), ("batch", "seq")
    )
    lam_grads = lam_pull(small[3])
    squares = sum(jnp.sum(g * g) for g in lam_grads)
    return (
        output, input_grad, small[0], head_grads[0], head_grads[1], head_grads[2],
        lam_grads[0], lam_grads[1], lam_grads[2], lam_grads[3], small[2], out_grads, small[1],
        ffn_grads[0], ffn_grads[1], ffn_grads[2], jnp.mean(lam_vals), jnp.sqrt(squares),
    )


def solution(mesh):
    rows = P("seq", None)
    in_specs = (
        P("batch", "seq", None), P("batch", "seq"), P("batch", "seq"), P("batch", "seq", None),
        P(), rows, rows, rows, P(), P(), P(), P(), P(), rows, P(), rows, rows, rows,
    )
    out_specs = (
        P("batch", "seq", None), P("batch", "seq", None), P(), rows, rows, rows,
        P(), P(), P(), P(), P(), rows, P(), rows, rows, rows, P(), P(),
    )
    return jax.shard_map(
        functools.partial(body, mesh.shape["seq"]),
        mesh=mesh, in_specs=in_specs, out_specs=out_specs, check_vma=False,
    )
```

time: 2230 us -> 810 us (0.36)
  waiting for transfers between devices: 1680 us -> 296 us
  matrix products: 207 us -> 71.8 us
  blocking collectives: 114 us -> 212 us
  other arithmetic: 105 us -> 35.8 us
  Pallas kernels: 0 us -> 39.1 us
  starting transfers between devices: 0.51 us -> 37.7 us
    reduce_scatter x1 -> x4, waiting for transfers between devices: 1010 us -> 159 us  [scatter_sum(): return lax.psum_scatter(value, 'seq', scatter_dimension=0, tiled=True)]
    all_gather x11 -> x4, waiting for transfers between devices: 562 us -> 63.3 us  [gather_rows(): return lax.all_gather(value, 'seq', axis=0, tiled=True)]
    dot_general x39 -> x12, matrix products: 207 us -> 71.8 us  [dot(): lax.dot_general(left, right, dims(left_axis, right_axis), preferred_eleme...]
    all_to_all x0 -> x2, blocking collectives: none -> 113 us  [exchange(): return lax.all_to_all(value, 'seq', split_axis=0, concat_axis=0, tiled=True)]
    psum x1 -> x0, waiting for transfers between devices: 103 us -> none  [body(): grad_total = lax.psum(grad_shard, 'batch')]
    concatenate x3 -> x1, other arithmetic: 74.1 us -> 1.57 us  [body(): jnp.concatenate([dot(two_all, gates_low, 0, 0), dot(grad_all, inner, 0, 0...]
    all_to_all x0 -> x4, waiting for transfers between devices: none -> 72.3 us  [exchange(): return lax.all_to_all(value, 'seq', split_axis=0, concat_axis=0, tiled=True)]
    pallas_call x0 -> x2, Pallas kernels: none -> 39.1 us  [the longest x1 22.2 us: backward_attention(): pl.pallas_call(functools.partial(backward_kernel, block), grid=(length //...]
  transfers between devices with their start and end apart: 13 -> 15, of which waited for: 11 -> 8; matrix products, arithmetic and copies ran while one was open for 10% -> 20% of each run, Pallas kernels for 0% -> 5%
where the time goes in v1:
time: 810 us; the launch traced here: 801 us
  waiting for transfers between devices  296 us (37%)
  blocking collectives  212 us (26%)
  local copies, waits for them, and re-layouts  87.7 us (11%)
  matrix products  71.8 us (9%)
  Pallas kernels  39.1 us (5%)
  starting transfers between devices  37.7 us (5%)
  other arithmetic  35.8 us (4%)
  between operations  20.9 us (3%)
    reduce_scatter x4, waiting for transfers between devices, scatter_sum(): return lax.psum_scatter(value, 'seq', scatter_dimension=0, tiled=True)  159 us
    all_to_all x2, blocking collectives, exchange(): return lax.all_to_all(value, 'seq', split_axis=0, concat_axis=0, tiled=True)  113 us
    all_to_all x4, waiting for transfers between devices, exchange(): return lax.all_to_all(value, 'seq', split_axis=0, concat_axis=0, tiled=True)  72.3 us
    dot_general x12, matrix products, dot(): lax.dot_general(left, right, dims(left_axis, right_axis), preferred_eleme...  71.8 us
    all_gather x4, waiting for transfers between devices, gather_rows(): return lax.all_gather(value, 'seq', axis=0, tiled=True)  63.3 us
    psum x1, blocking collectives, body(): lax.psum((gain_one, gain_two, dgain[:, 0] * active, hot * dlam[0, 0]), ('...  54.2 us
    all_gather x1, blocking collectives, gather_rows(): return lax.all_gather(value, 'seq', axis=0, tiled=True)  45.2 us
    all_to_all x4, starting transfers between devices, exchange(): return lax.all_to_all(value, 'seq', split_axis=0, concat_axis=0, tiled=True)  33.2 us
  transfers between devices with their start and end apart: 15, of which 8 were waited for; matrix products, arithmetic and copies ran while one was open for 20% of the time, Pallas kernels for 5%

profile of v1, /device:TPU:0, one launch (start us, length us, event | category | flops | bytes accessed | tf_op | source)
XLA Modules:
  0.0 800.8 jit_solution(15681104747266716666)
XLA Ops:
  7.3 1.2 fusion.15
  9.0 1.9 fusion.17
  11.7 1.2 stack_reshape.18
  15.3 1.7 gather_fusion
  17.0 7.4 all-to-all-start
  24.5 45.2 %all-gather = s32[1,2048]{1,0:T(1,128)S(1)} all-gather(s32[1,128]{1,0:T(1,128)S(1)} %copy-done.37), channel_id=2, replica_groups=mesh['batch'=2,'seq'=16] {'seq'}, dimensions={1}, use_global_device_ids=true | all-gather | bytes 8704 | tf_op jit(solution)/shard_map/all_gather | solution.py:276
  71.7 1.8 multiply_sine_fusion
  73.6 19.5 %all-gather.6.cloned.1.call-done = bf16[2048,1536]{1,0:T(8,128)(2,1)} async-done(((bf16[128,1536]{1,0:T(8,128)(2,1)}), bf16[2048,1536]{1,0:T(8,128)(2,1)}) %all-gather.6.cloned.1.call-update) | async-done | bytes 6291472 | tf_op jit(solution)/shard_map/all_gather | solution.py:276
  93.1 7.1 fusion.36.qkv_ref
  100.2 17.0 %attention_forward.1 = (bf16[2048,128]{1,0:T(8,128)(2,1)}, bf16[2048,128]{1,0:T(8,128)(2,1)}, bf16[2048,128]{1,0:T(8,128)(2,1)}, bf16[128,2048]{1,0:T(8,128)(2,1...) custom-call(f32[1]{0:T(128)} %dynamic_slice.3.lam_ref, ...), custom_call_target="tpu_custom_call" | custom-call | tf_op jit(solution)/shard_map/attention_forward/pallas_call | solution.py:136
  117.1 26.2 %all_to_all.30 = bf16[16,128,128]{2,1,0:T(8,128)(2,1)S(1)} all-to-all(bf16[16,128,128]{2,1,0:T(8,128)(2,1)} %bitcast.203), channel_id=1, replica_groups=mesh['batch'=2,'seq'=16] {'seq'}, dimensions={0} | all-to-all | bytes 1048576 | tf_op jit(solution)/shard_map/all_to_all | solution.py:284
  143.5 12.9 %all-gather.8.cloned.1.call-done = bf16[1536,1536]{1,0:T(8,128)(2,1)} async-done(((bf16[96,1536]{1,0:T(8,128)(2,1)}), bf16[1536,1536]{1,0:T(8,128)(2,1)}) %all-gather.8.cloned.1.call-update) | async-done | bytes 4718608 | tf_op jit(solution)/shard_map/all_gather | solution.py:276
  156.5 3.2 multiply_reduce_fusion
  162.7 3.6 stack_reshape.24
  166.3 4.9 stack_reshape.25
  171.2 3.0 stack_reshape.26
  174.2 7.7 pad_maximum_fusion
  181.8 7.1 reshape.164
  188.9 3.1 copy.80
  192.0 86.6 %all_to_all.31 = bf16[16,96,768]{2,1,0:T(8,128)(2,1)} all-to-all(bf16[16,96,768]{2,1,0:T(8,128)(2,1)S(1)} %copy.80), channel_id=1, replica_groups=mesh['batch'=2,'seq'=16] {'seq'}, dimensions={0} | all-to-all | bytes 4718592 | tf_op jit(solution)/shard_map/all_to_all | solution.py:284
  278.6 8.7 %fusion.2 = f32[2048,512]{0,1:T(8,128)} fusion(bf16[2048,1536]{1,0:T(8,128)(2,1)} %all-gather.10.cloned.1.call-done, bf16[1536,768]{1,0:T(8,128)(2,1)} %bitcast.184), kind=kOutput, calls=%fused_computation.26 | convolution fusion | flops 3221225472 | bytes 12058624 | tf_op jit(solution)/shard_map/dot_general | solution.py:32
  287.3 30.9 %all-gather.12.cloned.1.call-done = bf16[2048,1536]{1,0:T(8,128)(2,1)} async-done(((bf16[128,1536]{1,0:T(8,128)(2,1)}), bf16[2048,1536]{1,0:T(8,128)(2,1)}) %all-gather.12.cloned.1.call-update) | async-done | bytes 6291472 | tf_op jit(solution)/shard_map/all_gather | solution.py:276
  318.2 7.0 multiply_convert_fusion.2
  325.2 0.9 copy-done.42
  326.5 5.5 convolution_convert_fusion.1
  332.2 5.7 convolution_convert_fusion
  338.0 6.1 convolution_convert_fusion.5
  344.2 71.8 %reduce-scatter.7.cloned.1.call-done = bf16[128,1536]{1,0:T(8,128)(2,1)} async-done(((bf16[2048,1536]{1,0:T(8,128)(2,1)}), bf16[128,1536]{1,0:T(8,128)(2,1)}) %reduce-scatter.7.cloned.1.call-update) | async-done | bytes 393232 | tf_op jit(solution)/shard_map/reduce_scatter | solution.py:280
  416.0 1.3 fusion.14
  417.2 87.4 %reduce-scatter.5.cloned.1.call-done = bf16[128,1536]{1,0:T(8,128)(2,1)} async-done(((bf16[2048,1536]{1,0:T(8,128)(2,1)}), bf16[128,1536]{1,0:T(8,128)(2,1)}) %reduce-scatter.5.cloned.1.call-update) | async-done | bytes 393232 | tf_op jit(solution)/shard_map/reduce_scatter | solution.py:280
  504.7 2.1 fusion.11
  506.8 3.5 convolution_convert_fusion.2
  510.3 4.1 convolution_convert_fusion.6
  524.2 3.9 all-to-all-start.3
  528.1 6.8 convolution_convert_fusion.3
  535.0 1.6 pad_maximum_fusion.1
  536.5 6.0 all-to-all-done.3
  543.4 8.8 %all-to-all-start.5 = ((bf16[16,96,768]{2,1,0:T(8,128)(2,1)}), bf16[16,96,768]{2,1,0:T(8,128)(2,1)}, u32[]{:S(2)}, u32[]{:S(2)}) async-start(bf16[16,96,768]{2,1,0:T(8,128)(2,1)} %pad_maximum_fusion.1), calls=%async_computation.9 | async-start | bytes 4718592 | tf_op jit(solution)/shard_map/all_to_all | solution.py:284
  552.5 22.2 %attention_backward.1 = (bf16[2048,384]{1,0:T(8,128)(2,1)}, f32[128,1]{1,0:T(8,128)}, f32[1,1]{1,0:T(1,128)}) custom-call(f32[1]{0:T(128)} %dynamic_slice.3.lam_ref, bf16[2048,128]{1,0:T(8,128)(2,1)} %get-tuple-element.30.q_ref, bf16[2048,128]{1,0:T(8,128)(2,1)} %get-tuple-element.31.k_ref, bf16[2048,128]{1,0:T(8,128)(2,1)} %get-tuple-element.32.v_ref, ...), custom_call_target="tpu_custom_call" | custom-call | tf_op jit(solution)/shard_map/attention_backward/pallas_call | solution.py:256
  574.7 6.8 multiply_convert_fusion
  581.5 34.4 %all-to-all-done.5 = bf16[16,96,768]{2,1,0:T(8,128)(2,1)} async-done(((bf16[16,96,768]{2,1,0:T(8,128)(2,1)}), bf16[16,96,768]{2,1,0:T(8,128)(2,1)}, u32[]{:S(2)}, u32[]{:S(2)}) %all-to-all-start.5) | async-done | bytes 2359328 | tf_op jit(solution)/shard_map/all_to_all | solution.py:284
  615.9 1.3 collective-permute-start.2
  617.2 7.3 convolution_convert_fusion.4
  624.5 13.2 %all-to-all-start.4 = ((bf16[16,96,384]{2,1,0:T(8,128)(2,1)}), bf16[16,96,384]{2,1,0:T(8,128)(2,1)S(1)}, u32[]{:S(2)}, u32[]{:S(2)}) async-start(bf16[16,96,384]{2,1,0:T(8,128)(2,1)} %bitcast.198), calls=%async_computation.7 | async-start | bytes 2359296 | tf_op jit(solution)/shard_map/all_to_all | solution.py:284
  638.3 31.9 %all-to-all-done.4 = bf16[16,96,384]{2,1,0:T(8,128)(2,1)S(1)} async-done(((bf16[16,96,384]{2,1,0:T(8,128)(2,1)}), bf16[16,96,384]{2,1,0:T(8,128)(2,1)S(1)}, u32[]{:S(2)}, u32[]{:S(2)}) %all-to-all-start.4) | async-done | bytes 1179680 | tf_op jit(solution)/shard_map/all_to_all | solution.py:284
  670.3 5.1 convert_add_fusion
  675.5 8.1 %reshape.168 = f32[16,96,3,256]{3,2,1,0:T(4,128)} reshape(f32[16,96,768]{2,1,0:T(8,128)} %convert_add_fusion) | data formatting | bytes 9437184 | tf_op jit(solution)/shard_map/reshape | solution.py:393
  683.5 9.8 %fusion.33 = (f32[1,96,16,256]{3,0,1,2:T(1,128)S(1)}, f32[1,96,16,256]{3,0,1,2:T(1,128)S(1)}, f32[1,96,16,256]{3,0,1,2:T(1,128)S(1)}) fusion(f32[3,96,16,256]{3,0,1,2:T(4,128)} %bitcast.178), kind=kLoop, calls=%fused_computation.159 | loop fusion | bytes 9437184 | tf_op jit(solution)/shard_map/slice | solution.py:414
  693.3 0.9 copy.87
  694.3 2.2 copy.93
  697.4 2.2 copy.92
  700.6 2.2 copy.91
  703.6 1.6 convert_add_fusion.1
  706.8 1.0 stack.91
  716.3 1.9 collective-permute-start.1
  718.2 5.0 fusion.34
  723.6 1.0 copy.97
  725.0 1.0 copy.98
  726.4 1.0 copy.99
  728.3 1.3 fusion.21
  729.6 54.2 %all-reduce = (f32[1536]{0:T(1024)}, f32[12]{0:T(128)S(1)}, f32[128]{0:T(128)}, f32[1536]{0:T(1024)}) all-reduce(f32[1536]{0:T(1024)S(1)} %get-tuple-element.42, f32[12]{0:T(128)S(1)} %fusion.29, f32[128]{0:T(128)S(1)} %multiply_reduce_fusion.1, f32[1536]{0:T(1024)S(1)} %get-tuple-element.40), channel_id=1, replica_groups=mesh['batch'=2,'seq'=16] {'batch','seq'}, use_global_device_ids=true, to_apply=%region_10.11 | all-reduce | flops 3212 | bytes 25696 | tf_op jit(solution)/shard_map/psum | solution.py:406
  783.8 1.3 multiply_reduce_fusion.2
  785.2 1.3 multiply_reduce_fusion.4
  789.1 2.2 fusion.9
  (193 shorter events, 35.2 us)
Async XLA Ops:
  7.2 5.7 copy-start.11
  7.2 5.9 copy-start.12
  7.2 85.8 %all-gather.6.cloned.1.call-start = ((), (), s32[]{:S(2)}) async-start(), calls=%async_computation.10 | async-start | bytes 6684672 | tf_op jit(solution)/shard_map/all_gather | solution.py:276
  9.0 3.9 copy-start.29
  10.9 145.5 %all-gather.8.cloned.1.call-start = ((), (), s32[]{:S(2)}) async-start(), calls=%async_computation.11 | async-start | bytes 5013504 | tf_op jit(solution)/shard_map/all_gather | solution.py:276
  13.6 1.6 copy-start.38
  15.2 9.2 %copy-start.37 = (s32[1,128]{1,0:T(1,128)S(1)}, s32[1,128]{1,0:T(1,128)}, u32[]{:S(2)}) copy-start(s32[1,128]{1,0:T(1,128)} %param.20) | copy-start | bytes 1540
  15.2 54.4 %copy-start.35 = (f32[128]{0:T(128)S(1)}, f32[128]{0:T(128)}, u32[]{:S(2)}) copy-start(f32[128]{0:T(128)} %param.31) | copy-start | bytes 1540
  15.3 55.1 %copy-start.17 = (f32[12,64]{1,0:T(8,128)S(1)}, f32[12,64]{1,0:T(8,128)}, u32[]{:S(2)}) copy-start(f32[12,64]{1,0:T(8,128)} %param.29) | copy-start | bytes 9220
  15.3 55.1 %copy-start.19 = (f32[12,64]{1,0:T(8,128)S(1)}, f32[12,64]{1,0:T(8,128)}, u32[]{:S(2)}) copy-start(f32[12,64]{1,0:T(8,128)} %param.30) | copy-start | bytes 9220
  15.3 55.1 %copy-start.21 = (f32[12,64]{1,0:T(8,128)S(1)}, f32[12,64]{1,0:T(8,128)}, u32[]{:S(2)}) copy-start(f32[12,64]{1,0:T(8,128)} %param.27) | copy-start | bytes 9220
  15.3 55.1 %copy-start.23 = (f32[12,64]{1,0:T(8,128)S(1)}, f32[12,64]{1,0:T(8,128)}, u32[]{:S(2)}) copy-start(f32[12,64]{1,0:T(8,128)} %param.28) | copy-start | bytes 9220
  17.0 56.5 %all-to-all-start = ((bf16[16,96,384]{2,1,0:T(8,128)(2,1)}), bf16[16,96,384]{2,1,0:T(8,128)(2,1)S(1)}, u32[]{:S(2)}, u32[]{:S(2)}) async-start(bf16[16,96,384]{2,1,0:T(8,128)(2,1)} %gather_fusion), calls=%async_computation | async-start | bytes 2359296 | tf_op jit(solution)/shard_map/all_to_all | solution.py:284
  24.4 254.2 %all-gather.10.cloned.1.call-start = ((), (), s32[]{:S(2)}) async-start(), calls=%async_computation.12 | async-start | bytes 6684672 | tf_op jit(solution)/shard_map/all_gather | solution.py:276
  70.5 1.2 copy-start.25
  70.5 1.2 copy-start.27
  73.6 26.6 %copy-start.7 = (bf16[16,96,384]{2,1,0:T(8,128)(2,1)}, bf16[16,96,384]{2,1,0:T(8,128)(2,1)S(1)}, u32[]{:S(2)}) copy-start(bf16[16,96,384]{2,1,0:T(8,128)(2,1)S(1)} %all-to-all-done) | copy-start | bytes 3538948
  100.2 56.3 %copy-start = (bf16[1,128,1536]{2,1,0:T(8,128)(2,1)S(1)}, bf16[1,128,1536]{2,1,0:T(8,128)(2,1)}, u32[]{:S(2)}) copy-start(bf16[1,128,1536]{2,1,0:T(8,128)(2,1)} %param.19) | copy-start | bytes 1179652
  143.5 16.2 %copy-start.2 = (bf16[128,1536]{1,0:T(8,128)(2,1)}, bf16[128,1536]{1,0:T(8,128)(2,1)S(1)}, u32[]{:S(2)}) copy-start(bf16[128,1536]{1,0:T(8,128)(2,1)S(1)} %constant_dynamic-update-slice_fusion) | copy-start | bytes 1179652
  143.5 16.7 %copy-start.14 = (f32[1536]{0:T(1024)S(1)}, f32[1536]{0:T(1024)}, u32[]{:S(2)}) copy-start(f32[1536]{0:T(1024)} %param.33) | copy-start | bytes 18436
  143.5 17.7 %copy-start.41 = (s32[1,128]{1,0:T(1,128)S(1)}, s32[1,128]{1,0:T(1,128)}, u32[]{:S(2)}) copy-start(s32[1,128]{1,0:T(1,128)} %param.21) | copy-start | bytes 1540
  143.5 17.7 %copy-start.5 = (bf16[1,128,1536]{2,1,0:T(8,128)(2,1)S(1)}, bf16[1,128,1536]{2,1,0:T(8,128)(2,1)}, u32[]{:S(2)}) copy-start(bf16[1,128,1536]{2,1,0:T(8,128)(2,1)} %param.22) | copy-start | bytes 1179652
  160.2 1.9 copy-start.31
  161.1 157.1 %all-gather.12.cloned.1.call-start = ((), (), s32[]{:S(2)}) async-start(), calls=%async_computation.14 | async-start | bytes 6684672 | tf_op jit(solution)/shard_map/all_gather | solution.py:276
  161.2 0.9 copy-start.33
  162.1 9.1 %copy-start.10 = (bf16[96,4096]{1,0:T(8,128)(2,1)S(1)}, bf16[96,4096]{1,0:T(8,128)(2,1)}, u32[]{:S(2)}) copy-start(bf16[96,4096]{1,0:T(8,128)(2,1)} %param.36) | copy-start | bytes 2359300
  162.1 253.8 %reduce-scatter.7.cloned.1.call-start = ((), (), s32[]{:S(2)}) async-start(), calls=%async_computation.15 | async-start | bytes 6684672 | tf_op jit(solution)/shard_map/reduce_scatter | solution.py:280
  318.2 8.3 %copy-start.1 = (bf16[16,96,768]{2,1,0:T(8,128)(2,1)S(1)}, bf16[16,96,768]{2,1,0:T(8,128)(2,1)}, u32[]{:S(2)}) copy-start(bf16[16,96,768]{2,1,0:T(8,128)(2,1)} %all_to_all.31) | copy-start | bytes 7077892
  325.2 1.0 copy-start.42
  325.2 1.3 copy-start.44
  332.0 172.7 %reduce-scatter.5.cloned.1.call-start = ((), (), s32[]{:S(2)}) async-start(), calls=%async_computation.13 | async-start | bytes 6684672 | tf_op jit(solution)/shard_map/reduce_scatter | solution.py:280
  338.0 78.0 %copy-start.32 = (f32[128]{0:T(128)S(1)}, f32[128]{0:T(128)}, u32[]{:S(2)}) copy-start(f32[128]{0:T(128)} %copy-done.31) | copy-start | bytes 1540
  338.0 166.7 %copy-start.6 = (bf16[1,128,1536]{2,1,0:T(8,128)(2,1)S(1)}, bf16[1,128,1536]{2,1,0:T(8,128)(2,1)}, u32[]{:S(2)}) copy-start(bf16[1,128,1536]{2,1,0:T(8,128)(2,1)} %param.22) | copy-start | bytes 1179652
  338.0 166.7 %copy-start.34 = (f32[128]{0:T(128)S(1)}, f32[128]{0:T(128)}, u32[]{:S(2)}) copy-start(f32[128]{0:T(128)} %copy-done.33) | copy-start | bytes 1540
  338.0 166.7 %copy-start.39 = (f32[128]{0:T(128)S(1)}, f32[128]{0:T(128)}, u32[]{:S(2)}) copy-start(f32[128]{0:T(128)} %get-tuple-element.91) | copy-start | bytes 1540
  338.0 378.3 %reduce-scatter.11.cloned.1.call-start = ((), (), s32[]{:S(2)}) async-start(), calls=%async_computation.17 | async-start | bytes 5013504 | tf_op jit(solution)/shard_map/reduce_scatter | solution.py:280
  344.1 162.6 %copy-start.3 = (bf16[128,1536]{1,0:T(8,128)(2,1)S(1)}, bf16[128,1536]{1,0:T(8,128)(2,1)}, u32[]{:S(2)}) copy-start(bf16[128,1536]{1,0:T(8,128)(2,1)} %copy-done.2) | copy-start | bytes 1179652
  510.3 17.8 %copy-start.43 = (bf16[2048,256]{0,1:T(8,128)(2,1)S(1)}, bf16[2048,256]{0,1:T(8,128)(2,1)}, u32[]{:S(2)}) copy-start(bf16[2048,256]{0,1:T(8,128)(2,1)} %copy-done.42) | copy-start | bytes 3145732
  524.2 18.4 %all-to-all-start.3 = ((bf16[16,128,128]{2,1,0:T(8,128)(2,1)}), bf16[16,128,128]{2,1,0:T(8,128)(2,1)S(1)}, u32[]{:S(2)}, u32[]{:S(2)}) async-start(bf16[16,128,128]{2,1,0:T(8,128)(2,1)} %constant_dynamic-update-slice_fusion.12), calls=%async_computation.5 | async-start | bytes 1048576 | tf_op jit(solution)/shard_map/all_to_all | solution.py:284
  528.1 6.9 copy-start.9
  542.6 0.8 copy-start.4
  543.4 72.5 %all-to-all-start.5 = ((bf16[16,96,768]{2,1,0:T(8,128)(2,1)}), bf16[16,96,768]{2,1,0:T(8,128)(2,1)}, u32[]{:S(2)}, u32[]{:S(2)}) async-start(bf16[16,96,768]{2,1,0:T(8,128)(2,1)} %pad_maximum_fusion.1), calls=%async_computation.9 | async-start | bytes 4718592 | tf_op jit(solution)/shard_map/all_to_all | solution.py:284
  552.2 176.1 %reduce-scatter.9.cloned.1.call-start = ((), (), s32[]{:S(2)}) async-start(), calls=%async_computation.16 | async-start | bytes 6684672 | tf_op jit(solution)/shard_map/reduce_scatter | solution.py:280
  552.5 22.2 %copy-start.8 = (bf16[16,96,384]{2,1,0:T(8,128)(2,1)S(1)}, bf16[16,96,384]{2,1,0:T(8,128)(2,1)}, u32[]{:S(2)}) copy-start(bf16[16,96,384]{2,1,0:T(8,128)(2,1)} %copy-done.7) | copy-start | bytes 3538948
  581.5 35.7 %copy-start.40 = (bf16[2048,384]{1,0:T(8,128)(2,1)S(1)}, bf16[2048,384]{1,0:T(8,128)(2,1)}, u32[]{:S(2)}) copy-start(bf16[2048,384]{1,0:T(8,128)(2,1)} %get-tuple-element.37) | copy-start | bytes 4718596
  615.9 54.4 %collective-permute-start.2 = (bf16[16,96,768]{2,1,0:T(8,128)(2,1)}, bf16[16,96,768]{2,1,0:T(8,128)(2,1)}, u32[]{:S(2)}, u32[]{:S(2)}) collective-permute-start(bf16[16,96,768]{2,1,0:T(8,128)(2,1)} %all-to-all-done.5), channel_id=1, source_target_pairs={{0,16},{16,0},{1,17},{17,1},{2,18},{18,2},{3,19},{19,3},{4,20},{20... | collective-permute-start | bytes 7077896 | tf_op jit(solution)/shard_map/ppermute | solution.py:386
  624.5 45.7 %all-to-all-start.4 = ((bf16[16,96,384]{2,1,0:T(8,128)(2,1)}), bf16[16,96,384]{2,1,0:T(8,128)(2,1)S(1)}, u32[]{:S(2)}, u32[]{:S(2)}) async-start(bf16[16,96,384]{2,1,0:T(8,128)(2,1)} %bitcast.198), calls=%async_computation.7 | async-start | bytes 2359296 | tf_op jit(solution)/shard_map/all_to_all | solution.py:284
  670.2 33.4 %collective-permute-start = (bf16[16,96,384]{2,1,0:T(8,128)(2,1)S(1)}, bf16[16,96,384]{2,1,0:T(8,128)(2,1)}, u32[]{:S(2)}, u32[]{:S(2)}) collective-permute-start(bf16[16,96,384]{2,1,0:T(8,128)(2,1)S(1)} %all-to-all-done.4), channel_id=1, source_target_pairs={{0,16},{16,0},{1,17},{17,1},{2,18},{18,2},{3,19},{19,3},{4,20},{20... | collective-permute-start | bytes 3538952 | tf_op jit(solution)/shard_map/ppermute | solution.py:386
  700.6 2.9 copy-start.16
  716.3 11.1 %collective-permute-start.1 = (bf16[96,1536]{1,0:T(8,128)(2,1)}, bf16[96,1536]{1,0:T(8,128)(2,1)S(1)}, u32[]{:S(2)}, u32[]{:S(2)}) collective-permute-start(bf16[96,1536]{1,0:T(8,128)(2,1)} %reduce-scatter.11.cloned.1.call-done), channel_id=1, source_target_pairs={{0,16},{16,0},{1,17},{17,1},{2,18},{18,2},{3,19},{19,3},{4,20},{20... | collective-permute-start | bytes 884744 | tf_op jit(solution)/shard_map/ppermute | solution.py:386
  724.9 2.5 copy-start.13
  725.0 3.3 copy-start.15
  725.0 3.3 copy-start.30
  726.0 57.8 %copy-start.26 = (f32[12]{0:T(128)S(1)}, f32[12]{0:T(128)}, u32[]{:S(2)}) copy-start(f32[12]{0:T(128)} %copy-done.25) | copy-start | bytes 148
  726.0 57.8 %copy-start.28 = (f32[12]{0:T(128)S(1)}, f32[12]{0:T(128)}, u32[]{:S(2)}) copy-start(f32[12]{0:T(128)} %copy-done.27) | copy-start | bytes 148
  726.0 57.8 %copy-start.18 = (f32[12,64]{1,0:T(8,128)S(1)}, f32[12,64]{1,0:T(8,128)}, u32[]{:S(2)}) copy-start(f32[12,64]{1,0:T(8,128)} %param.29) | copy-start | bytes 9220
  726.0 57.8 %copy-start.20 = (f32[12,64]{1,0:T(8,128)S(1)}, f32[12,64]{1,0:T(8,128)}, u32[]{:S(2)}) copy-start(f32[12,64]{1,0:T(8,128)} %param.30) | copy-start | bytes 9220
  726.0 59.2 %copy-start.22 = (f32[12,64]{1,0:T(8,128)S(1)}, f32[12,64]{1,0:T(8,128)}, u32[]{:S(2)}) copy-start(f32[12,64]{1,0:T(8,128)} %param.27) | copy-start | bytes 9220
  726.0 59.2 %copy-start.24 = (f32[12,64]{1,0:T(8,128)S(1)}, f32[12,64]{1,0:T(8,128)}, u32[]{:S(2)}) copy-start(f32[12,64]{1,0:T(8,128)} %param.28) | copy-start | bytes 9220
  726.0 63.0 %copy-start.36 = (f32[128]{0:T(128)S(1)}, f32[128]{0:T(128)}, u32[]{:S(2)}) copy-start(f32[128]{0:T(128)} %get-tuple-element.89) | copy-start | bytes 1540
Sparse Core Ops, SparseCore 0:
  11.1 81.9 all-gather.5
  95.3 61.0 all-gather.7
  161.2 84.7 all-gather.9
  248.7 69.4 all-gather.11
  332.1 83.7 reduce-scatter.6
  420.3 84.3 reduce-scatter.4
  510.4 107.4 reduce-scatter.10
  622.3 91.4 reduce-scatter.8

commit v2 on v1

--- a/solution.py
+++ b/solution.py
@@ -237,14 +237,14 @@
     dkeys, dvalues = lax.fori_loop(
         step + 1, blocks, lambda index, now: visit(index, now, False), state
     )
-    both = jnp.concatenate(dkeys, axis=1).T * scale
+    both = jnp.concatenate(dkeys, axis=1).T * (scale * lam_ref[1])
     dqkv_ref[own, width : 2 * width] = (
         rotated(both, cos_ref[:, own], sin_ref[:, own], True).T.astype(bf16)
     )
-    dqkv_ref[own, 2 * width : 3 * width] = dvalues.astype(bf16)
+    dqkv_ref[own, 2 * width : 3 * width] = (dvalues * lam_ref[1]).astype(bf16)
 
     dqkv_ref[own, 0:width] = (
-        rotated(dqt_ref[:, own] * scale, cos_ref[:, own], sin_ref[:, own], True).T.astype(bf16)
+        rotated(dqt_ref[:, own] * (scale * lam_ref[1]), cos_ref[:, own], sin_ref[:, own], True).T.astype(bf16)
     )
 
 
@@ -272,12 +272,272 @@
     )(lam, *arrays)
 
 
-def gather_rows(value):
-    return lax.all_gather(value, "seq", axis=0, tiled=True)
-
-
-def scatter_sum(value):
-    return lax.psum_scatter(value, "seq", scatter_dimension=0, tiled=True)
+MESH = pl.DeviceIdType.MESH
+ANY = pl.BlockSpec(memory_space=pl.ANY)
+VMEM = pl.BlockSpec(memory_space=pltpu.VMEM)
+DMA = pltpu.SemaphoreType.DMA
+group = 16
+
+
+def place():
+    me = lax.axis_index("seq")
+    return me, me // 4, (me // 2) % 2, me % 2
+
+
+def remote(src, dst, send_sem, recv_sem, target):
+    return pltpu.make_async_remote_copy(
+        src_ref=src, dst_ref=dst, send_sem=send_sem, recv_sem=recv_sem,
+        device_id={"seq": target}, device_id_type=MESH,
+    )
+
+
+def greet():
+    me, z, _, _ = place()
+    barrier = pltpu.get_barrier_semaphore()
+
+    def tell(target):
+        pl.semaphore_signal(barrier, inc=1, device_id={"seq": target}, device_id_type=MESH)
+
+    tell(me ^ 1)
+    tell(me ^ 2)
+    pl.when(z > 0)(lambda: tell(me - 4))
+    pl.when(z < 3)(lambda: tell(me + 4))
+    pl.semaphore_wait(barrier, 2 + (z > 0).astype(jnp.int32) + (z < 3).astype(jnp.int32))
+
+
+def gather_kernel(parts, *refs):
+    count = len(parts)
+    ins, outs = refs[:count], refs[count : 2 * count]
+    local_sem, recv_sem, up_sem, down_sem, side_sem, core_sem = refs[2 * count :]
+    me, z, x, c = place()
+    greet()
+
+    def view(a, block, part):
+        rows = ins[a].shape[0]
+        sub = rows // parts[a]
+        return outs[a].at[pl.ds(pl.multiple_of(block * rows + part * sub, sub), sub)]
+
+    def copy(a, part, block, target, sems, own=False):
+        sub = ins[a].shape[0] // parts[a]
+        src = ins[a].at[pl.ds(part * sub, sub)] if own else view(a, block, part)
+        return remote(
+            src, view(a, block, part), sems.at[a, part, block], recv_sem.at[a, part, block], target
+        )
+
+    def local(a):
+        rows = ins[a].shape[0]
+        place_here = outs[a].at[pl.ds(pl.multiple_of(me * rows, rows), rows)]
+        return pltpu.make_async_copy(ins[a], place_here, local_sem.at[a])
+
+    every = [(a, p) for a in range(count) for p in range(parts[a])]
+    for a, p in every:
+        copy(a, p, me, me ^ 2, side_sem, True).start()
+        pl.when(z < 3)(lambda: copy(a, p, me, me + 4, up_sem, True).start())
+        pl.when(z > 0)(lambda: copy(a, p, me, me - 4, down_sem, True).start())
+        copy(a, p, me, me ^ 1, core_sem, True).start()
+    for a in range(count):
+        local(a).start()
+
+    def from_line(a, p, s):
+        def pass_on(block):
+            copy(a, p, block, me ^ 2, side_sem).start()
+            copy(a, p, block, me ^ 1, core_sem).start()
+
+        @pl.when(z >= s)
+        def _():
+            block = me - 4 * s
+            copy(a, p, block, me, side_sem).wait_recv()
+            pl.when(z < 3)(lambda: copy(a, p, block, me + 4, up_sem).start())
+            pass_on(block)
+
+        @pl.when(z + s <= 3)
+        def _():
+            block = me + 4 * s
+            copy(a, p, block, me, side_sem).wait_recv()
+            pl.when(z > 0)(lambda: copy(a, p, block, me - 4, down_sem).start())
+            pass_on(block)
+
+    def from_side(a, p, s):
+        def take(block):
+            copy(a, p, block, me, side_sem).wait_recv()
+            copy(a, p, block, me ^ 1, core_sem).start()
+
+        if s == 0:
+            take(me ^ 2)
+        else:
+            pl.when(z >= s)(lambda: take((me ^ 2) - 4 * s))
+            pl.when(z + s <= 3)(lambda: take((me ^ 2) + 4 * s))
+
+    for s in range(1, 4):
+        for a, p in every:
+            from_line(a, p, s)
+        for a, p in every:
+            from_side(a, p, s - 1)
+    for a, p in every:
+        from_side(a, p, 3)
+
+    def finish(i, carry):
+        pair = 4 * (i // 2) + 2 * (i % 2)
+        for a, p in every:
+            copy(a, p, pair + 1 - c, me, core_sem).wait_recv()
+            copy(a, p, pair + c, me, core_sem).wait_send()
+        return carry
+
+    lax.fori_loop(0, 8, finish, 0)
+
+    def sent(i, carry):
+        block = 4 * i + 2 * x + c
+        for a, p in every:
+            copy(a, p, block, me, side_sem).wait_send()
+            pl.when((i <= z) & (z < 3))(lambda: copy(a, p, block, me, up_sem).wait_send())
+            pl.when((i >= z) & (z > 0))(lambda: copy(a, p, block, me, down_sem).wait_send())
+        return carry
+
+    lax.fori_loop(0, 4, sent, 0)
+    for a in range(count):
+        local(a).wait()
+
+
+def gather(arrays, parts, collective_id):
+    devices = lax.axis_size("seq")
+    if devices != group:
+        return [lax.all_gather(a, "seq", axis=0, tiled=True) for a in arrays]
+    count = len(arrays)
+    sem = DMA((count, max(parts), group))
+    return pl.pallas_call(
+        functools.partial(gather_kernel, parts),
+        in_specs=[ANY] * count,
+        out_specs=[ANY] * count,
+        out_shape=[jax.ShapeDtypeStruct((group * a.shape[0],) + a.shape[1:], a.dtype) for a in arrays],
+        scratch_shapes=[DMA((count,)), sem, sem, sem, sem, sem],
+        compiler_params=pltpu.CompilerParams(collective_id=collective_id, has_side_effects=True),
+        name=f"gather{collective_id}",
+    )(*arrays)
+
+
+def scatter_kernel(
+    lhs_ref, rhs_ref, out_ref, own, core_in, side_in, up_in, down_in,
+    core_s, core_r, side_s, side_r, up_s, up_r, down_s, down_r,
+):
+    me, z, x, c = place()
+    rows, width = out_ref.shape
+    greet()
+    mine, across = 2 * x + c, 2 * (1 - x) + c
+
+    def order(g):
+        if g == 3:
+            return z
+        first = jnp.where(3 - g > z, 3 - g, 2 - g)
+        second = jnp.where(g < z, g, g + 1)
+        return jnp.where(z < 2, first, second)
+
+    def core_copy(t, i):
+        return remote(
+            own.at[t, 2 * i + 1 - c], core_in.at[t, i], core_s.at[t, i], core_r.at[t, i], me ^ 1
+        )
+
+    def side_copy(t):
+        return remote(own.at[t, across], side_in.at[t], side_s.at[t], side_r.at[t], me ^ 2)
+
+    def up_copy(t):
+        return remote(own.at[t, mine], up_in.at[t], up_s.at[t], up_r.at[t], me + 4)
+
+    def down_copy(t):
+        return remote(own.at[t, mine], down_in.at[t], down_s.at[t], down_r.at[t], me - 4)
+
+    def multiply(t):
+        left = lhs_ref[pl.ds(pl.multiple_of(t * 4 * rows, 4 * rows), 4 * rows), :]
+        own[t] = dot(left, rhs_ref[...], 1, 1).astype(bf16).reshape(4, rows, width)
+        core_copy(t, 0).start()
+        core_copy(t, 1).start()
+
+    def add(t, block, extra):
+        own[t, block] = (own[t, block].astype(f32) + extra.astype(f32)).astype(bf16)
+
+    def merge_core(t):
+        core_copy(t, 0).wait()
+        core_copy(t, 1).wait()
+        add(t, across, core_in[t, 1 - x])
+        side_copy(t).start()
+        add(t, mine, core_in[t, x])
+
+    def along(t):
+        side_copy(t).wait()
+        add(t, mine, side_in[t])
+
+        @pl.when(t > z)
+        def _():
+            @pl.when(z > 0)
+            def _():
+                up_copy(t).wait_recv()
+                add(t, mine, up_in[t])
+
+            up_copy(t).start()
+
+        @pl.when(t < z)
+        def _():
+            @pl.when(z < 3)
+            def _():
+                down_copy(t).wait_recv()
+                add(t, mine, down_in[t])
+
+            down_copy(t).start()
+
+    steps = [order(g) for g in range(4)]
+    multiply(steps[0])
+    multiply(steps[1])
+    merge_core(steps[0])
+    multiply(steps[2])
+    merge_core(steps[1])
+    multiply(steps[3])
+    merge_core(steps[2])
+    along(steps[0])
+    merge_core(steps[3])
+    along(steps[1])
+    along(steps[2])
+    side_copy(z).wait()
+    out_ref[...] = own[z, mine].astype(f32) + side_in[z].astype(f32)
+
+    @pl.when(z > 0)
+    def _():
+        up_copy(z).wait_recv()
+        out_ref[...] += up_in[z].astype(f32)
+
+    @pl.when(z < 3)
+    def _():
+        down_copy(z).wait_recv()
+        out_ref[...] += down_in[z].astype(f32)
+
+    def sent(i, carry):
+        pl.when(i > z)(lambda: up_copy(i).wait_send())
+        pl.when(i < z)(lambda: down_copy(i).wait_send())
+        return carry
+
+    lax.fori_loop(0, 4, sent, 0)
+
+
+def scatter(lhs, rhs, collective_id):
+    devices = lax.axis_size("seq")
+    if devices != group:
+        partial = dot(lhs, rhs, 1, 1).astype(bf16)
+        return lax.psum_scatter(partial, "seq", scatter_dimension=0, tiled=True).astype(f32)
+    rows, width = lhs.shape[0] // group, rhs.shape[0]
+    block = pltpu.VMEM((4, rows, width), bf16)
+    return pl.pallas_call(
+        scatter_kernel,
+        in_specs=[VMEM, VMEM],
+        out_specs=VMEM,
+        out_shape=jax.ShapeDtypeStruct((rows, width), f32),
+        scratch_shapes=[
+            pltpu.VMEM((4, 4, rows, width), bf16), pltpu.VMEM((4, 2, rows, width), bf16),
+            block, block, block, DMA((4, 2)), DMA((4, 2)),
+            DMA((4,)), DMA((4,)), DMA((4,)), DMA((4,)), DMA((4,)), DMA((4,)),
+        ],
+        compiler_params=pltpu.CompilerParams(
+            collective_id=collective_id, has_side_effects=True, vmem_limit_bytes=56 * 2**20
+        ),
+        name=f"scatter{collective_id}",
+    )(lhs, rhs)
 
 
 def exchange(value):
@@ -317,17 +577,17 @@
     tokens = block_input[0].astype(f32)
     factor1 = rms_parts(tokens)
     normed = (tokens * factor1 * norm_gain1).astype(bf16)
-    normed_all = gather_rows(normed)
-    places = gather_rows(positions[0])
+    here = jnp.broadcast_to(positions[0], (1, 8, rows))
+    normed_all, places = gather([normed, here], (2, 1), 0)
+    places = places[:, 0].reshape(length)
 
     by_head = jnp.stack([w.reshape(depth, heads, head_width) for w in (w_query, w_key, w_value)], 2)
     by_head = by_head.reshape(depth, heads, 3 * head_width).transpose(1, 0, 2)
     w_head = exchange(by_head[jnp.array(head_of)]).reshape(width, 3 * head_width)
 
-    w_o = gather_rows(w_out)
+    w_o, = gather([w_out], (1,), 1)
     grad_out = cotangent[0].astype(f32) * needle[0].astype(f32)[:, None]
     grad_low = grad_out.astype(bf16)
-    grad_all = gather_rows(grad_low)
 
     ffn = jnp.stack([w.reshape(depth, devices, columns) for w in (w_gate, w_up, w_down)], 2)
     ffn = ffn.reshape(depth, devices, 3 * columns).transpose(1, 0, 2)
@@ -337,7 +597,7 @@
     angles = inv_freq[:, None] * places.astype(f32)[None, :]
     cosine, sine = jnp.cos(angles), jnp.sin(angles)
     lam_vals, lam_pull = jax.vjp(lambdas, lam_q1, lam_k1, lam_q2, lam_k2)
-    lam_mine = lax.dynamic_slice_in_dim(lam_vals, my_head, 1, 0)
+    lam_mine = jnp.stack([lax.dynamic_index_in_dim(lam_vals, my_head, 0, False), active])
     gain_col = sub_gain[:, None]
     block = math.gcd(length, 512)
 
@@ -350,7 +610,7 @@
     resid = tokens + dot(attended, w_o)
     factor2 = rms_parts(resid)
     normed_two = (resid * factor2 * norm_gain2).astype(bf16)
-    two_all = gather_rows(normed_two)
+    two_all, grad_all = gather([normed_two, grad_low], (2, 2), 2)
 
     both = dot(two_all, w_ffn[:, : 2 * columns])
     gate, upper = both[:, :columns], both[:, columns:]
@@ -361,8 +621,8 @@
     gate_low = (grad_inner * upper * sigma * (1.0 + gate * (1.0 - sigma))).astype(bf16)
     upper_low = (grad_inner * silu).astype(bf16)
     gates_low = jnp.concatenate([gate_low, upper_low], axis=1)
-    grad_two = scatter_sum(dot(gates_low, w_ffn[:, : 2 * columns], 1, 1).astype(bf16)).astype(f32)
-    ffn_out = scatter_sum(dot(inner, w_ffn[:, 2 * columns :], 1, 1).astype(bf16)).astype(f32)
+    grad_two = scatter(gates_low, w_ffn[:, : 2 * columns], 3)
+    ffn_out = scatter(inner, w_ffn[:, 2 * columns :], 4)
     output = (resid + ffn_out).astype(bf16)[None]
 
     grad_resid_two, gain_two = rms_back(resid, factor2, norm_gain2, grad_two)
@@ -377,8 +637,7 @@
     dqkv, dgain, dlam = backward_attention(
         lam_mine, q, k, v, kt, o1, o2, lse, datt, cosine, sine, gain_col, block
     )
-    partial = (dot(dqkv, w_head, 1, 1) * active).astype(bf16)
-    grad_normed = scatter_sum(partial).astype(f32)
+    grad_normed = scatter(dqkv, w_head, 5)
     grad_tokens, gain_one = rms_back(tokens, factor1, norm_gain1, grad_normed)
     input_grad = (grad_resid + grad_tokens)[None]
 
@@ -399,8 +658,7 @@
     head_grads = head_grads.reshape(depth, heads, 3, head_width).transpose(2, 0, 1, 3)
     head_grads = head_grads.reshape(3, depth, width)
 
-    out_grads = dot(attended, resid_low, 0, 0).astype(bf16)
-    out_grads = settle(scatter_sum(out_grads))
+    out_grads = settle(scatter(attended.T, resid_low.T, 6).astype(bf16))
 
     hot = jax.nn.one_hot(my_head, heads, dtype=f32) * active
     small = lax.psum(

time: 810 us -> 803 us (level)
  Pallas kernels: 39.1 us -> 446 us
  waiting for transfers between devices: 296 us -> 56.3 us
  blocking collectives: 212 us -> 58.4 us
  matrix products: 71.8 us -> 45 us
  local copies, waits for them, and re-layouts: 87.7 us -> 104 us
  between operations: 20.9 us -> 7.23 us
    pallas_call x0 -> x7, Pallas kernels: none -> 408 us  [the longest x4 218 us: scatter(): pl.pallas_call(scatter_kernel, in_specs=[VMEM, VMEM], out_specs=VMEM, out...]
    reduce_scatter x4 -> x0, waiting for transfers between devices: 159 us -> none  [scatter_sum(): return lax.psum_scatter(value, 'seq', scatter_dimension=0, tiled=True)]
    all_to_all x2 -> x1, blocking collectives: 113 us -> 18.5 us  [exchange(): return lax.all_to_all(value, 'seq', split_axis=0, concat_axis=0, tiled=True)]
    all_gather x4 -> x0, waiting for transfers between devices: 63.3 us -> none  [gather_rows(): return lax.all_gather(value, 'seq', axis=0, tiled=True)]
    all_to_all x4 -> x5, waiting for transfers between devices: 72.3 us -> 12.4 us  [exchange(): return lax.all_to_all(value, 'seq', split_axis=0, concat_axis=0, tiled=True)]
    all_gather x1 -> x0, blocking collectives: 45.2 us -> none  [gather_rows(): return lax.all_gather(value, 'seq', axis=0, tiled=True)]
    ppermute x3, waiting for transfers between devices: 0.01 us -> 43.9 us  [settle(): other = lax.ppermute(value, 'batch', [(0, 1), (1, 0)])]
    dot_general x12 -> x8, matrix products: 71.8 us -> 45 us  [dot(): lax.dot_general(left, right, dims(left_axis, right_axis), preferred_eleme...]
  transfers between devices with their start and end apart: 15 -> 8, of which waited for: 8 -> 4; matrix products, arithmetic and copies ran while one was open for 20% -> 14% of each run, Pallas kernels for 5% -> 39%
where the time goes in v2:
time: 803 us; the launch traced here: 792 us
  Pallas kernels  446 us (56%)
  local copies, waits for them, and re-layouts  104 us (13%)
  blocking collectives  58.4 us (7%)
  waiting for transfers between devices  56.3 us (7%)
  matrix products  45 us (6%)
  other arithmetic  42.4 us (5%)
  starting transfers between devices  33.1 us (4%)
    pallas_call x4, Pallas kernels, scatter(): pl.pallas_call(scatter_kernel, in_specs=[VMEM, VMEM], out_specs=VMEM, out...  218 us
    pallas_call x3, Pallas kernels, gather(): pl.pallas_call(functools.partial(gather_kernel, parts), in_specs=[ANY] *...  189 us
    dot_general x8, matrix products, dot(): lax.dot_general(left, right, dims(left_axis, right_axis), preferred_eleme...  45 us
    ppermute x3, waiting for transfers between devices, settle(): other = lax.ppermute(value, 'batch', [(0, 1), (1, 0)])  43.9 us
    psum x1, blocking collectives, body(): lax.psum((gain_one, gain_two, dgain[:, 0] * active, hot * dlam[0, 0]), ('...  39.9 us
    unnamed x123, local copies, waits for them, and re-layouts  30.5 us
    all_to_all x5, starting transfers between devices, exchange(): return lax.all_to_all(value, 'seq', split_axis=0, concat_axis=0, tiled=True)  28.8 us
    pallas_call x1, Pallas kernels, backward_attention(): pl.pallas_call(functools.partial(backward_kernel, block), grid=(length //...  21.7 us
  transfers between devices with their start and end apart: 8, of which 4 were waited for; matrix products, arithmetic and copies ran while one was open for 14% of the time, Pallas kernels for 39%

profile of v2, /device:TPU:0, one launch (start us, length us, event | category | flops | bytes accessed | tf_op | source)
XLA Modules:
  0.0 792.0 jit_solution(2995066885210442792)
XLA Ops:
  6.1 1.7 gather_fusion
  7.9 7.5 all-to-all-start
  20.3 57.5 %gather0.1 = (bf16[2048,1536]{1,0:T(8,128)(2,1)}, s32[16,8,128]{2,1,0:T(8,128)}) custom-call(bf16[128,1536]{1,0:T(8,128)(2,1)} %copy.131.refs_0_, s32[1,8,128]{2,1,0:T(8,128)} %broadcast_in_dim.16.refs_1_), custom_call_target="tpu_custom_call" | custom-call | tf_op jit(solution)/shard_map/gather0/pallas_call | solution.py:407
  79.9 1.8 multiply_sine_fusion
  81.7 7.6 fusion.25.qkv_ref
  89.3 16.2 %attention_forward.1 = (bf16[2048,128]{1,0:T(8,128)(2,1)}, bf16[2048,128]{1,0:T(8,128)(2,1)}, bf16[2048,128]{1,0:T(8,128)(2,1)}, bf16[128,2048]{1,0:T(8,128)(2,1...) custom-call(f32[2]{0:T(128)} %pad_maximum_fusion.4.lam_ref, ...), custom_call_target="tpu_custom_call" | custom-call | tf_op jit(solution)/shard_map/attention_forward/pallas_call | solution.py:136
  105.5 2.1 copy.133
  107.6 5.7 all-to-all-start.1
  113.3 45.9 %gather1.1 = bf16[1536,1536]{1,0:T(8,128)(2,1)} custom-call(bf16[96,1536]{1,0:T(8,128)(2,1)} %refs_0_.1), custom_call_target="tpu_custom_call" | custom-call | tf_op jit(solution)/shard_map/gather1/pallas_call | solution.py:407
  160.2 3.0 stack_reshape.24
  163.2 3.0 stack_reshape.25
  166.1 3.0 stack_reshape.26
  169.1 6.8 pad_maximum_fusion
  175.9 4.6 reshape.169
  180.6 3.8 copy.141
  184.3 3.9 all-to-all-start.2
  198.5 4.2 multiply_reduce_fusion.2
  204.8 1.9 copy.136.refs_0_
  206.7 86.0 %gather2.1 = (bf16[2048,1536]{1,0:T(8,128)(2,1)}, bf16[2048,1536]{1,0:T(8,128)(2,1)}) custom-call(bf16[128,1536]{1,0:T(8,128)(2,1)} %copy.136.refs_0_, bf16[128,1536]{1,0:T(8,128)(2,1)} %copy.137.refs_1_), custom_call_target="tpu_custom_call" | custom-call | tf_op jit(solution)/shard_map/gather2/pallas_call | solution.py:407
  294.9 6.0 fusion.18
  301.0 4.1 multiply_convert_fusion.1
  305.1 56.1 %scatter4.1 = f32[128,1536]{1,0:T(8,128)} custom-call(bf16[2048,256]{1,0:T(8,128)(2,1)} %get-tuple-element.145.lhs_ref, bf16[1536,256]{1,0:T(8,128)(2,1)} %slice.217.rhs_ref), custom_call_target="tpu_custom_call" | custom-call | tf_op jit(solution)/shard_map/scatter4/pallas_call | solution.py:526
  361.3 2.3 copy.144
  363.6 1.5 pad_maximum_fusion.2.lhs_ref
  365.1 46.3 %scatter3.1 = f32[128,1536]{1,0:T(8,128)} custom-call(bf16[2048,512]{1,0:T(8,128)(2,1)} %pad_maximum_fusion.2.lhs_ref, bf16[1536,512]{1,0:T(8,128)(2,1)} %slice.214.rhs_ref), custom_call_target="tpu_custom_call" | custom-call | tf_op jit(solution)/shard_map/scatter3/pallas_call | solution.py:526
  411.4 1.4 copy.147
  414.0 2.3 convert_bitcast_fusion
  416.3 4.3 convolution_convert_fusion.3
  420.9 18.5 %all_to_all.30 = bf16[16,128,128]{2,1,0:T(8,128)(2,1)} all-to-all(bf16[16,128,128]{2,1,0:T(8,128)(2,1)S(1)} %constant_dynamic-update-slice_fusion.12), channel_id=1, replica_groups=mesh['batch'=2,'seq'=16] {'seq'}, dimensions={0} | all-to-all | bytes 1048576 | tf_op jit(solution)/shard_map/all_to_all | solution.py:544
  439.4 21.7 %attention_backward.1 = (bf16[2048,384]{1,0:T(8,128)(2,1)}, f32[128,1]{1,0:T(8,128)}, f32[1,1]{1,0:T(1,128)}) custom-call(f32[2]{0:T(128)} %pad_maximum_fusion.4.lam_ref, bf16[2048,128]{1,0:T(8,128)(2,1)} %get-tuple-element.38.q_ref, bf16[2048,128]{1,0:T(8,128)(2,1)} %get-tuple-element.39.k_ref, bf16[2048,128]{1,0:T(8,128)(2,1)} %get-tuple-element.40.v_ref, ...), custom_call_target="tpu_custom_call" | custom-call | tf_op jit(solution)/shard_map/attention_backward/pallas_call | solution.py:256
  461.1 7.7 convolution_convert_fusion.1
  468.8 4.2 all-to-all-start.4
  473.1 4.8 convolution_convert_fusion.2
  477.9 6.2 convolution_convert_fusion
  484.1 1.6 pad_maximum_fusion.1
  485.7 12.4 %all-to-all-done.4 = bf16[16,96,384]{2,1,0:T(8,128)(2,1)S(1)} async-done(((bf16[16,96,384]{2,1,0:T(8,128)(2,1)}), bf16[16,96,384]{2,1,0:T(8,128)(2,1)S(1)}, u32[]{:S(2)}, u32[]{:S(2)}) %all-to-all-start.4) | async-done | bytes 1179680 | tf_op jit(solution)/shard_map/all_to_all | solution.py:544
  499.2 7.5 all-to-all-start.5
  506.7 69.9 %scatter6.1 = f32[96,1536]{1,0:T(8,128)} custom-call(bf16[1536,128]{1,0:T(8,128)(2,1)} %bitcast.196, bf16[1536,128]{1,0:T(8,128)(2,1)} %get-tuple-element.138.rhs_ref), custom_call_target="tpu_custom_call" | custom-call | tf_op jit(solution)/shard_map/scatter6/pallas_call | solution.py:526
  577.7 1.6 collective-permute-start.1
  580.8 4.4 collective-permute-done.1
  585.3 2.0 convert_add_fusion.2
  587.3 46.0 %scatter5.1 = f32[128,1536]{1,0:T(8,128)} custom-call(bf16[2048,384]{1,0:T(8,128)(2,1)} %get-tuple-element.45.lhs_ref, bf16[1536,384]{1,0:T(8,128)(2,1)} %bitcast.191), custom_call_target="tpu_custom_call" | custom-call | tf_op jit(solution)/shard_map/scatter5/pallas_call | solution.py:526
  635.9 1.5 multiply_reduce_fusion.3
  637.3 1.7 fusion.10
  639.1 39.9 %all-reduce = (f32[1536]{0:T(1024)}, f32[12]{0:T(128)}, f32[128]{0:T(128)}, f32[1536]{0:T(1024)}) all-reduce(f32[1536]{0:T(1024)} %get-tuple-element.122, f32[12]{0:T(128)} %fusion.15, f32[128]{0:T(128)} %multiply_reduce_fusion.3, f32[1536]{0:T(1024)S(1)} %copy-done.19), channel_id=1, replica_groups=mesh['batch'=2,'seq'=16] {'batch','seq'}, use_global_device_ids=true, to_apply=%region_7.8 | all-reduce | flops 3212 | bytes 25696 | tf_op jit(solution)/shard_map/psum | solution.py:664
  679.7 2.7 collective-permute-start
  682.4 2.0 multiply_reduce_fusion.6
  685.7 2.0 multiply_reduce_fusion.4
  689.7 2.3 fusion.7
  692.0 2.3 copy.159
  694.3 15.3 %collective-permute-done = bf16[16,96,384]{2,1,0:T(8,128)(2,1)} collective-permute-done((bf16[16,96,384]{2,1,0:T(8,128)(2,1)}, bf16[16,96,384]{2,1,0:T(8,128)(2,1)}, u32[]{:S(2)}, u32[]{:S(2)}) %collective-permute-start) | collective-permute-done | bytes 1179680 | tf_op jit(solution)/shard_map/ppermute | solution.py:645
  709.6 1.9 convert_add_fusion.1
  712.4 1.6 stack.100
  714.1 1.6 stack.101
  715.7 1.6 stack.102
  717.3 1.6 stack.103
  728.0 1.7 fusion.23
  733.8 24.1 %collective-permute-done.2 = bf16[16,96,768]{2,1,0:T(8,128)(2,1)} collective-permute-done((bf16[16,96,768]{2,1,0:T(8,128)(2,1)S(1)}, bf16[16,96,768]{2,1,0:T(8,128)(2,1)}, u32[]{:S(2)}, u32[]{:S(2)}) %collective-permute-start.2) | collective-permute-done | bytes 2359328 | tf_op jit(solution)/shard_map/ppermute | solution.py:645
  757.9 4.4 convert_add_fusion
  762.3 8.1 %reshape.173 = f32[16,96,3,256]{3,2,1,0:T(4,128)} reshape(f32[16,96,768]{2,1,0:T(8,128)} %convert_add_fusion) | data formatting | bytes 9437184 | tf_op jit(solution)/shard_map/reshape | solution.py:652
  770.4 9.6 %fusion.22 = (f32[1,96,16,256]{3,0,1,2:T(1,128)S(1)}, f32[1,96,16,256]{3,0,1,2:T(1,128)S(1)}, f32[1,96,16,256]{3,0,1,2:T(1,128)S(1)}) fusion(f32[3,96,16,256]{3,0,1,2:T(4,128)} %bitcast.180), kind=kLoop, calls=%fused_computation.145 | loop fusion | bytes 9437184 | tf_op jit(solution)/shard_map/slice | solution.py:672
  781.0 2.2 copy.166
  784.1 2.2 copy.167
  787.3 2.2 copy.168
  (176 shorter events, 52.7 us)
Async XLA Ops:
  4.5 1.6 copy-start.33
  6.1 9.3 %copy-start.15 = (bf16[1,128,1536]{2,1,0:T(8,128)(2,1)S(1)}, bf16[1,128,1536]{2,1,0:T(8,128)(2,1)}, u32[]{:S(2)}) copy-start(bf16[1,128,1536]{2,1,0:T(8,128)(2,1)} %param.19) | copy-start | bytes 1179652
  7.8 8.6 %copy-start.18 = (f32[1536]{0:T(1024)S(1)}, f32[1536]{0:T(1024)}, u32[]{:S(2)}) copy-start(f32[1536]{0:T(1024)} %param.23) | copy-start | bytes 18436
  7.8 9.8 %copy-start.31 = (f32[128]{0:T(128)S(1)}, f32[128]{0:T(128)}, u32[]{:S(2)}) copy-start(f32[128]{0:T(128)} %param.31) | copy-start | bytes 1540
  7.8 10.5 %copy-start.20 = (f32[12,64]{1,0:T(8,128)S(1)}, f32[12,64]{1,0:T(8,128)}, u32[]{:S(2)}) copy-start(f32[12,64]{1,0:T(8,128)} %param.27) | copy-start | bytes 9220
  7.8 10.5 %copy-start.21 = (f32[12,64]{1,0:T(8,128)S(1)}, f32[12,64]{1,0:T(8,128)}, u32[]{:S(2)}) copy-start(f32[12,64]{1,0:T(8,128)} %param.28) | copy-start | bytes 9220
  7.8 10.5 %copy-start.22 = (f32[12,64]{1,0:T(8,128)S(1)}, f32[12,64]{1,0:T(8,128)}, u32[]{:S(2)}) copy-start(f32[12,64]{1,0:T(8,128)} %param.29) | copy-start | bytes 9220
  7.8 10.5 %copy-start.23 = (f32[12,64]{1,0:T(8,128)S(1)}, f32[12,64]{1,0:T(8,128)}, u32[]{:S(2)}) copy-start(f32[12,64]{1,0:T(8,128)} %param.30) | copy-start | bytes 9220
  7.9 11.8 %copy-start.32 = (s32[1,128]{1,0:T(1,128)S(1)}, s32[1,128]{1,0:T(1,128)}, u32[]{:S(2)}) copy-start(s32[1,128]{1,0:T(1,128)} %param.20) | copy-start | bytes 1540
  7.9 73.8 %all-to-all-start = ((bf16[16,96,384]{2,1,0:T(8,128)(2,1)}), bf16[16,96,384]{2,1,0:T(8,128)(2,1)S(1)}, u32[]{:S(2)}, u32[]{:S(2)}) async-start(bf16[16,96,384]{2,1,0:T(8,128)(2,1)} %gather_fusion), calls=%async_computation | async-start | bytes 2359296 | tf_op jit(solution)/shard_map/all_to_all | solution.py:544
  16.4 72.9 %copy-start.26 = (f32[128]{0:T(128)}, f32[128]{0:T(128)S(1)}, u32[]{:S(2)}) copy-start(f32[128]{0:T(128)S(1)} %get-tuple-element.171) | copy-start | bytes 1540
  18.5 60.5 %copy-start.24 = (f32[12]{0:T(128)}, f32[12]{0:T(128)S(1)}, u32[]{:S(2)}) copy-start(f32[12]{0:T(128)S(1)} %get-tuple-element.176) | copy-start | bytes 148
  18.5 60.5 %copy-start.25 = (f32[12]{0:T(128)}, f32[12]{0:T(128)S(1)}, u32[]{:S(2)}) copy-start(f32[12]{0:T(128)S(1)} %get-tuple-element.177) | copy-start | bytes 148
  81.7 7.6 copy-start.1
  107.6 76.8 %all-to-all-start.1 = ((bf16[16,128,128]{1,2,0:T(8,128)(2,1)}), bf16[16,128,128]{1,2,0:T(8,128)(2,1)}, u32[]{:S(2)}, u32[]{:S(2)}) async-start(bf16[16,128,128]{1,2,0:T(8,128)(2,1)} %copy.133), calls=%async_computation.1 | async-start | bytes 1048576 | tf_op jit(solution)/shard_map/all_to_all | solution.py:544
  113.3 46.0 %copy-start.16 = (bf16[1,128,1536]{2,1,0:T(8,128)(2,1)S(1)}, bf16[1,128,1536]{2,1,0:T(8,128)(2,1)}, u32[]{:S(2)}) copy-start(bf16[1,128,1536]{2,1,0:T(8,128)(2,1)} %param.22) | copy-start | bytes 1179652
  113.3 46.9 %copy-start.12 = (bf16[96,4096]{1,0:T(8,128)(2,1)S(1)}, bf16[96,4096]{1,0:T(8,128)(2,1)}, u32[]{:S(2)}) copy-start(bf16[96,4096]{1,0:T(8,128)(2,1)} %param.34) | copy-start | bytes 2359300
  159.3 3.9 copy-start.13
  160.2 6.0 copy-start.14
  184.3 3.9 copy-start.35
  184.3 3.9 copy-start.3
  184.3 108.4 %all-to-all-start.2 = ((bf16[16,96,768]{2,1,0:T(8,128)(2,1)}), bf16[16,96,768]{2,1,0:T(8,128)(2,1)S(1)}, u32[]{:S(2)}, u32[]{:S(2)}) async-start(bf16[16,96,768]{2,1,0:T(8,128)(2,1)} %copy.141), calls=%async_computation.2 | async-start | bytes 4718592 | tf_op jit(solution)/shard_map/all_to_all | solution.py:544
  188.2 9.5 %copy-start.29 = (f32[128]{0:T(128)}, f32[128]{0:T(128)S(1)}, u32[]{:S(2)}) copy-start(f32[128]{0:T(128)S(1)} %convert_bitcast_fusion.1) | copy-start | bytes 1540
  198.5 4.2 copy-start.5
  198.5 5.3 copy-start.17
  203.2 0.5 copy-start.27
  293.7 7.3 slice-start
  294.9 6.1 slice-start.1
  305.1 58.4 %copy-start.8 = (bf16[2048,256]{1,0:T(8,128)(2,1)S(1)}, bf16[2048,256]{1,0:T(8,128)(2,1)}, u32[]{:S(2)}) copy-start(bf16[2048,256]{1,0:T(8,128)(2,1)} %get-tuple-element.143) | copy-start | bytes 3145732
  305.1 58.4 %copy-start.10 = (bf16[2048,256]{1,0:T(8,128)(2,1)S(1)}, bf16[2048,256]{1,0:T(8,128)(2,1)}, u32[]{:S(2)}) copy-start(bf16[2048,256]{1,0:T(8,128)(2,1)} %get-tuple-element.144) | copy-start | bytes 3145732
  365.1 47.8 %copy-start.28 = (f32[128]{0:T(128)S(1)}, f32[128]{0:T(128)}, u32[]{:S(2)}) copy-start(f32[128]{0:T(128)} %copy-done.27) | copy-start | bytes 1540
  411.4 2.6 copy-start.4
  411.4 2.6 copy-start.30
  411.4 2.6 copy-start.34
  416.3 4.3 copy-start
  468.8 4.2 copy-start.7
  468.8 29.4 %all-to-all-start.4 = ((bf16[16,96,384]{2,1,0:T(8,128)(2,1)}), bf16[16,96,384]{2,1,0:T(8,128)(2,1)S(1)}, u32[]{:S(2)}, u32[]{:S(2)}) async-start(bf16[16,96,384]{2,1,0:T(8,128)(2,1)} %bitcast.40), calls=%async_computation.4 | async-start | bytes 2359296 | tf_op jit(solution)/shard_map/all_to_all | solution.py:544
  473.0 4.8 copy-start.9
  473.1 4.8 copy-start.11
  485.7 94.2 %copy-start.6 = (bf16[1,128,1536]{1,2,0:T(8,128)(2,1)S(1)}, bf16[1,128,1536]{1,2,0:T(8,128)(2,1)}, u32[]{:S(2)}) copy-start(bf16[1,128,1536]{1,2,0:T(8,128)(2,1)} %get-tuple-element.161) | copy-start | bytes 1179652
  498.2 1.0 copy-start.2
  499.2 195.1 %all-to-all-start.5 = ((bf16[16,96,768]{2,1,0:T(8,128)(2,1)}), bf16[16,96,768]{2,1,0:T(8,128)(2,1)S(1)}, u32[]{:S(2)}, u32[]{:S(2)}) async-start(bf16[16,96,768]{2,1,0:T(8,128)(2,1)} %pad_maximum_fusion.1), calls=%async_computation.5 | async-start | bytes 4718592 | tf_op jit(solution)/shard_map/all_to_all | solution.py:544
  577.7 7.6 collective-permute-start.1
  587.3 51.8 %copy-start.19 = (f32[1536]{0:T(1024)S(1)}, f32[1536]{0:T(1024)}, u32[]{:S(2)}) copy-start(f32[1536]{0:T(1024)} %get-tuple-element.120) | copy-start | bytes 18436
  679.7 29.9 %collective-permute-start = (bf16[16,96,384]{2,1,0:T(8,128)(2,1)}, bf16[16,96,384]{2,1,0:T(8,128)(2,1)}, u32[]{:S(2)}, u32[]{:S(2)}) collective-permute-start(bf16[16,96,384]{2,1,0:T(8,128)(2,1)} %copy-done.2), channel_id=1, source_target_pairs={{0,16},{16,0},{1,17},{17,1},{2,18},{18,2},{3,19},{19,3},{4,20},{20... | collective-permute-start | bytes 3538952 | tf_op jit(solution)/shard_map/ppermute | solution.py:645
  694.2 63.6 %collective-permute-start.2 = (bf16[16,96,768]{2,1,0:T(8,128)(2,1)S(1)}, bf16[16,96,768]{2,1,0:T(8,128)(2,1)}, u32[]{:S(2)}, u32[]{:S(2)}) collective-permute-start(bf16[16,96,768]{2,1,0:T(8,128)(2,1)S(1)} %all-to-all-done.5), channel_id=1, source_target_pairs={{0,16},{16,0},{1,17},{17,1},{2,18},{18,2},{3,19},{19,3},{4,20},{20... | collective-permute-start | bytes 7077896 | tf_op jit(solution)/shard_map/ppermute | solution.py:645

commit v3 on v1

--- a/solution.py
+++ b/solution.py
@@ -30,6 +30,633 @@
 
 def dot(left, right, left_axis=1, right_axis=0):
     return lax.dot_general(left, right, dims(left_axis, right_axis), preferred_element_type=f32)
+
+
+MESH = pl.DeviceIdType.MESH
+ANY = pl.BlockSpec(memory_space=pl.ANY)
+VMEM = pl.BlockSpec(memory_space=pltpu.VMEM)
+SMEM = pl.BlockSpec(memory_space=pltpu.SMEM)
+DMA = pltpu.SemaphoreType.DMA
+group = 16
+busy = pl.CostEstimate(flops=4 * 10**10, bytes_accessed=10**7, transcendentals=0)
+sides = (8, 4, 2)
+
+
+def place():
+    seq = lax.axis_index("seq")
+    return lax.axis_index("batch") * 8 + seq % 8, seq // 8
+
+
+def device(number, cube=None):
+    return {"batch": number // 8, "seq": (place()[1] if cube is None else cube) * 8 + number % 8}
+
+
+def partner():
+    return {"batch": lax.axis_index("batch"), "seq": lax.axis_index("seq") ^ 8}
+
+
+def swapped():
+    batch, seq = lax.axis_index("batch"), lax.axis_index("seq")
+    return {"batch": 1 - batch, "seq": seq ^ 8}, batch != seq // 8
+
+
+def anyone(index):
+    return index // group * 8 + index % 8, index % group // 8
+
+
+def everywhere():
+    return lax.axis_index("batch") * group + lax.axis_index("seq")
+
+
+def remote(src, dst, send_sem, recv_sem, number):
+    return pltpu.make_async_remote_copy(
+        src_ref=src, dst_ref=dst, send_sem=send_sem, recv_sem=recv_sem,
+        device_id=device(number), device_id_type=MESH,
+    )
+
+
+def greet(cross=False, swap=False):
+    me = place()[0]
+    barrier = pltpu.get_barrier_semaphore()
+    count = 1 + len(sides)
+    for mask in (1,) + sides:
+        pl.semaphore_signal(barrier, inc=1, device_id=device(me ^ mask), device_id_type=MESH)
+    if cross:
+        pl.semaphore_signal(barrier, inc=1, device_id=partner(), device_id_type=MESH)
+        count = count + 1
+    if swap:
+        target, moved = swapped()
+
+        @pl.when(moved)
+        def _():
+            pl.semaphore_signal(barrier, inc=1, device_id=target, device_id_type=MESH)
+
+        count = count + moved.astype(jnp.int32)
+    pl.semaphore_wait(barrier, count)
+
+
+def greet_all():
+    barrier = pltpu.get_barrier_semaphore()
+    me = everywhere()
+
+    def tell(mask, carry):
+        target = device(*anyone(me ^ mask))
+        pl.semaphore_signal(barrier, inc=1, device_id=target, device_id_type=MESH)
+        return carry
+
+    lax.fori_loop(1, 2 * group, tell, 0)
+    pl.semaphore_wait(barrier, 2 * group - 1)
+
+
+class Cargo:
+    def __init__(self, cross, swap, sems):
+        self.cross, self.swap, self.sems = cross, swap, sems
+
+    def copies(self):
+        for i, (src, dst) in enumerate(self.cross):
+            yield None, pltpu.make_async_remote_copy(
+                src_ref=src, dst_ref=dst, send_sem=self.sems.at[0, i], recv_sem=self.sems.at[1, i],
+                device_id=partner(), device_id_type=MESH,
+            ), None
+        target, moved = swapped()
+        for i, (src, dst) in enumerate(self.swap):
+            j = len(self.cross) + i
+            yield moved, pltpu.make_async_remote_copy(
+                src_ref=src, dst_ref=dst, send_sem=self.sems.at[0, j], recv_sem=self.sems.at[1, j],
+                device_id=target, device_id_type=MESH,
+            ), pltpu.make_async_copy(src, dst, self.sems.at[0, j])
+
+    def start(self):
+        for moved, far, near in self.copies():
+            if moved is None:
+                far.start()
+            else:
+                pl.when(moved)(lambda: far.start())
+                pl.when(jnp.logical_not(moved))(lambda: near.start())
+
+    def finish(self):
+        for moved, far, near in self.copies():
+            if moved is None:
+                far.wait()
+            else:
+                pl.when(moved)(lambda: far.wait())
+                pl.when(jnp.logical_not(moved))(lambda: near.wait())
+
+
+class Gather:
+    def __init__(self, items, send_sem, recv_sem, local_sem):
+        self.items, self.send_sem, self.recv_sem, self.local_sem = items, send_sem, recv_sem, local_sem
+        self.me = place()[0]
+
+    def order(self, part):
+        return [sides[(part + k) % 3] for k in range(3)]
+
+    def view(self, item, part, number):
+        src, out, row, parts = self.items[item]
+        rows, width = src.shape[0], src.shape[-1] // parts
+        at = pl.ds(row(number), rows)
+        if parts == 1:
+            return out.at[at]
+        return out.at[at, pl.ds(part * width, width)]
+
+    def copy(self, item, part, number, lane, target, own=False):
+        src, out, row, parts = self.items[item]
+        width = src.shape[-1] // parts
+        here = self.view(item, part, number)
+        source = (src if parts == 1 else src.at[:, pl.ds(part * width, width)]) if own else here
+        return remote(
+            source, here, self.send_sem.at[item, part, number, lane],
+            self.recv_sem.at[item, part, number], target,
+        )
+
+    def every(self):
+        return [(i, p) for i in range(len(self.items)) for p in range(self.items[i][3])]
+
+    def local(self, item):
+        src, out, row, _ = self.items[item]
+        return pltpu.make_async_copy(src, out.at[pl.ds(row(self.me), src.shape[0])], self.local_sem.at[item])
+
+    def start(self, items=None):
+        chosen = [(i, p) for i, p in self.every() if items is None or i in items]
+        for k in range(3):
+            for i, p in chosen:
+                self.copy(i, p, self.me, k, self.me ^ self.order(p)[k], True).start()
+        for i, p in chosen:
+            self.copy(i, p, self.me, 3, self.me ^ 1, True).start()
+        for i in range(len(self.items)):
+            if items is None or i in items:
+                self.local(i).start()
+
+    def arrivals(self, part, step):
+        order = self.order(part)
+        masks = [0]
+        for side in order[:step]:
+            masks = masks + [m ^ side for m in masks]
+        return [m ^ order[step] for m in masks]
+
+    def step(self, step, items=None):
+        for i, p in self.every():
+            if items is not None and i not in items:
+                continue
+            for mask in self.arrivals(p, step):
+                number = self.me ^ mask
+                self.copy(i, p, number, 0, self.me).wait_recv()
+                for k in range(step + 1, 3):
+                    self.copy(i, p, number, k, self.me ^ self.order(p)[k]).start()
+                self.copy(i, p, number, 3, self.me ^ 1).start()
+
+    def finish(self, items=None):
+        for i, p in self.every():
+            if items is not None and i not in items:
+                continue
+
+            def pair(j, carry, i=i, p=p):
+                number = (self.me ^ 1) ^ (2 * j)
+                self.copy(i, p, number, 3, self.me).wait_recv()
+                self.copy(i, p, number ^ 1, 3, self.me).wait_send()
+                return carry
+
+            lax.fori_loop(0, 8, pair, 0)
+            self.copy(i, p, self.me, 0, self.me).wait_send()
+            for step in range(3):
+                if step:
+                    self.copy(i, p, self.me, step, self.me).wait_send()
+                for mask in self.arrivals(p, step):
+                    for k in range(step + 1, 3):
+                        self.copy(i, p, self.me ^ mask, k, self.me).wait_send()
+        for i in range(len(self.items)):
+            if items is None or i in items:
+                self.local(i).wait()
+
+    @staticmethod
+    def scratch(count):
+        return [DMA((count, 3, group, 4)), DMA((count, 3, group)), DMA((count,))]
+
+
+def natural(rows):
+    return lambda number: pl.multiple_of(number * rows, rows)
+
+
+def gather_kernel(parts, columns, *refs):
+    count = len(parts)
+    ins, weight, outs, column, sems = (
+        refs[:count], refs[count], refs[count + 1 : 2 * count + 1], refs[2 * count + 1], refs[2 * count + 2 :]
+    )
+    greet_all()
+    run = Gather([(a, b, natural(a.shape[0]), p) for a, b, p in zip(ins, outs, parts)], *sems[:3])
+    deal = Deal([(weight, column, natural(columns))], *sems[3:])
+    run.start()
+    deal.start()
+    for step in range(3):
+        run.step(step)
+    run.finish()
+    deal.finish()
+
+
+def gather(arrays, parts, weight, columns, collective_id):
+    count = len(arrays)
+    outs = [((group * a.shape[0],) + a.shape[1:], a.dtype) for a in arrays]
+    outs.append(((2 * 8 * weight.shape[0], columns), bf16))
+    return pl.pallas_call(
+        functools.partial(gather_kernel, parts, columns),
+        in_specs=[ANY] * (count + 1),
+        out_specs=[ANY] * (count + 1),
+        out_shape=[jax.ShapeDtypeStruct(shape, kind) for shape, kind in outs],
+        scratch_shapes=Gather.scratch(count) + Deal.scratch(1),
+        compiler_params=pltpu.CompilerParams(collective_id=collective_id, has_side_effects=True),
+        cost_estimate=busy,
+        name=f"gather{collective_id}",
+    )(*arrays, weight)
+
+
+class Scatter:
+    def __init__(self, own, core_in, side_in, core_s, core_r, side_s, side_r):
+        self.own, self.core_in, self.side_in = own, core_in, side_in
+        self.core_s, self.core_r, self.side_s, self.side_r = core_s, core_r, side_s, side_r
+        self.me = place()[0]
+        self.core = self.me % 2
+        self.rows, self.width = own.shape[2], own.shape[3]
+        self.part = self.width // 3
+
+    def cols(self, part):
+        return pl.ds(part * self.part, self.part)
+
+    def order(self, part):
+        return [sides[(part + k) % 3] for k in range(3)]
+
+    def core_copy(self, part):
+        c = self.cols(part)
+        return remote(
+            self.own.at[1 - self.core, :, :, c], self.core_in.at[:, :, c],
+            self.core_s.at[part], self.core_r.at[part], self.me ^ 1,
+        )
+
+    def moves(self, part, step):
+        order = self.order(part)
+        masks = [0]
+        for side in order[:step:-1]:
+            masks = masks + [m ^ side for m in masks]
+        base = {0: 0, 1: 4, 2: 6}[step]
+        masks = sorted(masks, key=lambda m: [not m & side for side in order[step + 1 :]])
+        return [(m ^ order[step], base + j) for j, m in enumerate(masks)]
+
+    def side_copy(self, part, step, mask, slot):
+        c = self.cols(part)
+        peer = self.me ^ self.order(part)[step]
+        return remote(
+            self.own.at[self.core, (self.me ^ mask) // 2, :, c], self.side_in.at[slot, :, c],
+            self.side_s.at[part, slot], self.side_r.at[part, slot], peer,
+        )
+
+    def multiply(self, part, lhs, rhs):
+        c = self.cols(part)
+        chunk = 4 * self.rows
+        for q in range(4):
+            p = dot(lhs[q * chunk : (q + 1) * chunk, :], rhs[part * self.part : (part + 1) * self.part, :], 1, 1)
+            p = p.astype(bf16).reshape(4, self.rows, self.part)
+            for j in range(4):
+                self.own[j % 2, 2 * q + j // 2, :, c] = p[j]
+        self.core_copy(part).start()
+
+    def add(self, number, part, extra):
+        c = self.cols(part)
+        at = (self.core, number // 2, slice(None), c)
+        self.own[at] = (self.own[at].astype(f32) + extra.astype(f32)).astype(bf16)
+
+    def merge(self, part):
+        c = self.cols(part)
+        self.core_copy(part).wait()
+        moves = self.moves(part, 0)
+        for mask, slot in moves:
+            self.add(self.me ^ mask, part, self.core_in[(self.me ^ mask) // 2, :, c])
+            self.side_copy(part, 0, mask, slot).start()
+        for mask, _ in moves:
+            number = self.me ^ mask ^ self.order(part)[0]
+            self.add(number, part, self.core_in[number // 2, :, c])
+
+    def halve(self, part, step, out=None):
+        c = self.cols(part)
+        leaving = dict(self.moves(part, step + 1)) if step < 2 else {}
+        for mask, slot in self.moves(part, step):
+            kept = mask ^ self.order(part)[step]
+            self.side_copy(part, step, mask, slot).wait_recv()
+            if out is not None:
+                at = (self.core, self.me // 2, slice(None), c)
+                out[:, c] = self.own[at].astype(f32) + self.side_in[slot, :, c].astype(f32)
+                continue
+            self.add(self.me ^ kept, part, self.side_in[slot, :, c])
+            if kept in leaving:
+                self.side_copy(part, step + 1, kept, leaving[kept]).start()
+
+    def finish(self):
+        for part in range(3):
+            for step in range(3):
+                for mask, slot in self.moves(part, step):
+                    self.side_copy(part, step, mask, slot).wait_send()
+
+    @staticmethod
+    def scratch(rows, width):
+        return [
+            pltpu.VMEM((2, 8, rows, width), bf16), pltpu.VMEM((8, rows, width), bf16),
+            pltpu.VMEM((7, rows, width), bf16), DMA((3,)), DMA((3,)), DMA((3, 7)), DMA((3, 7)),
+        ]
+
+
+def cargo_refs(cross, swap, ins, outs, sems):
+    cube = place()[1]
+    pairs = []
+    for src, dst, whole in zip(ins, outs, list(cross) + [True] * swap):
+        if not whole:
+            rows = dst.shape[0]
+            src = src.at[pl.ds(pl.multiple_of((1 - cube) * rows, rows), rows)]
+        pairs.append((src, dst))
+    return Cargo(pairs[: len(cross)], pairs[len(cross) :], sems)
+
+
+def cargo_shapes(cross, swap):
+    shapes = []
+    for array, whole in cross:
+        rows = array.shape[0] if whole else array.shape[0] // 2
+        shapes.append(jax.ShapeDtypeStruct((rows,) + array.shape[1:], array.dtype))
+    return shapes + [jax.ShapeDtypeStruct(a.shape, a.dtype) for a in swap]
+
+
+def scatter_kernel(cross, swap, lhs, rhs, *refs):
+    count = len(cross) + swap
+    ins, out, outs, sems, scratch = refs[:count], refs[count], refs[count + 1 : 2 * count + 1], refs[2 * count + 1], refs[2 * count + 2 :]
+    greet(cross=bool(cross), swap=bool(swap))
+    cargo = cargo_refs(cross, swap, ins, outs, sems)
+    cargo.start()
+    run = Scatter(*scratch)
+    run.multiply(0, lhs, rhs)
+    run.multiply(1, lhs, rhs)
+    run.merge(0)
+    run.multiply(2, lhs, rhs)
+    run.merge(1)
+    run.merge(2)
+    for step in range(3):
+        for part in range(3):
+            run.halve(part, step, out if step == 2 else None)
+    run.finish()
+    cargo.finish()
+
+
+def scatter(lhs, rhs, collective_id, cross=(), swap=()):
+    rows, width = lhs.shape[0] // group, rhs.shape[0]
+    count = len(cross) + len(swap)
+    return pl.pallas_call(
+        functools.partial(scatter_kernel, tuple(whole for _, whole in cross), len(swap)),
+        in_specs=[VMEM, VMEM] + [ANY] * count,
+        out_specs=[VMEM] + [ANY] * count,
+        out_shape=[jax.ShapeDtypeStruct((rows, width), f32)] + cargo_shapes(cross, swap),
+        scratch_shapes=[DMA((2, max(count, 1)))] + Scatter.scratch(rows, width),
+        compiler_params=pltpu.CompilerParams(
+            collective_id=collective_id, has_side_effects=True, vmem_limit_bytes=56 * 2**20
+        ),
+        cost_estimate=busy,
+        name=f"scatter{collective_id}",
+    )(lhs, rhs, *[a for a, _ in cross], *swap)
+
+
+def head_of(number, heads):
+    return number * heads // group
+
+
+def is_active(number, heads):
+    return (number + 1) * heads // group > number * heads // group
+
+
+def owner_of(head, heads):
+    return ((head + 1) * group + heads - 1) // heads - 1
+
+
+class Deal:
+    def __init__(self, items, send_sem, recv_sem, local_sem):
+        self.items, self.send_sem, self.recv_sem, self.local_sem = items, send_sem, recv_sem, local_sem
+        self.me = everywhere()
+
+    def views(self, item, source, target):
+        own, out, column = self.items[item]
+        rows, width = own.shape[0] // 2, out.shape[1]
+        number, cube = anyone(source)
+        half = pl.ds(pl.multiple_of(number // 8 * rows, rows), rows)
+        row = (cube * 8 + number % 8) * (2 * rows) + number // 8 * rows
+        cols = pl.ds(column(anyone(target)[0]), width)
+        return own.at[half, cols], out.at[pl.ds(pl.multiple_of(row, rows), rows)]
+
+    def copy(self, item, source, target):
+        src, dst = self.views(item, source, target)
+        return pltpu.make_async_remote_copy(
+            src_ref=src, dst_ref=dst, send_sem=self.send_sem.at[item, target],
+            recv_sem=self.recv_sem.at[item, source], device_id=device(*anyone(target)), device_id_type=MESH,
+        )
+
+    def local(self, item):
+        src, dst = self.views(item, self.me, self.me)
+        return pltpu.make_async_copy(src, dst, self.local_sem.at[item])
+
+    def start(self):
+        def begin(mask, carry):
+            for i in range(len(self.items)):
+                self.copy(i, self.me, self.me ^ mask).start()
+            return carry
+
+        lax.fori_loop(1, 2 * group, begin, 0)
+        for i in range(len(self.items)):
+            self.local(i).start()
+
+    def finish(self):
+        def end(mask, carry):
+            for i in range(len(self.items)):
+                self.copy(i, self.me ^ mask, self.me).wait_recv()
+                self.copy(i, self.me, self.me ^ mask).wait_send()
+            return carry
+
+        lax.fori_loop(1, 2 * group, end, 0)
+        for i in range(len(self.items)):
+            self.local(i).wait()
+
+    @staticmethod
+    def scratch(count):
+        return [DMA((count, 2 * group)), DMA((count, 2 * group)), DMA((count,))]
+
+
+def first_kernel(
+    head_width, heads, given, places, gain, w_q, w_k, w_v, tokens, tokens_all, places_all, w_head,
+    land, places_land, normed, cargo_sem, *sems,
+):
+    greet_all()
+    cargo = Cargo([], [(given, land), (places, places_land)], cargo_sem)
+    cargo.start()
+    column = lambda number: pl.multiple_of(head_of(number, heads) * head_width, head_width)
+    deal = Deal(
+        [
+            (w, w_head.at[:, pl.ds(i * head_width, head_width)], column)
+            for i, w in enumerate((w_q, w_k, w_v))
+        ],
+        *sems[3:],
+    )
+    deal.start()
+    cargo.finish()
+    value = land[...].astype(f32)
+    factor = lax.rsqrt(jnp.mean(value * value, axis=-1, keepdims=True) + norm_eps)
+    normed[...] = (value * factor * gain[...]).astype(bf16)
+    run = Gather(
+        [(normed, tokens_all, natural(normed.shape[0]), 3), (places_land, places_all, natural(1), 1)], *sems[:3]
+    )
+    run.start()
+    tokens[...] = land[...]
+    for step in range(3):
+        run.step(step)
+    run.finish()
+    deal.finish()
+
+
+def first_exchange(given, places, gain, weights, heads, head_width, collective_id):
+    rows, width = given.shape
+    outs = [
+        ((rows, width), bf16), ((group * rows, width), bf16), ((group,) + places.shape[1:], jnp.int32),
+        ((width, 3 * head_width), bf16),
+    ]
+    return pl.pallas_call(
+        functools.partial(first_kernel, head_width, heads),
+        in_specs=[VMEM, VMEM, VMEM] + [ANY] * 3,
+        out_specs=[VMEM] + [ANY] * 3,
+        out_shape=[jax.ShapeDtypeStruct(shape, kind) for shape, kind in outs],
+        scratch_shapes=[
+            pltpu.VMEM((rows, width), bf16), pltpu.VMEM(places.shape, jnp.int32),
+            pltpu.VMEM((rows, width), bf16), DMA((2, 2)),
+        ] + Gather.scratch(2) + Deal.scratch(3),
+        compiler_params=pltpu.CompilerParams(
+            collective_id=collective_id, has_side_effects=True, vmem_limit_bytes=32 * 2**20
+        ),
+        cost_estimate=busy,
+        name="first_exchange",
+    )(given, places, gain, *weights)
+
+
+class Restore:
+    def __init__(self, grads, land, sources, column, send_sem, recv_sem, local_sem):
+        self.grads, self.land, self.sources, self.column = grads, land, sources, column
+        self.send_sem, self.recv_sem, self.local_sem = send_sem, recv_sem, local_sem
+        self.me = place()[0]
+        self.count, self.rows = land.shape[0], land.shape[1]
+        self.width = grads.shape[1] // self.count
+
+    def move(self, i, source, target):
+        rows = pl.ds(pl.multiple_of(target % 8 * self.rows, self.rows), self.rows)
+        src = self.grads.at[rows, pl.ds(i * self.width, self.width)]
+        return src, self.land.at[i, :, pl.ds(self.column(source), self.width)]
+
+    def send(self, i, source, target):
+        src, dst = self.move(i, source, target)
+        return remote(src, dst, self.send_sem.at[i, target], self.recv_sem.at[i, source], target)
+
+    def keep(self, i):
+        src, dst = self.move(i, self.me, self.me)
+        return pltpu.make_async_copy(src, dst, self.local_sem.at[i])
+
+    def start(self):
+        def begin(mask, carry):
+            for i in range(self.count):
+                pl.when(self.sources(self.me))(lambda: self.send(i, self.me, self.me ^ mask).start())
+            return carry
+
+        lax.fori_loop(1, group, begin, 0)
+        for i in range(self.count):
+            pl.when(self.sources(self.me))(lambda: self.keep(i).start())
+
+    def finish(self):
+        def taken(mask, carry):
+            for i in range(self.count):
+                other = self.me ^ mask
+                pl.when(self.sources(other))(lambda: self.send(i, other, self.me).wait_recv())
+                pl.when(self.sources(self.me))(lambda: self.send(i, self.me, other).wait_send())
+            return carry
+
+        lax.fori_loop(1, group, taken, 0)
+        for i in range(self.count):
+            pl.when(self.sources(self.me))(lambda: self.keep(i).wait())
+
+    @staticmethod
+    def scratch(count, rows, total):
+        return [
+            pltpu.VMEM((count, rows, total), bf16), DMA((count, group)), DMA((count, group)), DMA((count,)),
+        ]
+
+
+def last_kernel(
+    heads, head_width, columns, ffn, head, small, out_sum, output, *refs,
+):
+    outs, (total_out, pair_out, output_out), refs = refs[:6], refs[6:9], refs[9:]
+    ffn_land, *ffn_sems = refs[:4]
+    head_land, *head_sems = refs[4:8]
+    land, send_sem, recv_sem, pair_sem, cargo_sem = refs[8:]
+    me = everywhere()
+    greet_all()
+    cargo = Cargo([], [(output, output_out)], cargo_sem)
+    pair = remote(out_sum, pair_out, pair_sem.at[0], pair_sem.at[1], place()[0] ^ 8)
+
+    def send(source, target):
+        return pltpu.make_async_remote_copy(
+            src_ref=small, dst_ref=land.at[source], send_sem=send_sem.at[target],
+            recv_sem=recv_sem.at[source], device_id=device(*anyone(target)), device_id_type=MESH,
+        )
+
+    def begin(mask, carry):
+        send(me, me ^ mask).start()
+        return carry
+
+    def taken(mask, carry):
+        send(me ^ mask, me).wait_recv()
+        send(me, me ^ mask).wait_send()
+        return carry
+
+    lax.fori_loop(1, 2 * group, begin, 0)
+    land[me] = small[...]
+    pair.start()
+    cargo.start()
+    first = Restore(ffn, ffn_land, lambda n: n >= 0, natural(columns), *ffn_sems)
+    column = lambda n: pl.multiple_of(head_of(n, heads) * head_width, head_width)
+    second = Restore(head, head_land, lambda n: is_active(n, heads), column, *head_sems)
+    second.start()
+    first.start()
+    lax.fori_loop(1, 2 * group, taken, 0)
+    result = land[0]
+    for number in range(1, 2 * group):
+        result = result + land[number]
+    total_out[...] = result
+    second.finish()
+    for i in range(3):
+        outs[3 + i][...] = head_land[i].astype(f32)
+    first.finish()
+    for i in range(3):
+        outs[i][...] = ffn_land[i].astype(f32)
+    pair.wait()
+    cargo.finish()
+
+
+def last_exchange(ffn, head, small, out_sum, output, heads, columns, collective_id):
+    rows, width = out_sum.shape
+    head_width = head.shape[1] // 3
+    hidden = columns * group
+    outs = [((rows, hidden), f32)] * 3 + [((rows, width), f32)] * 3
+    outs += [(small.shape, f32), (out_sum.shape, bf16), (output.shape, bf16)]
+    return pl.pallas_call(
+        functools.partial(last_kernel, heads, head_width, columns),
+        in_specs=[ANY, ANY, VMEM, ANY, ANY],
+        out_specs=[VMEM] * 7 + [ANY] * 2,
+        out_shape=[jax.ShapeDtypeStruct(shape, kind) for shape, kind in outs],
+        scratch_shapes=Restore.scratch(3, rows, hidden) + Restore.scratch(3, rows, width) + [
+            pltpu.VMEM((2 * group,) + small.shape, f32), DMA((2 * group,)), DMA((2 * group,)),
+            DMA((2,)), DMA((2, 1)),
+        ],
+        compiler_params=pltpu.CompilerParams(
+            collective_id=collective_id, has_side_effects=True, vmem_limit_bytes=48 * 2**20
+        ),
+        cost_estimate=busy,
+        name="last_exchange",
+    )(ffn, head, small, out_sum, output)
 
 
 def rotated(value, cosine, sine, inverse=False):
@@ -45,11 +672,59 @@
 
 
 def forward_kernel(
-    block, lam_ref, qkv_ref, cos_ref, sin_ref, gain_ref,
-    q_ref, k_ref, v_ref, kt_ref, o1_ref, o2_ref, lse_ref, att_ref,
-    qt_ref, vt_ref,
+    block, share, lam_ref, qkv_ref, cos_ref, sin_ref, gain_ref, *refs,
 ):
     step = pl.program_id(0)
+    if share:
+        (w_one, w_two, w_rows, given), refs = refs[:4], refs[4:]
+    q_ref, k_ref, v_ref, kt_ref, o1_ref, o2_ref, lse_ref, *refs = refs
+    if share:
+        out_ref, both_ref, w_all, taken_ref = refs[:4]
+        qt_ref, vt_ref, att_ref, w_land, send_sem, recv_sem, local_sem, cargo_sem, *sems = refs[4:]
+        me, cube = place()
+        columns = both_ref.shape[1] // 2
+        deal = Deal(
+            [
+                (w, both_ref.at[:, pl.ds(i * columns, columns)], natural(columns))
+                for i, w in enumerate((w_one, w_two))
+            ],
+            *sems[3:],
+        )
+        sub = w_land.shape[0]
+        w_half = w_rows.at[pl.ds(pl.multiple_of(me // 8 * sub, sub), sub)]
+
+        def spot(which):
+            return lambda number: pl.multiple_of((which * 8 + number % 8) * (2 * sub) + number // 8 * sub, sub)
+
+        run = Gather([(w_half, w_all, spot(cube), 3), (w_land, w_all, spot(1 - cube), 3)], *sems[:3])
+        rows_cargo = Cargo([(w_half, w_land)], [], cargo_sem.at[0])
+        token_cargo = Cargo([], [(given, taken_ref)], cargo_sem.at[1])
+
+        @pl.when(step == 0)
+        def _():
+            greet_all()
+            rows_cargo.start()
+            run.start([0])
+            token_cargo.start()
+            deal.start()
+
+        @pl.when(step == 1)
+        def _():
+            rows_cargo.finish()
+            run.start([1])
+            run.step(0, [0])
+
+        @pl.when(step == 2)
+        def _():
+            run.step(1, [0])
+            run.step(0, [1])
+
+        @pl.when(step == 3)
+        def _():
+            run.step(2, [0])
+            run.step(1, [1])
+    else:
+        att_ref, qt_ref, vt_ref = refs
     width = v_ref.shape[1]
     half = width // 2
     length = q_ref.shape[0]
@@ -117,9 +792,47 @@
     factor = lax.rsqrt(jnp.mean(mixed * mixed, axis=0, keepdims=True) + norm_eps)
     attended = mixed * factor * gain_ref[...] * (1.0 - lam_init)
     att_ref[own, :] = attended.T.astype(bf16)
-
-
-def forward_attention(lam, qkv, cosine, sine, gain, block):
+    if share:
+        rows, heads = out_ref.shape[0], out_ref.shape[1] // width
+        active = is_active(me, heads)
+
+        def part(number, head):
+            cols = pl.ds(pl.multiple_of(head * width, width), width)
+            return att_ref.at[pl.ds(pl.multiple_of(number * rows, rows), rows)], out_ref.at[:, cols]
+
+        def send(number, head):
+            src, dst = part(number, head)
+            return remote(src, dst, send_sem.at[number], recv_sem.at[head], number)
+
+        def keep():
+            src, dst = part(me, head_of(me, heads))
+            return pltpu.make_async_copy(src, dst, local_sem.at[0])
+
+        for j in range(block // rows):
+            number = step * (block // rows) + j
+            pl.when(active & (number != me))(lambda: send(number, head_of(me, heads)).start())
+            pl.when(active & (number == me))(lambda: keep().start())
+
+        @pl.when(step == pl.num_programs(0) - 1)
+        def _():
+            def sent(number, carry):
+                pl.when(active & (number != me))(lambda: send(number, 0).wait_send())
+                return carry
+
+            def taken(head, carry):
+                pl.when(owner_of(head, heads) != me)(lambda: send(me, head).wait_recv())
+                return carry
+
+            lax.fori_loop(0, heads, taken, 0)
+            lax.fori_loop(0, group, sent, 0)
+            pl.when(active)(lambda: keep().wait())
+            run.step(2, [1])
+            run.finish()
+            token_cargo.finish()
+            deal.finish()
+
+
+def forward_attention(lam, qkv, cosine, sine, gain, block, weights=(), rows=0, heads=0, columns=0, collective_id=None):
     width = qkv.shape[0] // 3
     length = qkv.shape[1]
     full = lambda shape: pl.BlockSpec(shape, lambda i: (0,) * len(shape))
@@ -131,34 +844,50 @@
         ((width, length), f32),
         ((width, length), f32),
         ((8, length), f32),
-        ((length, width), bf16),
     ]
+    scratch = [pltpu.VMEM((width, length), bf16), pltpu.VMEM((width, length), bf16)]
+    out_specs = [full(shape) for shape, _ in outs]
+    share = bool(weights)
+    if share:
+        wide = heads * width
+        more = [((rows, wide), bf16), ((wide, 2 * columns), bf16), ((wide, wide), bf16), ((rows, wide), bf16)]
+        outs, out_specs = outs + more, out_specs + [ANY] * 4
+        scratch += [
+            pltpu.VMEM((length, width), bf16), pltpu.VMEM((weights[2].shape[0] // 2, wide), bf16),
+            DMA((group,)), DMA((heads,)), DMA((1,)), DMA((2, 2, 1)),
+        ]
+        scratch += Gather.scratch(2) + Deal.scratch(2)
+    else:
+        outs, out_specs = outs + [((length, width), bf16)], out_specs + [full((length, width))]
     return pl.pallas_call(
-        functools.partial(forward_kernel, block),
+        functools.partial(forward_kernel, block, share),
         grid=(length // block,),
-        in_specs=[
-            pl.BlockSpec(memory_space=pltpu.SMEM),
-            full(qkv.shape),
-            full(cosine.shape),
-            full(sine.shape),
-            full(gain.shape),
-        ],
-        out_specs=[full(shape) for shape, _ in outs],
+        in_specs=[SMEM] + [full(a.shape) for a in (qkv, cosine, sine, gain)] + [ANY] * len(weights),
+        out_specs=out_specs,
         out_shape=[jax.ShapeDtypeStruct(shape, kind) for shape, kind in outs],
-        scratch_shapes=[pltpu.VMEM((width, length), bf16), pltpu.VMEM((width, length), bf16)],
+        scratch_shapes=scratch,
         compiler_params=pltpu.CompilerParams(
-            dimension_semantics=("arbitrary",), vmem_limit_bytes=60 * 2**20
+            dimension_semantics=("arbitrary",), vmem_limit_bytes=56 * 2**20,
+            collective_id=collective_id, has_side_effects=share,
         ),
+        cost_estimate=busy,
         name="attention_forward",
-    )(lam, qkv, cosine, sine, gain)
+    )(lam, qkv, cosine, sine, gain, *weights)
 
 
 def backward_kernel(
-    block, lam_ref, q_ref, k_ref, v_ref, kt_ref, o1_ref, o2_ref, lse_ref, datt_ref,
-    cos_ref, sin_ref, gain_ref,
-    dqkv_ref, dgain_ref, dlam_ref,
-    dmix_ref, dmixt_ref, delta_ref, dqt_ref,
+    block, share, lam_ref, q_ref, k_ref, v_ref, kt_ref, o1_ref, o2_ref, lse_ref, datt_ref,
+    cos_ref, sin_ref, gain_ref, *refs,
 ):
+    if share:
+        cargo_in, refs = refs[0], refs[1:]
+    dqkv_ref, dgain_ref, dlam_ref, *refs = refs
+    if share:
+        cargo_out, refs = refs[0], refs[1:]
+    dmix_ref, dmixt_ref, delta_ref, dqt_ref, *refs = refs
+    if share:
+        cargo_sem, *refs = refs
+        cargo = cargo_refs((False,), 0, [cargo_in], [cargo_out], cargo_sem)
     step = pl.program_id(0)
     blocks = pl.num_programs(0)
     width = v_ref.shape[1]
@@ -166,9 +895,14 @@
     length = q_ref.shape[0]
     scale = half ** -0.5
     lam = lam_ref[0]
+    used = lam_ref[1] > 0.0
 
     @pl.when(step == 0)
     def _():
+        if share:
+            greet_all()
+            collect(cargo, datt_ref, *refs)
+        source = refs[0] if share else datt_ref
         dgain_ref[...] = jnp.zeros_like(dgain_ref)
         dlam_ref[...] = jnp.zeros_like(dlam_ref)
         dqt_ref[...] = jnp.zeros_like(dqt_ref)
@@ -178,7 +912,7 @@
             first, second = o1_ref[:, cols], o2_ref[:, cols]
             mixed = first - lam * second
             factor = lax.rsqrt(jnp.mean(mixed * mixed, axis=0, keepdims=True) + norm_eps)
-            upstream = datt_ref[cols, :].astype(f32).T * (1.0 - lam_init)
+            upstream = source[cols, :].astype(f32).T * (1.0 - lam_init)
             dgain_ref[...] += jnp.sum(upstream * mixed * factor, axis=1, keepdims=True)
             scaled = upstream * gain_ref[...]
             dmixed = factor * scaled - mixed * (factor * factor * factor) * jnp.mean(
@@ -237,51 +971,88 @@
     dkeys, dvalues = lax.fori_loop(
         step + 1, blocks, lambda index, now: visit(index, now, False), state
     )
-    both = jnp.concatenate(dkeys, axis=1).T * scale
+    both = jnp.where(used, jnp.concatenate(dkeys, axis=1).T * scale, 0.0)
     dqkv_ref[own, width : 2 * width] = (
         rotated(both, cos_ref[:, own], sin_ref[:, own], True).T.astype(bf16)
     )
-    dqkv_ref[own, 2 * width : 3 * width] = dvalues.astype(bf16)
+    dqkv_ref[own, 2 * width : 3 * width] = jnp.where(used, dvalues, 0.0).astype(bf16)
 
     dqkv_ref[own, 0:width] = (
-        rotated(dqt_ref[:, own] * scale, cos_ref[:, own], sin_ref[:, own], True).T.astype(bf16)
-    )
-
-
-def backward_attention(lam, q, k, v, kt, o1, o2, lse, datt, cosine, sine, gain, block):
+        rotated(jnp.where(used, dqt_ref[:, own] * scale, 0.0), cos_ref[:, own], sin_ref[:, own], True).T.astype(bf16)
+    )
+    if share:
+        pl.when(step == blocks - 1)(lambda: cargo.finish())
+
+
+def collect(cargo, grad_ref, out_ref, send_sem, recv_sem, local_sem):
+    me = place()[0]
+    rows = grad_ref.shape[0]
+    width = out_ref.shape[1]
+    heads = grad_ref.shape[1] // width
+    active = is_active(me, heads)
+
+    def move(head, number):
+        src = grad_ref.at[:, pl.ds(pl.multiple_of(head * width, width), width)]
+        dst = out_ref.at[pl.ds(pl.multiple_of(number * rows, rows), rows)]
+        return src, dst
+
+    def send(head, number):
+        src, dst = move(head, number)
+        return remote(src, dst, send_sem.at[head], recv_sem.at[number], owner_of(head, heads))
+
+    def keep():
+        src, dst = move(head_of(me, heads), me)
+        return pltpu.make_async_copy(src, dst, local_sem.at[0])
+
+    def begin(head, carry):
+        pl.when(owner_of(head, heads) != me)(lambda: send(head, me).start())
+        return carry
+
+    def taken(number, carry):
+        pl.when(active & (number != me))(lambda: send(0, number).wait_recv())
+        return carry
+
+    def sent(head, carry):
+        pl.when(owner_of(head, heads) != me)(lambda: send(head, me).wait_send())
+        return carry
+
+    lax.fori_loop(0, heads, begin, 0)
+    pl.when(active)(lambda: keep().start())
+    cargo.start()
+    lax.fori_loop(0, group, taken, 0)
+    pl.when(active)(lambda: keep().wait())
+    lax.fori_loop(0, heads, sent, 0)
+
+
+def backward_attention(lam, q, k, v, kt, o1, o2, lse, datt, cosine, sine, gain, block, cargo=None, collective_id=None):
     length, width = q.shape
     full = lambda shape: pl.BlockSpec(shape, lambda i: (0,) * len(shape))
     arrays = (q, k, v, kt, o1, o2, lse, datt, cosine, sine, gain)
     outs = [((length, 3 * width), bf16), ((width, 1), f32), ((1, 1), f32)]
+    share = collective_id is not None
+    more, cargo_out, cargo_in = [], [], []
+    if share:
+        cargo_out, cargo_in = cargo_shapes([(cargo, False)], ()), [cargo]
+        more = [DMA((2, 1)), pltpu.VMEM((length, width), bf16), DMA((datt.shape[1] // width,)), DMA((group,)), DMA((1,))]
     return pl.pallas_call(
-        functools.partial(backward_kernel, block),
+        functools.partial(backward_kernel, block, share),
         grid=(length // block,),
-        in_specs=[pl.BlockSpec(memory_space=pltpu.SMEM)] + [full(a.shape) for a in arrays],
-        out_specs=[full(shape) for shape, _ in outs],
-        out_shape=[jax.ShapeDtypeStruct(shape, kind) for shape, kind in outs],
+        in_specs=[SMEM] + [full(a.shape) for a in arrays] + [ANY] * len(cargo_in),
+        out_specs=[full(shape) for shape, _ in outs] + [ANY] * len(cargo_in),
+        out_shape=[jax.ShapeDtypeStruct(shape, kind) for shape, kind in outs] + cargo_out,
         scratch_shapes=[
             pltpu.VMEM((length, width), bf16),
             pltpu.VMEM((width, length), bf16),
             pltpu.VMEM((8, length), f32),
             pltpu.VMEM((width, length), f32),
-        ],
+        ] + more,
         compiler_params=pltpu.CompilerParams(
-            dimension_semantics=("arbitrary",), vmem_limit_bytes=60 * 2**20
+            dimension_semantics=("arbitrary",), vmem_limit_bytes=56 * 2**20,
+            collective_id=collective_id, has_side_effects=share,
         ),
+        cost_estimate=busy,
         name="attention_backward",
-    )(lam, *arrays)
-
-
-def gather_rows(value):
-    return lax.all_gather(value, "seq", axis=0, tiled=True)
-
-
-def scatter_sum(value):
-    return lax.psum_scatter(value, "seq", scatter_dimension=0, tiled=True)
-
-
-def exchange(value):
-    return lax.all_to_all(value, "seq", split_axis=0, concat_axis=0, tiled=True)
+    )(lam, *arrays, *cargo_in)
 
 
 def rms_parts(value):
@@ -295,7 +1066,129 @@
     return grad, jnp.sum(upstream * value * factor, axis=0)
 
 
-def body(
+def cube_body(
+    block_input, positions, needle, cotangent, norm_gain1, w_query, w_key, w_value,
+    lam_q1, lam_k1, lam_q2, lam_k2, sub_gain, w_out, norm_gain2, w_gate, w_up, w_down,
+):
+    rows, width = block_input.shape[1:]
+    heads, half = lam_q1.shape
+    head_width = sub_gain.shape[0]
+    hidden = w_gate.shape[1]
+    depth = w_query.shape[0]
+    length = rows * group
+    columns = hidden // group
+    y = lax.axis_index("batch")
+    me, cube = place()
+    my_head = head_of(me, heads)
+    used = is_active(me, heads)
+    active = used.astype(f32)
+    here = jnp.broadcast_to(positions[0], (1, 8, rows))
+    tokens_low, normed_all, places, w_head = first_exchange(
+        block_input[0], here, norm_gain1[None], (w_query, w_key, w_value), heads, head_width, 0
+    )
+    tokens = tokens_low.astype(f32)
+    factor1 = rms_parts(tokens)
+    upstream = cotangent[0].astype(f32) * needle[0].astype(f32)[:, None]
+    upstream_low = upstream.astype(bf16)
+    places = places[:, 0].reshape(length)
+
+    inv_freq = jnp.exp(-math.log(10000.0) * jnp.arange(half // 2, dtype=f32) / (half // 2))
+    angles = inv_freq[:, None] * places.astype(f32)[None, :]
+    cosine, sine = jnp.cos(angles), jnp.sin(angles)
+    lam_vals, lam_pull = jax.vjp(lambdas, lam_q1, lam_k1, lam_q2, lam_k2)
+    lam_mine = jnp.stack([lax.dynamic_index_in_dim(lam_vals, my_head, 0, False), active])
+    gain_col = sub_gain[:, None]
+    block = 4 * rows
+
+    qkv = dot(w_head, normed_all, 0, 1)
+    q, k, v, kt, o1, o2, lse, attended, w_gates, w_o, grad_low = forward_attention(
+        lam_mine, qkv, cosine, sine, gain_col, block,
+        (w_gate, w_up, w_out, upstream_low), rows, heads, columns, 1,
+    )
+    resid = tokens + dot(attended, w_o)
+    factor2 = rms_parts(resid)
+    normed_two = (resid * factor2 * norm_gain2).astype(bf16)
+    two_all, grad_all, w_d = gather([normed_two, grad_low], (3, 3), w_down, columns, 2)
+
+    both = dot(two_all, w_gates)
+    gate, upper = both[:, :columns], both[:, columns:]
+    grad_inner = dot(grad_all, w_d)
+    sigma = jax.nn.sigmoid(gate)
+    silu = gate * sigma
+    inner = (silu * upper).astype(bf16)
+    gate_low = (grad_inner * upper * sigma * (1.0 + gate * (1.0 - sigma))).astype(bf16)
+    upper_low = (grad_inner * silu).astype(bf16)
+    gates_low = jnp.concatenate([gate_low, upper_low], axis=1)
+    gate_grads = dot(two_all, gates_low, 0, 0).astype(bf16)
+    down_grads = dot(grad_all, inner, 0, 0).astype(bf16)
+    early = jnp.concatenate([gate_grads[:, :columns], down_grads[:, : columns // 2]], axis=1)
+    later = jnp.concatenate([gate_grads[:, columns:], down_grads[:, columns // 2 :]], axis=1)
+    grad_two, early_theirs = scatter(gates_low, w_gates, 3, [(early, False)])
+
+    grad_resid_two, gain_two = rms_back(resid, factor2, norm_gain2, grad_two)
+    grad_resid = grad_low.astype(f32) + grad_resid_two
+    resid_low = grad_resid.astype(bf16)
+    grad_att = dot(resid_low, w_o, 1, 1).astype(bf16)
+
+    def combine(mine, theirs):
+        part = mine.shape[0] // 2
+        mine = lax.dynamic_slice_in_dim(mine, cube * part, part, 0)
+        return (mine.astype(f32) + theirs.astype(f32)).astype(bf16)
+
+    dqkv, dgain, dlam, later_theirs = backward_attention(
+        lam_mine, q, k, v, kt, o1, o2, lse, grad_att, cosine, sine, gain_col, block, later, 4,
+    )
+    head_grads = dot(normed_all, dqkv, 0, 0).astype(bf16)
+    grad_normed, head_theirs = scatter(dqkv, w_head, 8, [(head_grads, False)])
+    grad_tokens, gain_one = rms_back(tokens, factor1, norm_gain1, grad_normed)
+    input_low = (grad_resid + grad_tokens).astype(bf16)
+    out_part, input_back = scatter(attended.T, resid_low.T, 7, [], [input_low])
+    out_part = out_part.astype(bf16)
+    ffn_out, out_theirs = scatter(inner, w_d, 5, [(out_part, True)])
+    output_low = (resid + ffn_out).astype(bf16)
+    out_sum = (out_part.astype(f32) + out_theirs.astype(f32)).astype(bf16)
+    early_sum, later_sum = combine(early, early_theirs), combine(later, later_theirs)
+    ffn_sum = jnp.concatenate(
+        [early_sum[:, :columns], later_sum[:, :columns], early_sum[:, columns:], later_sum[:, columns:]], axis=1
+    )
+
+    hot = jax.nn.one_hot(my_head, heads, dtype=f32)
+    mine = jnp.concatenate([dgain[:, 0], hot * dlam[0, 0]])
+    small = jnp.concatenate([gain_one, gain_two, jnp.where(used, mine, 0.0)])
+    count = small.shape[0]
+    lanes = -(-count // 1024) * 128
+    small = jnp.pad(small, (0, 8 * lanes - count)).reshape(8, lanes)
+    *grads, small, out_pair, output_back = last_exchange(
+        ffn_sum, combine(head_grads, head_theirs), small, out_sum, output_low, heads, columns, 6
+    )
+    small = small.reshape(-1)
+    output = output_back[None]
+    input_grad = input_back.astype(f32)[None]
+    out_grads = jnp.where(y == cube, out_sum, out_pair).astype(f32)
+    gain_one, gain_two = small[:width], small[width : 2 * width]
+    sub_grad = small[2 * width : 2 * width + head_width]
+    lam_grads = lam_pull(small[2 * width + head_width : count])
+    squares = sum(jnp.sum(g * g) for g in lam_grads)
+    return (
+        output, input_grad, gain_one, grads[3], grads[4], grads[5],
+        lam_grads[0], lam_grads[1], lam_grads[2], lam_grads[3], sub_grad, out_grads, gain_two,
+        grads[0], grads[1], grads[2], jnp.mean(lam_vals), jnp.sqrt(squares),
+    )
+
+
+def gather_rows(value):
+    return lax.all_gather(value, "seq", axis=0, tiled=True)
+
+
+def scatter_sum(value):
+    return lax.psum_scatter(value, "seq", scatter_dimension=0, tiled=True)
+
+
+def exchange(value):
+    return lax.all_to_all(value, "seq", split_axis=0, concat_axis=0, tiled=True)
+
+
+def plain_body(
     devices, block_input, positions, needle, cotangent, norm_gain1, w_query, w_key, w_value,
     lam_q1, lam_k1, lam_q2, lam_k2, sub_gain, w_out, norm_gain2, w_gate, w_up, w_down,
 ):
@@ -306,8 +1199,6 @@
     depth = w_query.shape[0]
     length = rows * devices
     columns = hidden // devices
-    if heads > devices or hidden % devices:
-        raise ValueError("unsupported mesh")
     head_of = [d * heads // devices for d in range(devices)]
     owner_of = [max(d for d in range(devices) if head_of[d] == h) for h in range(heads)]
     me = lax.axis_index("seq")
@@ -337,7 +1228,7 @@
     angles = inv_freq[:, None] * places.astype(f32)[None, :]
     cosine, sine = jnp.cos(angles), jnp.sin(angles)
     lam_vals, lam_pull = jax.vjp(lambdas, lam_q1, lam_k1, lam_q2, lam_k2)
-    lam_mine = lax.dynamic_slice_in_dim(lam_vals, my_head, 1, 0)
+    lam_mine = jnp.stack([lax.dynamic_index_in_dim(lam_vals, my_head, 0, False), active])
     gain_col = sub_gain[:, None]
     block = math.gcd(length, 512)
 
@@ -425,7 +1316,8 @@
         P("batch", "seq", None), P("batch", "seq", None), P(), rows, rows, rows,
         P(), P(), P(), P(), P(), rows, P(), rows, rows, rows, P(), P(),
     )
-    return jax.shard_map(
-        functools.partial(body, mesh.shape["seq"]),
-        mesh=mesh, in_specs=in_specs, out_specs=out_specs, check_vma=False,
-    )
+    if mesh.shape["seq"] == group and mesh.shape["batch"] == 2:
+        body = cube_body
+    else:
+        body = functools.partial(plain_body, mesh.shape["seq"])
+    return jax.shard_map(body, mesh=mesh, in_specs=in_specs, out_specs=out_specs, check_vma=False)

time: 810 us -> 605 us (0.75)
  the two profiles are of different devices: /device:TPU:0 before, /device:TPU:9 now
where the time goes in v3:
time: 605 us; the launch traced here: 595 us
  Pallas kernels  502 us (83%)
  matrix products  31.9 us (5%)
  other arithmetic  30.5 us (5%)
  local copies, waits for them, and re-layouts  23.9 us (4%)
  between operations  7.29 us (1%)
    pallas_call x4, Pallas kernels, scatter(): pl.pallas_call(functools.partial(scatter_kernel, tuple((whole for _, whol...  175 us
    pallas_call x1, Pallas kernels, forward_attention(): pl.pallas_call(functools.partial(forward_kernel, block, share), grid=(len...  81.5 us
    pallas_call x1, Pallas kernels, last_exchange(): pl.pallas_call(functools.partial(last_kernel, heads, head_width, columns)...  75.4 us
    pallas_call x1, Pallas kernels, gather(): pl.pallas_call(functools.partial(gather_kernel, parts, columns), in_specs...  68 us
    pallas_call x1, Pallas kernels, first_exchange(): pl.pallas_call(functools.partial(first_kernel, head_width, heads), in_spe...  66.8 us
    pallas_call x1, Pallas kernels, backward_attention(): pl.pallas_call(functools.partial(backward_kernel, block, share), grid=(le...  34.9 us
    dot_general x8, matrix products, dot(): lax.dot_general(left, right, dims(left_axis, right_axis), preferred_eleme...  31.9 us
    unnamed x90, local copies, waits for them, and re-layouts  14.8 us

profile of v3, /device:TPU:9, one launch (start us, length us, event | category | flops | bytes accessed | tf_op | source)
XLA Modules:
  0.0 595.5 jit_solution(5801092815907172992)
XLA Ops:
  0.7 0.7 convert_bitcast_fusion.1
  1.4 0.9 multiply_reduce_fusion.7
  2.3 0.5 copy-done.27
  2.8 0.6 fusion.13
  4.0 0.6 dynamic_slice.13
  4.6 1.2 pad_maximum_fusion.4.lam_ref
  5.9 0.7 broadcast_in_dim.40.places
  6.5 0.7 broadcast_in_dim.41.gain
  7.2 1.4 copy.46.gain_ref
  8.6 1.9 fusion.9.refs_3_
  10.5 1.0 copy-done.4
  11.5 1.0 copy-done.5
  12.4 1.0 copy-done.6
  13.4 1.0 copy-done.7
  14.4 66.8 %first_exchange.1 = (bf16[128,1536]{1,0:T(8,128)(2,1)S(1)}, bf16[2048,1536]{1,0:T(8,128)(2,1)S(1)}, s32[16,8,128]{2,1,0:T(8,128)S(1)}, bf16[1536,384]{1,0:T(8,128)(2,1)S(1)}) custom-call(bf16[128,1536]{1,0:T(8,128)(2,1)S(1)} %bitcast.36, s32[1,8,128]{2,1,0:T(8,128)S(1)} %broadcast_in_dim.40.places, f32[1,1536]{1,0:T(1,128)S(1)} %broadcast_in_dim.41.gain, ...), custom_call_target="tpu_custom_call" | custom-call | flops 40000000000 | bytes 10000000 | tf_op jit(solution)/shard_map/first_exchange/pallas_call | solution.py:521
  81.4 0.7 multiply_multiply_fusion
  82.1 2.4 multiply_sine_fusion
  84.5 4.4 fusion.17.qkv_ref
  88.9 81.5 %attention_forward.1 = (bf16[2048,128]{1,0:T(8,128)(2,1)}, bf16[2048,128]{1,0:T(8,128)(2,1)}, bf16[2048,128]{1,0:T(8,128)(2,1)}, bf16[128,2048]{1,0:T(8,128)(2,1...) custom-call(f32[2]{0:T(128)} %pad_maximum_fusion.4.lam_ref, ...), custom_call_target="tpu_custom_call" | custom-call | flops 40000000000 | bytes 10000000 | tf_op jit(solution)/shard_map/attention_forward/pallas_call | solution.py:862
  170.4 1.9 copy.54
  172.3 3.3 multiply_reduce_fusion.2
  175.7 1.0 multiply_convert_fusion.3.refs_0_
  176.7 68.0 %gather2.1 = (bf16[2048,1536]{1,0:T(8,128)(2,1)}, bf16[2048,1536]{1,0:T(8,128)(2,1)}, bf16[1536,256]{1,0:T(8,128)(2,1)}) custom-call(bf16[128,1536]{1,0:T(8,128)(2,1)} %multiply_convert_fusion.3.refs_0_, bf16[128,1536]{1,0:T(8,128)(2,1)} %get-tuple-element.63.refs_1_, bf16[96,4096]{1,0:T(8,128)(2,1)} %refs_2_.3), custom_call_target="tpu_custom_call" | custom-call | flops 40000000000 | bytes 10000000 | tf_op jit(solution)/shard_map/gather2/pallas_call | solution.py:260
  244.7 5.6 fusion.18
  250.4 2.4 multiply_convert_fusion.2
  252.9 1.8 convolution_convert_fusion.2
  254.8 3.5 convolution_convert_fusion
  258.2 1.6 pad_maximum_fusion.lhs
  260.0 1.1 pad_maximum_fusion.2.refs_0_
  261.1 1.1 pad_maximum_fusion.1.refs_0_
  262.2 53.8 %scatter3.1 = (f32[128,1536]{1,0:T(8,128)}, bf16[768,384]{1,0:T(8,128)(2,1)}) custom-call(bf16[2048,512]{1,0:T(8,128)(2,1)} %pad_maximum_fusion.lhs, bf16[1536,512]{1,0:T(8,128)(2,1)} %get-tuple-element.67.rhs, bf16[1536,384]{1,0:T(8,128)(2,1)} %pad_maximum_fusion.1.refs_0_), custom_call_target="tpu_custom_call" | custom-call | flops 40000000000 | bytes 10000000 | tf_op jit(solution)/shard_map/scatter3/pallas_call | solution.py:407
  316.0 1.3 add_convert_fusion.2
  317.6 1.0 convert_bitcast_fusion
  318.6 0.9 copy-done.12
  319.5 4.9 convolution_convert_fusion.3.datt_ref
  324.4 34.9 %attention_backward.1 = (bf16[2048,384]{1,0:T(8,128)(2,1)}, f32[128,1]{1,0:T(8,128)}, f32[1,1]{1,0:T(1,128)}, bf16[768,384]{1,0:T(8,128)(2,1)}) custom-call(f32[2]{0:T(128)} %pad_maximum_fusion.4.lam_ref, bf16[2048,128]{1,0:T(8,128)(2,1)} %get-tuple-element.69.q_ref, bf16[2048,128]{1,0:T(8,128)(2,1)} %get-tuple-element.70.k_ref, ...), custom_call_target="tpu_custom_call" | custom-call | flops 40000000000 | bytes 10000000 | tf_op jit(solution)/shard_map/attention_backward/pallas_call | solution.py:1037
  359.3 5.9 convolution_convert_fusion.1.refs_0_
  365.2 1.9 copy.55.rhs
  367.1 0.6 compare_select_fusion
  367.8 1.2 add_convert_fusion.1
  369.4 44.1 %scatter8.1 = (f32[128,1536]{1,0:T(8,128)}, bf16[768,384]{1,0:T(8,128)(2,1)}) custom-call(bf16[2048,384]{1,0:T(8,128)(2,1)} %get-tuple-element.78.lhs, bf16[1536,384]{1,0:T(8,128)(2,1)} %copy-done.9, bf16[1536,384]{1,0:T(8,128)(2,1)} %convolution_convert_fusion.1.refs_0_), custom_call_target="tpu_custom_call" | custom-call | flops 40000000000 | bytes 10000000 | tf_op jit(solution)/shard_map/scatter8/pallas_call | solution.py:407
  413.6 2.1 add_convert_fusion.head
  416.0 1.1 fusion.7.refs_0_
  417.1 36.0 %scatter7.1 = (f32[96,1536]{1,0:T(8,128)}, bf16[128,1536]{1,0:T(8,128)(2,1)}) custom-call(bf16[1536,128]{1,0:T(8,128)(2,1)} %bitcast.39, bf16[1536,128]{1,0:T(8,128)(2,1)} %copy.55.rhs, bf16[128,1536]{1,0:T(8,128)(2,1)} %fusion.7.refs_0_), custom_call_target="tpu_custom_call" | custom-call | flops 40000000000 | bytes 10000000 | tf_op jit(solution)/shard_map/scatter7/pallas_call | solution.py:407
  453.2 1.8 convert_element_type.144.refs_0_
  455.0 41.4 %scatter5.1 = (f32[128,1536]{1,0:T(8,128)}, bf16[96,1536]{1,0:T(8,128)(2,1)}) custom-call(bf16[2048,256]{1,0:T(8,128)(2,1)} %copy-done.34, bf16[1536,256]{1,0:T(8,128)(2,1)} %get-tuple-element.66.rhs, bf16[96,1536]{1,0:T(8,128)(2,1)} %convert_element_type.144.refs_0_), custom_call_target="tpu_custom_call" | custom-call | flops 40000000000 | bytes 10000000 | tf_op jit(solution)/shard_map/scatter5/pallas_call | solution.py:407
  496.4 1.3 add_convert_fusion.3.output
  497.9 1.0 bitcast_convert_fusion
  498.8 75.4 %last_exchange.1 = (f32[96,4096]{1,0:T(8,128)}, f32[96,4096]{1,0:T(8,128)}, f32[96,4096]{1,0:T(8,128)}, f32[96,1536]{1,0:T(8,128)S(1)}, f32[96,1536]{1,0:T(8,128...) custom-call(bf16[768,768]{1,0:T(8,128)(2,1)S(1)} %pad_maximum_fusion, ...), custom_call_target="tpu_custom_call" | custom-call | flops 40000000000 | bytes 10000000 | tf_op jit(solution)/shard_map/last_exchange/pallas_call | solution.py:645
  574.3 0.7 copy-done.3
  575.0 0.5 slice.79
  575.6 0.6 slice.67
  576.2 0.6 slice.63
  576.8 2.0 multiply_reduce_fusion.3
  578.8 2.0 multiply_reduce_fusion.5
  583.4 0.9 select_convert_fusion
  584.3 1.9 copy.68
  586.1 0.8 copy.69
  587.0 0.8 copy.70
  587.8 0.8 copy.71
  588.6 1.1 copy.72
  589.7 1.1 copy.73
  590.9 0.8 copy-done.17
  591.7 1.1 copy.74
  (99 shorter events, 1.4 us)
Async XLA Ops:
  2.3 0.5 copy-start.27
  2.3 1.1 copy-start.29
  10.5 1.0 copy-start.4
  11.5 1.0 copy-start.5
  12.4 1.0 copy-start.6
  13.4 1.0 copy-start.7
  81.2 3.3 copy-start.8
  81.2 3.3 copy-start.9
  81.2 91.1 %copy-start = (bf16[128,1536]{1,0:T(8,128)(2,1)}, bf16[128,1536]{1,0:T(8,128)(2,1)S(1)}, u32[]{:S(2)}) copy-start(bf16[128,1536]{1,0:T(8,128)(2,1)S(1)} %get-tuple-element.57) | copy-start | bytes 1179652
  172.3 3.4 copy-start.24
  175.7 141.9 %copy-start.10 = (f32[128,1536]{1,0:T(8,128)}, f32[128,1536]{1,0:T(8,128)S(1)}, u32[]{:S(2)}) copy-start(f32[128,1536]{1,0:T(8,128)S(1)} %get-tuple-element.134) | copy-start | bytes 2359300
  176.7 68.0 %copy-start.35 = (bf16[1536,512]{1,0:T(8,128)(2,1)S(1)}, bf16[1536,512]{1,0:T(8,128)(2,1)}, u32[]{:S(2)}) copy-start(bf16[1536,512]{1,0:T(8,128)(2,1)} %get-tuple-element.67.rhs) | copy-start | bytes 4718596
  244.7 5.7 copy-start.33
  244.7 5.7 copy-start.36
  244.7 10.0 %slice-start.2 = ((s8[6291456]{0:T(1024)(128)(4,1)}), s8[4194304]{0:T(1024)(128)(4,1)S(1)}, s32[]{:S(2)}) async-start(s8[6291456]{0:T(1024)(128)(4,1)} %bitcast.45), calls=%async_computation.2 | async-start | bytes 8388608
  250.4 4.3 slice-start.3
  252.9 1.9 copy-start.34
  316.0 1.3 copy-start.14
  316.0 1.6 copy-start.20
  318.6 0.9 copy-start.12
  319.5 39.8 %slice-start = ((s8[6291456]{0:T(1024)(128)(4,1)}), s8[4194304]{0:T(1024)(128)(4,1)S(1)}, s32[]{:S(2)}) async-start(s8[6291456]{0:T(1024)(128)(4,1)} %bitcast.37), calls=%async_computation | async-start | bytes 8388608
  324.4 34.9 %slice-start.1 = ((s8[6291456]{0:T(1024)(128)(4,1)}), s8[2097152]{0:T(1024)(128)(4,1)S(1)}, s32[]{:S(2)}) async-start(s8[6291456]{0:T(1024)(128)(4,1)} %bitcast.37), calls=%async_computation.1 | async-start | bytes 4194304
  365.2 3.8 copy-start.26
  369.4 44.2 %copy-start.22 = (bf16[1536,384]{1,0:T(8,128)(2,1)S(1)}, bf16[1536,384]{1,0:T(8,128)(2,1)}, u32[]{:S(2)}) copy-start(bf16[1536,384]{1,0:T(8,128)(2,1)} %convolution_convert_fusion.1.refs_0_) | copy-start | bytes 3538948
  369.4 46.4 %copy-start.1 = (bf16[128,1536]{1,0:T(8,128)(2,1)S(1)}, bf16[128,1536]{1,0:T(8,128)(2,1)}, u32[]{:S(2)}) copy-start(bf16[128,1536]{1,0:T(8,128)(2,1)} %copy-done) | copy-start | bytes 1179652
  369.4 46.4 %copy-start.25 = (f32[1536]{0:T(1024)S(1)}, f32[1536]{0:T(1024)}, u32[]{:S(2)}) copy-start(f32[1536]{0:T(1024)} %param.22) | copy-start | bytes 18436
  369.4 46.4 %copy-start.31 = (f32[128]{0:T(128)S(1)}, f32[128]{0:T(128)}, u32[]{:S(2)}) copy-start(f32[128]{0:T(128)} %get-tuple-element.130) | copy-start | bytes 1540
  413.6 2.2 copy-start.15
  413.6 2.4 copy-start.13
  413.6 2.4 copy-start.32
  455.0 41.4 %copy-start.11 = (f32[128,1536]{1,0:T(8,128)S(1)}, f32[128,1536]{1,0:T(8,128)}, u32[]{:S(2)}) copy-start(f32[128,1536]{1,0:T(8,128)} %copy-done.10) | copy-start | bytes 2359300
  496.4 1.4 copy-start.16
  496.4 1.4 copy-start.23
  496.4 1.5 copy-start.21
  496.4 2.4 copy-start.2
  498.8 76.2 %copy-start.28 = (f32[12]{0:T(128)S(1)}, f32[12]{0:T(128)}, u32[]{:S(2)}) copy-start(f32[12]{0:T(128)} %copy-done.27) | copy-start | bytes 148
  498.8 76.2 %copy-start.30 = (f32[12]{0:T(128)S(1)}, f32[12]{0:T(128)}, u32[]{:S(2)}) copy-start(f32[12]{0:T(128)} %copy-done.29) | copy-start | bytes 148
  574.3 0.7 copy-start.3
  584.3 4.3 copy-start.19
  587.8 2.0 copy-start.18
  589.7 2.0 copy-start.17

commit v4 on v3

--- a/solution.py
+++ b/solution.py
@@ -33,13 +33,18 @@
 
 
 MESH = pl.DeviceIdType.MESH
-ANY = pl.BlockSpec(memory_space=pl.ANY)
+ANY = pl.BlockSpec(memory_space=pltpu.HBM)
 VMEM = pl.BlockSpec(memory_space=pltpu.VMEM)
 SMEM = pl.BlockSpec(memory_space=pltpu.SMEM)
 DMA = pltpu.SemaphoreType.DMA
 group = 16
 busy = pl.CostEstimate(flops=4 * 10**10, bytes_accessed=10**7, transcendentals=0)
 sides = (8, 4, 2)
+even = ((8, 4, 2), (4, 2, 8), (2, 8, 4))
+few_z = ((4, 8, 2), (4, 2, 8))
+mid_z = ((4, 8, 2), (4, 2, 8), (2, 4, 8), (8, 4, 2))
+sum_even = ((2, 8, 4), (8, 2, 4), (4, 2, 8))
+sum_few_z = ((2, 8, 4), (8, 2, 4))
 
 
 def place():
@@ -144,12 +149,14 @@
 
 
 class Gather:
-    def __init__(self, items, send_sem, recv_sem, local_sem):
-        self.items, self.send_sem, self.recv_sem, self.local_sem = items, send_sem, recv_sem, local_sem
+    def __init__(self, orders, items, send_sem, recv_sem, local_sem):
+        self.orders = orders
+        self.items = [item if len(item) == 4 else item + (len(orders),) for item in items]
+        self.send_sem, self.recv_sem, self.local_sem = send_sem, recv_sem, local_sem
         self.me = place()[0]
 
     def order(self, part):
-        return [sides[(part + k) % 3] for k in range(3)]
+        return list(self.orders[part])
 
     def view(self, item, part, number):
         src, out, row, parts = self.items[item]
@@ -164,10 +171,8 @@
         width = src.shape[-1] // parts
         here = self.view(item, part, number)
         source = (src if parts == 1 else src.at[:, pl.ds(part * width, width)]) if own else here
-        return remote(
-            source, here, self.send_sem.at[item, part, number, lane],
-            self.recv_sem.at[item, part, number], target,
-        )
+        arrival = self.recv_sem.at[item, 0, group] if lane == 3 else self.recv_sem.at[item, part, number]
+        return remote(source, here, self.send_sem.at[item], arrival, target)
 
     def every(self):
         return [(i, p) for i in range(len(self.items)) for p in range(self.items[i][3])]
@@ -206,83 +211,70 @@
                 self.copy(i, p, number, 3, self.me ^ 1).start()
 
     def finish(self, items=None):
-        for i, p in self.every():
-            if items is not None and i not in items:
-                continue
-
-            def pair(j, carry, i=i, p=p):
-                number = (self.me ^ 1) ^ (2 * j)
-                self.copy(i, p, number, 3, self.me).wait_recv()
-                self.copy(i, p, number ^ 1, 3, self.me).wait_send()
-                return carry
-
-            lax.fori_loop(0, 8, pair, 0)
-            self.copy(i, p, self.me, 0, self.me).wait_send()
-            for step in range(3):
-                if step:
-                    self.copy(i, p, self.me, step, self.me).wait_send()
-                for mask in self.arrivals(p, step):
-                    for k in range(step + 1, 3):
-                        self.copy(i, p, self.me ^ mask, k, self.me).wait_send()
         for i in range(len(self.items)):
             if items is None or i in items:
+                src, out = self.items[i][:2]
+                for blocks, sem in ((8, self.recv_sem.at[i, 0, group]), (15, self.send_sem.at[i])):
+                    some = out.at[pl.ds(0, blocks * src.shape[0])]
+                    pltpu.make_async_copy(some, some, sem).wait()
                 self.local(i).wait()
 
     @staticmethod
     def scratch(count):
-        return [DMA((count, 3, group, 4)), DMA((count, 3, group)), DMA((count,))]
+        return [DMA((count,)), DMA((count, 4, group + 1)), DMA((count,))]
 
 
 def natural(rows):
     return lambda number: pl.multiple_of(number * rows, rows)
 
 
-def gather_kernel(parts, columns, *refs):
-    count = len(parts)
-    ins, weight, outs, column, sems = (
-        refs[:count], refs[count], refs[count + 1 : 2 * count + 1], refs[2 * count + 1], refs[2 * count + 2 :]
-    )
-    greet_all()
-    run = Gather([(a, b, natural(a.shape[0]), p) for a, b, p in zip(ins, outs, parts)], *sems[:3])
-    deal = Deal([(weight, column, natural(columns))], *sems[3:])
-    run.start()
-    deal.start()
+def second_kernel(normed, given, grads, normed_all, grads_all, cargo_sem, *sems):
+    greet(swap=True)
+    cargo = Cargo([], [(given, grads)], cargo_sem)
+    cargo.start()
+    row = natural(normed.shape[0])
+    run = Gather(even, [(normed, normed_all, row), (grads, grads_all, row)], *sems[:3])
+    run.start([0])
+    run.step(0, [0])
+    run.step(1, [0])
+    cargo.finish()
+    run.start([1])
+    run.step(2, [0])
     for step in range(3):
-        run.step(step)
+        run.step(step, [1])
     run.finish()
-    deal.finish()
-
-
-def gather(arrays, parts, weight, columns, collective_id):
-    count = len(arrays)
-    outs = [((group * a.shape[0],) + a.shape[1:], a.dtype) for a in arrays]
-    outs.append(((2 * 8 * weight.shape[0], columns), bf16))
+
+
+def second_exchange(normed, given, collective_id):
+    rows, width = normed.shape
+    outs = [(rows, width), (group * rows, width), (group * rows, width)]
     return pl.pallas_call(
-        functools.partial(gather_kernel, parts, columns),
-        in_specs=[ANY] * (count + 1),
-        out_specs=[ANY] * (count + 1),
-        out_shape=[jax.ShapeDtypeStruct(shape, kind) for shape, kind in outs],
-        scratch_shapes=Gather.scratch(count) + Deal.scratch(1),
+        second_kernel,
+        in_specs=[ANY] * 2,
+        out_specs=[ANY] * 3,
+        out_shape=[jax.ShapeDtypeStruct(shape, bf16) for shape in outs],
+        scratch_shapes=[DMA((2, 1))] + Gather.scratch(2),
         compiler_params=pltpu.CompilerParams(collective_id=collective_id, has_side_effects=True),
         cost_estimate=busy,
-        name=f"gather{collective_id}",
-    )(*arrays, weight)
+        name="second_exchange",
+    )(normed, given)
 
 
 class Scatter:
-    def __init__(self, own, core_in, side_in, core_s, core_r, side_s, side_r):
+    def __init__(self, orders, own, core_in, side_in, core_s, core_r, side_s, side_r):
+        self.orders, self.parts = orders, len(orders)
         self.own, self.core_in, self.side_in = own, core_in, side_in
         self.core_s, self.core_r, self.side_s, self.side_r = core_s, core_r, side_s, side_r
         self.me = place()[0]
         self.core = self.me % 2
         self.rows, self.width = own.shape[2], own.shape[3]
-        self.part = self.width // 3
+        self.part = self.width // self.parts
 
     def cols(self, part):
         return pl.ds(part * self.part, self.part)
 
     def order(self, part):
-        return [sides[(part + k) % 3] for k in range(3)]
+        return list(self.orders[part])
 
     def core_copy(self, part):
         c = self.cols(part)
@@ -311,11 +303,16 @@
     def multiply(self, part, lhs, rhs):
         c = self.cols(part)
         chunk = 4 * self.rows
-        for q in range(4):
-            p = dot(lhs[q * chunk : (q + 1) * chunk, :], rhs[part * self.part : (part + 1) * self.part, :], 1, 1)
+
+        def quarter(q, carry):
+            left = lhs[pl.ds(pl.multiple_of(q * chunk, chunk), chunk), :]
+            p = dot(left, rhs[part * self.part : (part + 1) * self.part, :], 1, 1)
             p = p.astype(bf16).reshape(4, self.rows, self.part)
             for j in range(4):
                 self.own[j % 2, 2 * q + j // 2, :, c] = p[j]
+            return carry
+
+        lax.fori_loop(0, 4, quarter, 0)
         self.core_copy(part).start()
 
     def add(self, number, part, extra):
@@ -333,6 +330,13 @@
         for mask, _ in moves:
             number = self.me ^ mask ^ self.order(part)[0]
             self.add(number, part, self.core_in[number // 2, :, c])
+
+    def begin(self, lhs, rhs):
+        self.multiply(0, lhs, rhs)
+        for part in range(1, self.parts):
+            self.multiply(part, lhs, rhs)
+            self.merge(part - 1)
+        self.merge(self.parts - 1)
 
     def halve(self, part, step, out=None):
         c = self.cols(part)
@@ -348,8 +352,12 @@
             if kept in leaving:
                 self.side_copy(part, step + 1, kept, leaving[kept]).start()
 
+    def halve_all(self, step, out):
+        for part in range(self.parts):
+            self.halve(part, step, out if step == 2 else None)
+
     def finish(self):
-        for part in range(3):
+        for part in range(self.parts):
             for step in range(3):
                 for mask, slot in self.moves(part, step):
                     self.side_copy(part, step, mask, slot).wait_send()
@@ -358,64 +366,44 @@
     def scratch(rows, width):
         return [
             pltpu.VMEM((2, 8, rows, width), bf16), pltpu.VMEM((8, rows, width), bf16),
-            pltpu.VMEM((7, rows, width), bf16), DMA((3,)), DMA((3,)), DMA((3, 7)), DMA((3, 7)),
+            pltpu.VMEM((7, rows, width), bf16), DMA((4,)), DMA((4,)), DMA((4, 7)), DMA((4, 7)),
         ]
 
 
-def cargo_refs(cross, swap, ins, outs, sems):
-    cube = place()[1]
-    pairs = []
-    for src, dst, whole in zip(ins, outs, list(cross) + [True] * swap):
-        if not whole:
-            rows = dst.shape[0]
-            src = src.at[pl.ds(pl.multiple_of((1 - cube) * rows, rows), rows)]
-        pairs.append((src, dst))
-    return Cargo(pairs[: len(cross)], pairs[len(cross) :], sems)
-
-
-def cargo_shapes(cross, swap):
-    shapes = []
-    for array, whole in cross:
-        rows = array.shape[0] if whole else array.shape[0] // 2
-        shapes.append(jax.ShapeDtypeStruct((rows,) + array.shape[1:], array.dtype))
-    return shapes + [jax.ShapeDtypeStruct(a.shape, a.dtype) for a in swap]
-
-
-def scatter_kernel(cross, swap, lhs, rhs, *refs):
-    count = len(cross) + swap
-    ins, out, outs, sems, scratch = refs[:count], refs[count], refs[count + 1 : 2 * count + 1], refs[2 * count + 1], refs[2 * count + 2 :]
-    greet(cross=bool(cross), swap=bool(swap))
-    cargo = cargo_refs(cross, swap, ins, outs, sems)
+def for_partner(grads, rows):
+    return grads.at[pl.ds(pl.multiple_of((1 - place()[1]) * rows, rows), rows)]
+
+
+def scatter_kernel(lhs, rhs, lhs_two, rhs_two, given, out, out_two, taken, cargo_sem, *scratch):
+    greet(cross=True)
+    cargo = Cargo([(for_partner(given, taken.shape[0]), taken)], [], cargo_sem)
+    run, more = Scatter(sum_even, *scratch[:7]), Scatter(sum_even, *scratch[7:])
+    run.begin(lhs, rhs)
+    more.begin(lhs_two, rhs_two)
     cargo.start()
-    run = Scatter(*scratch)
-    run.multiply(0, lhs, rhs)
-    run.multiply(1, lhs, rhs)
-    run.merge(0)
-    run.multiply(2, lhs, rhs)
-    run.merge(1)
-    run.merge(2)
     for step in range(3):
-        for part in range(3):
-            run.halve(part, step, out if step == 2 else None)
+        run.halve_all(step, out)
+        more.halve_all(step, out_two)
     run.finish()
+    more.finish()
     cargo.finish()
 
 
-def scatter(lhs, rhs, collective_id, cross=(), swap=()):
+def scatter(lhs, rhs, lhs_two, rhs_two, given, collective_id):
     rows, width = lhs.shape[0] // group, rhs.shape[0]
-    count = len(cross) + len(swap)
     return pl.pallas_call(
-        functools.partial(scatter_kernel, tuple(whole for _, whole in cross), len(swap)),
-        in_specs=[VMEM, VMEM] + [ANY] * count,
-        out_specs=[VMEM] + [ANY] * count,
-        out_shape=[jax.ShapeDtypeStruct((rows, width), f32)] + cargo_shapes(cross, swap),
-        scratch_shapes=[DMA((2, max(count, 1)))] + Scatter.scratch(rows, width),
+        scatter_kernel,
+        in_specs=[VMEM] * 4 + [ANY],
+        out_specs=[VMEM, VMEM, ANY],
+        out_shape=[jax.ShapeDtypeStruct((rows, width), f32)] * 2
+        + [jax.ShapeDtypeStruct((given.shape[0] // 2, given.shape[1]), bf16)],
+        scratch_shapes=[DMA((2, 1))] + Scatter.scratch(rows, width) + Scatter.scratch(rows, width),
         compiler_params=pltpu.CompilerParams(
             collective_id=collective_id, has_side_effects=True, vmem_limit_bytes=56 * 2**20
         ),
         cost_estimate=busy,
         name=f"scatter{collective_id}",
-    )(lhs, rhs, *[a for a, _ in cross], *swap)
+    )(lhs, rhs, lhs_two, rhs_two, given)
 
 
 def head_of(number, heads):
@@ -431,8 +419,8 @@
 
 
 class Deal:
-    def __init__(self, items, send_sem, recv_sem, local_sem):
-        self.items, self.send_sem, self.recv_sem, self.local_sem = items, send_sem, recv_sem, local_sem
+    def __init__(self, items, send_sem, recv_sem):
+        self.items, self.send_sem, self.recv_sem = items, send_sem, recv_sem
         self.me = everywhere()
 
     def views(self, item, source, target):
@@ -444,46 +432,58 @@
         cols = pl.ds(column(anyone(target)[0]), width)
         return own.at[half, cols], out.at[pl.ds(pl.multiple_of(row, rows), rows)]
 
-    def copy(self, item, source, target):
+    def copy(self, item, source, target, far):
         src, dst = self.views(item, source, target)
         return pltpu.make_async_remote_copy(
-            src_ref=src, dst_ref=dst, send_sem=self.send_sem.at[item, target],
-            recv_sem=self.recv_sem.at[item, source], device_id=device(*anyone(target)), device_id_type=MESH,
+            src_ref=src, dst_ref=dst, send_sem=self.send_sem.at[item, far],
+            recv_sem=self.recv_sem.at[item, far], device_id=device(*anyone(target)), device_id_type=MESH,
         )
 
     def local(self, item):
         src, dst = self.views(item, self.me, self.me)
-        return pltpu.make_async_copy(src, dst, self.local_sem.at[item])
-
-    def start(self):
+        return pltpu.make_async_copy(src, dst, self.recv_sem.at[item, 0])
+
+    def whole(self, item, sem, blocks):
+        own, out, _ = self.items[item]
+        some = out.at[pl.ds(0, blocks * own.shape[0] // 2)]
+        pltpu.make_async_copy(some, some, sem).wait()
+
+    def start_near(self):
         def begin(mask, carry):
             for i in range(len(self.items)):
-                self.copy(i, self.me, self.me ^ mask).start()
+                self.copy(i, self.me, self.me ^ (mask % 8 + mask // 8 * group), 0).start()
             return carry
 
-        lax.fori_loop(1, 2 * group, begin, 0)
+        lax.fori_loop(1, group, begin, 0)
         for i in range(len(self.items)):
             self.local(i).start()
 
-    def finish(self):
-        def end(mask, carry):
+    def start_far(self):
+        def begin(mask, carry):
             for i in range(len(self.items)):
-                self.copy(i, self.me ^ mask, self.me).wait_recv()
-                self.copy(i, self.me, self.me ^ mask).wait_send()
+                self.copy(i, self.me, self.me ^ (8 + mask % 8 + mask // 8 * group), 1).start()
             return carry
 
-        lax.fori_loop(1, 2 * group, end, 0)
+        lax.fori_loop(0, group, begin, 0)
+
+    def finish_near(self):
         for i in range(len(self.items)):
-            self.local(i).wait()
+            self.whole(i, self.recv_sem.at[i, 0], group)
+            self.whole(i, self.send_sem.at[i, 0], group - 1)
+
+    def finish_far(self):
+        for i in range(len(self.items)):
+            self.whole(i, self.recv_sem.at[i, 1], group)
+            self.whole(i, self.send_sem.at[i, 1], group)
 
     @staticmethod
     def scratch(count):
-        return [DMA((count, 2 * group)), DMA((count, 2 * group)), DMA((count,))]
+        return [DMA((count, 2)), DMA((count, 2))]
 
 
 def first_kernel(
-    head_width, heads, given, places, gain, w_q, w_k, w_v, tokens, tokens_all, places_all, w_head,
-    land, places_land, normed, cargo_sem, *sems,
+    head_width, heads, columns, given, places, gain, w_q, w_k, w_v, w_down,
+    tokens, tokens_all, places_all, w_head, w_d, land, places_land, normed, cargo_sem, *sems,
 ):
     greet_all()
     cargo = Cargo([], [(given, land), (places, places_land)], cargo_sem)
@@ -494,41 +494,55 @@
             (w, w_head.at[:, pl.ds(i * head_width, head_width)], column)
             for i, w in enumerate((w_q, w_k, w_v))
         ],
-        *sems[3:],
-    )
-    deal.start()
+        *sems[3:5],
+    )
+    own = natural(columns)
+    down = Deal([(w_down, w_d, own)], *sems[5:7])
+    deal.start_near()
+    down.start_near()
     cargo.finish()
     value = land[...].astype(f32)
     factor = lax.rsqrt(jnp.mean(value * value, axis=-1, keepdims=True) + norm_eps)
     normed[...] = (value * factor * gain[...]).astype(bf16)
     run = Gather(
-        [(normed, tokens_all, natural(normed.shape[0]), 3), (places_land, places_all, natural(1), 1)], *sems[:3]
+        mid_z, [(normed, tokens_all, natural(normed.shape[0])), (places_land, places_all, natural(1), 1)], *sems[:3]
     )
     run.start()
+    deal.start_far()
     tokens[...] = land[...]
-    for step in range(3):
-        run.step(step)
+    run.step(0)
+    down.start_far()
+    run.step(1)
+    run.step(2)
     run.finish()
-    deal.finish()
-
-
-def first_exchange(given, places, gain, weights, heads, head_width, collective_id):
+    for some in (deal, down):
+        some.finish_near()
+        some.finish_far()
+
+
+def gate_deal(w_gate, w_up, w_gates, sems):
+    columns = w_gates.shape[1] // 2
+    views = [w_gates.at[:, pl.ds(i * columns, columns)] for i in range(2)]
+    return Deal([(w, view, natural(columns)) for w, view in zip((w_gate, w_up), views)], *sems)
+
+
+def first_exchange(given, places, gain, weights, heads, head_width, columns, collective_id):
     rows, width = given.shape
     outs = [
         ((rows, width), bf16), ((group * rows, width), bf16), ((group,) + places.shape[1:], jnp.int32),
-        ((width, 3 * head_width), bf16),
+        ((width, 3 * head_width), bf16), ((width, columns), bf16),
     ]
     return pl.pallas_call(
-        functools.partial(first_kernel, head_width, heads),
-        in_specs=[VMEM, VMEM, VMEM] + [ANY] * 3,
-        out_specs=[VMEM] + [ANY] * 3,
+        functools.partial(first_kernel, head_width, heads, columns),
+        in_specs=[VMEM, VMEM, VMEM] + [ANY] * 4,
+        out_specs=[VMEM] + [ANY] * 4,
         out_shape=[jax.ShapeDtypeStruct(shape, kind) for shape, kind in outs],
         scratch_shapes=[
             pltpu.VMEM((rows, width), bf16), pltpu.VMEM(places.shape, jnp.int32),
             pltpu.VMEM((rows, width), bf16), DMA((2, 2)),
-        ] + Gather.scratch(2) + Deal.scratch(3),
+        ] + Gather.scratch(2) + Deal.scratch(3) + Deal.scratch(1),
         compiler_params=pltpu.CompilerParams(
-            collective_id=collective_id, has_side_effects=True, vmem_limit_bytes=32 * 2**20
+            collective_id=collective_id, has_side_effects=True, vmem_limit_bytes=60 * 2**20
         ),
         cost_estimate=busy,
         name="first_exchange",
@@ -542,6 +556,7 @@
         self.me = place()[0]
         self.count, self.rows = land.shape[0], land.shape[1]
         self.width = grads.shape[1] // self.count
+        self.blocks = land.shape[2] // self.width // 2
 
     def move(self, i, source, target):
         rows = pl.ds(pl.multiple_of(target % 8 * self.rows, self.rows), self.rows)
@@ -550,113 +565,174 @@
 
     def send(self, i, source, target):
         src, dst = self.move(i, source, target)
-        return remote(src, dst, self.send_sem.at[i, target], self.recv_sem.at[i, source], target)
+        return remote(src, dst, self.send_sem.at[i, 0], self.recv_sem.at[i, source], target)
 
     def keep(self, i):
         src, dst = self.move(i, self.me, self.me)
         return pltpu.make_async_copy(src, dst, self.local_sem.at[i])
 
+    def pass_on(self, i, source):
+        here = self.move(i, source, self.me)[1]
+        return remote(here, here, self.send_sem.at[i, 1], self.recv_sem.at[i, group], self.me ^ 8)
+
     def start(self):
+        mine = self.sources(self.me)
+
         def begin(mask, carry):
             for i in range(self.count):
-                pl.when(self.sources(self.me))(lambda: self.send(i, self.me, self.me ^ mask).start())
+                pl.when(mine)(lambda: self.send(i, self.me, self.me ^ mask).start())
             return carry
 
-        lax.fori_loop(1, group, begin, 0)
+        lax.fori_loop(1, 8, begin, 0)
         for i in range(self.count):
-            pl.when(self.sources(self.me))(lambda: self.keep(i).start())
+            pl.when(mine)(lambda: self.keep(i).start())
+
+    def middle(self):
+        mine = self.sources(self.me)
+
+        def forward(mask, carry):
+            other = self.me ^ mask
+            for i in range(self.count):
+
+                @pl.when(self.sources(other))
+                def _():
+                    self.send(i, other, self.me).wait_recv()
+                    self.pass_on(i, other).start()
+
+            return carry
+
+        for i in range(self.count):
+
+            @pl.when(mine)
+            def _():
+                self.keep(i).wait()
+                self.pass_on(i, self.me).start()
+
+        lax.fori_loop(1, 8, forward, 0)
 
     def finish(self):
-        def taken(mask, carry):
-            for i in range(self.count):
-                other = self.me ^ mask
-                pl.when(self.sources(other))(lambda: self.send(i, other, self.me).wait_recv())
-                pl.when(self.sources(self.me))(lambda: self.send(i, self.me, other).wait_send())
-            return carry
-
-        lax.fori_loop(1, group, taken, 0)
+        mine = self.sources(self.me)
+
+        def wait(i, blocks, sem):
+            some = self.land.at[i, :, pl.ds(0, blocks * self.width)]
+            pltpu.make_async_copy(some, some, sem).wait()
+
         for i in range(self.count):
-            pl.when(self.sources(self.me))(lambda: self.keep(i).wait())
+            pl.when(mine)(lambda: wait(i, 7, self.send_sem.at[i, 0]))
+            wait(i, self.blocks, self.send_sem.at[i, 1])
+            wait(i, self.blocks, self.recv_sem.at[i, group])
 
     @staticmethod
-    def scratch(count, rows, total):
-        return [
-            pltpu.VMEM((count, rows, total), bf16), DMA((count, group)), DMA((count, group)), DMA((count,)),
-        ]
+    def scratch(count):
+        return [DMA((count, 2)), DMA((count, group + 1)), DMA((count,))]
 
 
 def last_kernel(
-    heads, head_width, columns, ffn, head, small, out_sum, output, *refs,
+    heads, head_width, columns,
+    dqkv, w_head, tokens, gain, grad_resid, head, small, ffn_sum, out_sum,
+    ffn_out, head_out, pair_out, total_out, input_out,
+    result8, input_low, small_all, small_land, head_land, head_sum,
+    cargo_sem, pair_sem, total_send, total_recv, *refs,
 ):
-    outs, (total_out, pair_out, output_out), refs = refs[:6], refs[6:9], refs[9:]
-    ffn_land, *ffn_sems = refs[:4]
-    head_land, *head_sems = refs[4:8]
-    land, send_sem, recv_sem, pair_sem, cargo_sem = refs[8:]
-    me = everywhere()
+    me, cube = place()
+    width = tokens.shape[1]
     greet_all()
-    cargo = Cargo([], [(output, output_out)], cargo_sem)
-    pair = remote(out_sum, pair_out, pair_sem.at[0], pair_sem.at[1], place()[0] ^ 8)
+    run = Scatter(sum_even, *refs[:7])
+    sems = refs[7:]
+    column = lambda n: pl.multiple_of(head_of(n, heads) * head_width, head_width)
+    ffn_back = Restore(ffn_sum, ffn_out, lambda n: n >= 0, natural(columns), *sems[0:3])
+    head_back = Restore(head_sum, head_out, lambda n: is_active(n, heads), column, *sems[3:6])
+    half = head_land.shape[0]
+    head_cargo = Cargo([(for_partner(head, half), head_land)], [], cargo_sem.at[0])
+    input_cargo = Cargo([], [(input_low, input_out)], cargo_sem.at[1])
+    small_cargo = Cargo([(small_all.at[me], small_land)], [], cargo_sem.at[3])
+    pair = remote(out_sum, pair_out, pair_sem.at[0], pair_sem.at[1], me ^ 8)
 
     def send(source, target):
-        return pltpu.make_async_remote_copy(
-            src_ref=small, dst_ref=land.at[source], send_sem=send_sem.at[target],
-            recv_sem=recv_sem.at[source], device_id=device(*anyone(target)), device_id_type=MESH,
+        return remote(
+            small_all.at[me], small_all.at[source], total_send.at[target], total_recv.at[source], target
         )
+
+    head_cargo.start()
+    run.begin(dqkv, w_head)
+    ffn_back.start()
+    pair.start()
+    run.halve_all(0, None)
+    run.halve_all(1, None)
+    ffn_back.middle()
+    run.halve_all(2, result8)
+
+    value = tokens[...].astype(f32)
+    factor = lax.rsqrt(jnp.mean(value * value, axis=-1, keepdims=True) + norm_eps)
+    upstream = result8[...]
+    scaled = upstream * gain[...]
+    mean = jnp.mean(scaled * value, axis=-1, keepdims=True)
+    grad = factor * scaled - value * (factor * factor * factor) * mean
+    input_low[...] = (grad_resid[...] + grad).astype(bf16)
+    input_cargo.start()
+    gain_one = jnp.sum(upstream * value * factor, axis=0, keepdims=True)
+    small_all[me] = small[...]
+    for i in range(width // head_width):
+        small_all[me, i : i + 1, :] = gain_one[:, i * head_width : (i + 1) * head_width]
+    small_cargo.start()
+    head_cargo.finish()
+    mine = pl.ds(pl.multiple_of(cube * half, half), half)
+    head_sum[...] = (head[mine, :].astype(f32) + head_land[...].astype(f32)).astype(bf16)
+    head_back.start()
+    small_cargo.finish()
+    small_all[me] = small_all[me] + small_land[...]
 
     def begin(mask, carry):
         send(me, me ^ mask).start()
         return carry
+
+    lax.fori_loop(1, group, begin, 0)
+    head_back.middle()
 
     def taken(mask, carry):
         send(me ^ mask, me).wait_recv()
         send(me, me ^ mask).wait_send()
         return carry
 
-    lax.fori_loop(1, 2 * group, begin, 0)
-    land[me] = small[...]
-    pair.start()
-    cargo.start()
-    first = Restore(ffn, ffn_land, lambda n: n >= 0, natural(columns), *ffn_sems)
-    column = lambda n: pl.multiple_of(head_of(n, heads) * head_width, head_width)
-    second = Restore(head, head_land, lambda n: is_active(n, heads), column, *head_sems)
-    second.start()
-    first.start()
-    lax.fori_loop(1, 2 * group, taken, 0)
-    result = land[0]
-    for number in range(1, 2 * group):
-        result = result + land[number]
+    lax.fori_loop(1, group, taken, 0)
+    result = small_all[0]
+    for number in range(1, group):
+        result = result + small_all[number]
     total_out[...] = result
-    second.finish()
-    for i in range(3):
-        outs[3 + i][...] = head_land[i].astype(f32)
-    first.finish()
-    for i in range(3):
-        outs[i][...] = ffn_land[i].astype(f32)
     pair.wait()
-    cargo.finish()
-
-
-def last_exchange(ffn, head, small, out_sum, output, heads, columns, collective_id):
-    rows, width = out_sum.shape
-    head_width = head.shape[1] // 3
-    hidden = columns * group
-    outs = [((rows, hidden), f32)] * 3 + [((rows, width), f32)] * 3
-    outs += [(small.shape, f32), (out_sum.shape, bf16), (output.shape, bf16)]
+    run.finish()
+    input_cargo.finish()
+    ffn_back.finish()
+    head_back.finish()
+
+
+def last_exchange(arrays, heads, head_width, columns, collective_id):
+    dqkv, w_head, tokens, gain, grad_resid, head, small, ffn_sum, out_sum = arrays
+    rows, width = tokens.shape
+    part = out_sum.shape[0]
+    half = (head.shape[0] // 2, head.shape[1])
+    outs = [
+        ((1, part, columns * group), bf16), ((3, part, width), bf16), (out_sum.shape, bf16),
+        (small.shape, f32), ((rows, width), bf16),
+    ]
+    memory = pltpu.VMEM
     return pl.pallas_call(
         functools.partial(last_kernel, heads, head_width, columns),
-        in_specs=[ANY, ANY, VMEM, ANY, ANY],
-        out_specs=[VMEM] * 7 + [ANY] * 2,
+        in_specs=[VMEM] * 7 + [ANY] * 2,
+        out_specs=[ANY, ANY, ANY, VMEM, ANY],
         out_shape=[jax.ShapeDtypeStruct(shape, kind) for shape, kind in outs],
-        scratch_shapes=Restore.scratch(3, rows, hidden) + Restore.scratch(3, rows, width) + [
-            pltpu.VMEM((2 * group,) + small.shape, f32), DMA((2 * group,)), DMA((2 * group,)),
-            DMA((2,)), DMA((2, 1)),
-        ],
+        scratch_shapes=[
+            memory((rows, width), f32), memory((rows, width), bf16),
+            memory((group,) + small.shape, f32), memory(small.shape, f32), memory(half, bf16), memory(half, bf16),
+            DMA((4, 2, 1)), DMA((2,)), DMA((group,)), DMA((group,)),
+        ]
+        + Scatter.scratch(rows, width) + Restore.scratch(1) + Restore.scratch(3),
         compiler_params=pltpu.CompilerParams(
             collective_id=collective_id, has_side_effects=True, vmem_limit_bytes=48 * 2**20
         ),
         cost_estimate=busy,
         name="last_exchange",
-    )(ffn, head, small, out_sum, output)
+    )(*arrays)
 
 
 def rotated(value, cosine, sine, inverse=False):
@@ -676,53 +752,42 @@
 ):
     step = pl.program_id(0)
     if share:
-        (w_one, w_two, w_rows, given), refs = refs[:4], refs[4:]
+        (w_one, w_two, w_rows), refs = refs[:3], refs[3:]
     q_ref, k_ref, v_ref, kt_ref, o1_ref, o2_ref, lse_ref, *refs = refs
     if share:
-        out_ref, both_ref, w_all, taken_ref = refs[:4]
-        qt_ref, vt_ref, att_ref, w_land, send_sem, recv_sem, local_sem, cargo_sem, *sems = refs[4:]
+        out_ref, both_ref, w_all = refs[:3]
+        qt_ref, vt_ref, att_ref, w_land, send_sem, recv_sem, local_sem, cargo_sem, *sems = refs[3:]
         me, cube = place()
-        columns = both_ref.shape[1] // 2
-        deal = Deal(
-            [
-                (w, both_ref.at[:, pl.ds(i * columns, columns)], natural(columns))
-                for i, w in enumerate((w_one, w_two))
-            ],
-            *sems[3:],
-        )
+        deal = gate_deal(w_one, w_two, both_ref, sems[3:])
         sub = w_land.shape[0]
         w_half = w_rows.at[pl.ds(pl.multiple_of(me // 8 * sub, sub), sub)]
 
         def spot(which):
             return lambda number: pl.multiple_of((which * 8 + number % 8) * (2 * sub) + number // 8 * sub, sub)
 
-        run = Gather([(w_half, w_all, spot(cube), 3), (w_land, w_all, spot(1 - cube), 3)], *sems[:3])
-        rows_cargo = Cargo([(w_half, w_land)], [], cargo_sem.at[0])
-        token_cargo = Cargo([], [(given, taken_ref)], cargo_sem.at[1])
+        run = Gather(few_z, [(w_half, w_all, spot(cube)), (w_land, w_all, spot(1 - cube))], *sems[:3])
+        rows_cargo = Cargo([(w_half, w_land)], [], cargo_sem)
 
         @pl.when(step == 0)
         def _():
             greet_all()
             rows_cargo.start()
             run.start([0])
-            token_cargo.start()
-            deal.start()
+            deal.start_near()
 
         @pl.when(step == 1)
         def _():
             rows_cargo.finish()
             run.start([1])
-            run.step(0, [0])
+            deal.start_far()
 
         @pl.when(step == 2)
         def _():
-            run.step(1, [0])
-            run.step(0, [1])
+            run.step(0)
 
         @pl.when(step == 3)
         def _():
-            run.step(2, [0])
-            run.step(1, [1])
+            run.step(1)
     else:
         att_ref, qt_ref, vt_ref = refs
     width = v_ref.shape[1]
@@ -826,10 +891,10 @@
             lax.fori_loop(0, heads, taken, 0)
             lax.fori_loop(0, group, sent, 0)
             pl.when(active)(lambda: keep().wait())
-            run.step(2, [1])
+            run.step(2)
             run.finish()
-            token_cargo.finish()
-            deal.finish()
+            deal.finish_near()
+            deal.finish_far()
 
 
 def forward_attention(lam, qkv, cosine, sine, gain, block, weights=(), rows=0, heads=0, columns=0, collective_id=None):
@@ -850,11 +915,11 @@
     share = bool(weights)
     if share:
         wide = heads * width
-        more = [((rows, wide), bf16), ((wide, 2 * columns), bf16), ((wide, wide), bf16), ((rows, wide), bf16)]
-        outs, out_specs = outs + more, out_specs + [ANY] * 4
+        more = [((rows, wide), bf16), ((wide, 2 * columns), bf16), ((wide, wide), bf16)]
+        outs, out_specs = outs + more, out_specs + [ANY] * 3
         scratch += [
             pltpu.VMEM((length, width), bf16), pltpu.VMEM((weights[2].shape[0] // 2, wide), bf16),
-            DMA((group,)), DMA((heads,)), DMA((1,)), DMA((2, 2, 1)),
+            DMA((group,)), DMA((heads,)), DMA((1,)), DMA((2, 1)),
         ]
         scratch += Gather.scratch(2) + Deal.scratch(2)
     else:
@@ -880,14 +945,19 @@
     cos_ref, sin_ref, gain_ref, *refs,
 ):
     if share:
-        cargo_in, refs = refs[0], refs[1:]
+        (left_ref, right_ref, cargo_in, given_ref, rows_ref), refs = refs[:5], refs[5:]
     dqkv_ref, dgain_ref, dlam_ref, *refs = refs
     if share:
-        cargo_out, refs = refs[0], refs[1:]
+        (part_ref, theirs_ref, cargo_out, taken_ref, back_ref), refs = refs[:5], refs[5:]
     dmix_ref, dmixt_ref, delta_ref, dqt_ref, *refs = refs
     if share:
-        cargo_sem, *refs = refs
-        cargo = cargo_refs((False,), 0, [cargo_in], [cargo_out], cargo_sem)
+        cargo_sem, part_sum, *refs = refs
+        run, back_sems, refs = Scatter(sum_few_z, *refs[:7]), refs[7:10], refs[10:]
+        back = Restore(rows_ref, back_ref, lambda n: n >= 0, natural(rows_ref.shape[1] // 2), *back_sems)
+        part_cargo = Cargo([(part_ref, theirs_ref)], [], cargo_sem.at[1])
+        cargo = Cargo(
+            [(for_partner(cargo_in, cargo_out.shape[0]), cargo_out)], [(given_ref, taken_ref)], cargo_sem.at[0]
+        )
     step = pl.program_id(0)
     blocks = pl.num_programs(0)
     width = v_ref.shape[1]
@@ -901,7 +971,14 @@
     def _():
         if share:
             greet_all()
-            collect(cargo, datt_ref, *refs)
+
+
+            def meanwhile():
+                run.begin(left_ref, right_ref)
+                cargo.start()
+                back.start()
+
+            collect(meanwhile, datt_ref, *refs)
         source = refs[0] if share else datt_ref
         dgain_ref[...] = jnp.zeros_like(dgain_ref)
         dlam_ref[...] = jnp.zeros_like(dlam_ref)
@@ -929,6 +1006,18 @@
             return carry
 
         lax.fori_loop(0, length // block, prepare, 0)
+
+    if share:
+        for i in range(3):
+
+            @pl.when(step == i + 1)
+            def _(i=i):
+                run.halve_all(i, part_sum)
+                if i == 0:
+                    back.middle()
+                if i == 2:
+                    part_ref[...] = part_sum[...].astype(bf16)
+                    part_cargo.start()
 
     own = pl.ds(pl.multiple_of(step * block, block), block)
     key_ids = lax.broadcasted_iota(jnp.int32, (block, block), 0)
@@ -981,10 +1070,16 @@
         rotated(jnp.where(used, dqt_ref[:, own] * scale, 0.0), cos_ref[:, own], sin_ref[:, own], True).T.astype(bf16)
     )
     if share:
-        pl.when(step == blocks - 1)(lambda: cargo.finish())
-
-
-def collect(cargo, grad_ref, out_ref, send_sem, recv_sem, local_sem):
+
+        @pl.when(step == blocks - 1)
+        def _():
+            run.finish()
+            cargo.finish()
+            part_cargo.finish()
+            back.finish()
+
+
+def collect(meanwhile, grad_ref, out_ref, send_sem, recv_sem, local_sem):
     me = place()[0]
     rows = grad_ref.shape[0]
     width = out_ref.shape[1]
@@ -1018,28 +1113,39 @@
 
     lax.fori_loop(0, heads, begin, 0)
     pl.when(active)(lambda: keep().start())
-    cargo.start()
+    meanwhile()
     lax.fori_loop(0, group, taken, 0)
     pl.when(active)(lambda: keep().wait())
     lax.fori_loop(0, heads, sent, 0)
 
 
-def backward_attention(lam, q, k, v, kt, o1, o2, lse, datt, cosine, sine, gain, block, cargo=None, collective_id=None):
+def backward_attention(lam, q, k, v, kt, o1, o2, lse, datt, cosine, sine, gain, block, extra=None, collective_id=None):
     length, width = q.shape
     full = lambda shape: pl.BlockSpec(shape, lambda i: (0,) * len(shape))
     arrays = (q, k, v, kt, o1, o2, lse, datt, cosine, sine, gain)
     outs = [((length, 3 * width), bf16), ((width, 1), f32), ((1, 1), f32)]
     share = collective_id is not None
-    more, cargo_out, cargo_in = [], [], []
+    more, more_out, more_in, more_specs, out_specs = [], [], [], [], []
     if share:
-        cargo_out, cargo_in = cargo_shapes([(cargo, False)], ()), [cargo]
-        more = [DMA((2, 1)), pltpu.VMEM((length, width), bf16), DMA((datt.shape[1] // width,)), DMA((group,)), DMA((1,))]
+        rows, wide = datt.shape
+        grads, part = extra[2], (extra[0].shape[0] // group, wide)
+        more_in, more_specs = list(extra), [full(a.shape) for a in extra[:2]] + [ANY] * 3
+        more_out = [
+            jax.ShapeDtypeStruct(part, bf16), jax.ShapeDtypeStruct(part, bf16),
+            jax.ShapeDtypeStruct((grads.shape[0] // 2, grads.shape[1]), bf16),
+            jax.ShapeDtypeStruct((rows, wide), bf16),
+            jax.ShapeDtypeStruct((2, part[0], extra[4].shape[1] // 2 * group), bf16),
+        ]
+        out_specs = [full(part), ANY, ANY, ANY, ANY]
+        more = [DMA((2, 2, 2)), pltpu.VMEM(part, f32)] + Scatter.scratch(*part) + Restore.scratch(2) + [
+            pltpu.VMEM((length, width), bf16), DMA((wide // width,)), DMA((group,)), DMA((1,)),
+        ]
     return pl.pallas_call(
         functools.partial(backward_kernel, block, share),
         grid=(length // block,),
-        in_specs=[SMEM] + [full(a.shape) for a in arrays] + [ANY] * len(cargo_in),
-        out_specs=[full(shape) for shape, _ in outs] + [ANY] * len(cargo_in),
-        out_shape=[jax.ShapeDtypeStruct(shape, kind) for shape, kind in outs] + cargo_out,
+        in_specs=[SMEM] + [full(a.shape) for a in arrays] + more_specs,
+        out_specs=[full(shape) for shape, _ in outs] + out_specs,
+        out_shape=[jax.ShapeDtypeStruct(shape, kind) for shape, kind in outs] + more_out,
         scratch_shapes=[
             pltpu.VMEM((length, width), bf16),
             pltpu.VMEM((width, length), bf16),
@@ -1052,7 +1158,7 @@
         ),
         cost_estimate=busy,
         name="attention_backward",
-    )(lam, *arrays, *cargo_in)
+    )(lam, *arrays, *more_in)
 
 
 def rms_parts(value):
@@ -1077,14 +1183,14 @@
     depth = w_query.shape[0]
     length = rows * group
     columns = hidden // group
-    y = lax.axis_index("batch")
     me, cube = place()
     my_head = head_of(me, heads)
     used = is_active(me, heads)
     active = used.astype(f32)
     here = jnp.broadcast_to(positions[0], (1, 8, rows))
-    tokens_low, normed_all, places, w_head = first_exchange(
-        block_input[0], here, norm_gain1[None], (w_query, w_key, w_value), heads, head_width, 0
+    tokens_low, normed_all, places, w_head, w_d = first_exchange(
+        block_input[0], here, norm_gain1[None], (w_query, w_key, w_value, w_down),
+        heads, head_width, columns, 0,
     )
     tokens = tokens_low.astype(f32)
     factor1 = rms_parts(tokens)
@@ -1101,14 +1207,14 @@
     block = 4 * rows
 
     qkv = dot(w_head, normed_all, 0, 1)
-    q, k, v, kt, o1, o2, lse, attended, w_gates, w_o, grad_low = forward_attention(
+    q, k, v, kt, o1, o2, lse, attended, w_gates, w_o = forward_attention(
         lam_mine, qkv, cosine, sine, gain_col, block,
-        (w_gate, w_up, w_out, upstream_low), rows, heads, columns, 1,
+        (w_gate, w_up, w_out), rows, heads, columns, 1,
     )
     resid = tokens + dot(attended, w_o)
     factor2 = rms_parts(resid)
     normed_two = (resid * factor2 * norm_gain2).astype(bf16)
-    two_all, grad_all, w_d = gather([normed_two, grad_low], (3, 3), w_down, columns, 2)
+    grad_low, two_all, grad_all = second_exchange(normed_two, upstream_low, 2)
 
     both = dot(two_all, w_gates)
     gate, upper = both[:, :columns], both[:, columns:]
@@ -1121,9 +1227,8 @@
     gates_low = jnp.concatenate([gate_low, upper_low], axis=1)
     gate_grads = dot(two_all, gates_low, 0, 0).astype(bf16)
     down_grads = dot(grad_all, inner, 0, 0).astype(bf16)
-    early = jnp.concatenate([gate_grads[:, :columns], down_grads[:, : columns // 2]], axis=1)
-    later = jnp.concatenate([gate_grads[:, columns:], down_grads[:, columns // 2 :]], axis=1)
-    grad_two, early_theirs = scatter(gates_low, w_gates, 3, [(early, False)])
+    grad_two, ffn_out, gate_theirs = scatter(gates_low, w_gates, inner, w_d, gate_grads, 3)
+    output_low = (resid + ffn_out).astype(bf16)
 
     grad_resid_two, gain_two = rms_back(resid, factor2, norm_gain2, grad_two)
     grad_resid = grad_low.astype(f32) + grad_resid_two
@@ -1131,43 +1236,41 @@
     grad_att = dot(resid_low, w_o, 1, 1).astype(bf16)
 
     def combine(mine, theirs):
-        part = mine.shape[0] // 2
+        part = theirs.shape[0]
         mine = lax.dynamic_slice_in_dim(mine, cube * part, part, 0)
         return (mine.astype(f32) + theirs.astype(f32)).astype(bf16)
 
-    dqkv, dgain, dlam, later_theirs = backward_attention(
-        lam_mine, q, k, v, kt, o1, o2, lse, grad_att, cosine, sine, gain_col, block, later, 4,
+    dqkv, dgain, dlam, out_part, out_theirs, down_theirs, output_back, gate_back = backward_attention(
+        lam_mine, q, k, v, kt, o1, o2, lse, grad_att, cosine, sine, gain_col, block,
+        (attended.T, resid_low.T, down_grads, output_low, combine(gate_grads, gate_theirs)), 4,
     )
     head_grads = dot(normed_all, dqkv, 0, 0).astype(bf16)
-    grad_normed, head_theirs = scatter(dqkv, w_head, 8, [(head_grads, False)])
-    grad_tokens, gain_one = rms_back(tokens, factor1, norm_gain1, grad_normed)
-    input_low = (grad_resid + grad_tokens).astype(bf16)
-    out_part, input_back = scatter(attended.T, resid_low.T, 7, [], [input_low])
-    out_part = out_part.astype(bf16)
-    ffn_out, out_theirs = scatter(inner, w_d, 5, [(out_part, True)])
-    output_low = (resid + ffn_out).astype(bf16)
+
+    hot = jax.nn.one_hot(my_head, heads, dtype=f32)
+    lines = width // head_width
+    small = jnp.concatenate([
+        jnp.zeros((lines, head_width), f32), gain_two.reshape(lines, head_width),
+        jnp.where(used, dgain[:, 0], 0.0)[None],
+        jnp.pad(jnp.where(used, hot * dlam[0, 0], 0.0), (0, head_width - heads))[None],
+    ])
+    small = jnp.pad(small, ((0, -small.shape[0] % 8), (0, 0)))
     out_sum = (out_part.astype(f32) + out_theirs.astype(f32)).astype(bf16)
-    early_sum, later_sum = combine(early, early_theirs), combine(later, later_theirs)
-    ffn_sum = jnp.concatenate(
-        [early_sum[:, :columns], later_sum[:, :columns], early_sum[:, columns:], later_sum[:, columns:]], axis=1
-    )
-
-    hot = jax.nn.one_hot(my_head, heads, dtype=f32)
-    mine = jnp.concatenate([dgain[:, 0], hot * dlam[0, 0]])
-    small = jnp.concatenate([gain_one, gain_two, jnp.where(used, mine, 0.0)])
-    count = small.shape[0]
-    lanes = -(-count // 1024) * 128
-    small = jnp.pad(small, (0, 8 * lanes - count)).reshape(8, lanes)
-    *grads, small, out_pair, output_back = last_exchange(
-        ffn_sum, combine(head_grads, head_theirs), small, out_sum, output_low, heads, columns, 6
-    )
-    small = small.reshape(-1)
+    down_back, head_back, out_pair, small, input_back = last_exchange(
+        (
+            dqkv, w_head, tokens_low, norm_gain1[None], grad_resid, head_grads, small,
+            combine(down_grads, down_theirs), out_sum,
+        ),
+        heads, head_width, columns, 5,
+    )
     output = output_back[None]
     input_grad = input_back.astype(f32)[None]
-    out_grads = jnp.where(y == cube, out_sum, out_pair).astype(f32)
-    gain_one, gain_two = small[:width], small[width : 2 * width]
-    sub_grad = small[2 * width : 2 * width + head_width]
-    lam_grads = lam_pull(small[2 * width + head_width : count])
+    out_grads = jnp.where(me // 8 == cube, out_sum, out_pair).astype(f32)
+    grads = [a.astype(f32) for a in (gate_back[0], gate_back[1], down_back[0])]
+    grads += [head_back[i].astype(f32) for i in range(3)]
+    gain_one = small[:lines].reshape(-1)
+    gain_two = small[lines : 2 * lines].reshape(-1)
+    sub_grad = small[2 * lines]
+    lam_grads = lam_pull(small[2 * lines + 1, :heads])
     squares = sum(jnp.sum(g * g) for g in lam_grads)
     return (
         output, input_grad, gain_one, grads[3], grads[4], grads[5],

time: 605 us -> 494 us (0.82)
  the two profiles are of different devices: /device:TPU:9 before, /device:TPU:0 now
where the time goes in v4:
time: 494 us; the launch traced here: 486 us
  Pallas kernels  408 us (83%)
  matrix products  36.6 us (7%)
  other arithmetic  23.9 us (5%)
  local copies, waits for them, and re-layouts  10.6 us (2%)
  between operations  7.17 us (1%)
    pallas_call x1, Pallas kernels, last_exchange(): pl.pallas_call(functools.partial(last_kernel, heads, head_width, columns)...  78.8 us
    pallas_call x1, Pallas kernels, scatter(): pl.pallas_call(scatter_kernel, in_specs=[VMEM] * 4 + [ANY], out_specs=[VM...  71.6 us
    pallas_call x1, Pallas kernels, backward_attention(): pl.pallas_call(functools.partial(backward_kernel, block, share), grid=(le...  69.9 us
    pallas_call x1, Pallas kernels, first_exchange(): pl.pallas_call(functools.partial(first_kernel, head_width, heads, columns...  68.7 us
    pallas_call x1, Pallas kernels, forward_attention(): pl.pallas_call(functools.partial(forward_kernel, block, share), grid=(len...  65.2 us
    pallas_call x1, Pallas kernels, second_exchange(): pl.pallas_call(second_kernel, in_specs=[ANY] * 2, out_specs=[ANY] * 3, ou...  53.8 us
    dot_general x8, matrix products, dot(): lax.dot_general(left, right, dims(left_axis, right_axis), preferred_eleme...  36.6 us

profile of v4, /device:TPU:0, one launch (start us, length us, event | category | flops | bytes accessed | tf_op | source)
XLA Modules:
  0.0 486.2 jit_solution(10394820435444004985)
XLA Ops:
  0.8 0.7 convert_bitcast_fusion.1
  1.4 0.5 pad.10.clone
  1.9 0.9 multiply_reduce_fusion.7
  2.8 0.0 copy-start.22
  2.8 0.5 copy-done.20
  3.3 0.6 fusion.4
  4.6 0.6 dynamic_slice.10
  5.2 1.2 pad_maximum_fusion.2.lam_ref
  6.4 1.2 broadcast_in_dim.47.places
  7.7 1.3 broadcast_in_dim.48.gain
  9.0 1.4 copy.44.gain_ref
  10.3 1.9 fusion.1.given
  12.2 68.7 %first_exchange.1 = (bf16[128,1536]{1,0:T(8,128)(2,1)}, bf16[2048,1536]{1,0:T(8,128)(2,1)}, s32[16,8,128]{2,1,0:T(8,128)}, bf16[1536,384]{1,0:T(8,128)(2,1)}, bf16[1536,256]{1,0:T(8,128)(2,1)}) custom-call(bf16[128,1536]{1,0:T(8,128)(2,1)} %bitcast.74, s32[1,8,128]{2,1,0:T(8,128)} %broadcast_in_dim.47.places, f32[1,1536]{1,0:T(1,128)} %broadcast_in_dim.48.gain, ...), custom_call_target="tpu_custom_call" | custom-call | flops 40000000000 | bytes 10000000 | tf_op jit(solution)/shard_map/first_exchange/pallas_call | solution.py:535
  80.9 0.8 slice_convert_fusion
  81.7 1.8 multiply_sine_fusion
  83.5 7.5 %fusion.5.qkv_ref = f32[384,2048]{1,0:T(8,128)} fusion(bf16[1536,384]{1,0:T(8,128)(2,1)} %get-tuple-element.52.w_head, bf16[2048,1536]{1,0:T(8,128)(2,1)} %get-tuple-element.53), kind=kOutput, calls=%fused_computation.64 | convolution fusion | flops 2415919104 | bytes 10616832 | tf_op jit(solution)/shard_map/dot_general | solution.py:32
  91.0 65.2 %attention_forward.1 = (bf16[2048,128]{1,0:T(8,128)(2,1)}, bf16[2048,128]{1,0:T(8,128)(2,1)}, bf16[2048,128]{1,0:T(8,128)(2,1)}, bf16[128,2048]{1,0:T(8,128)(2,1...) custom-call(f32[2]{0:T(128)} %pad_maximum_fusion.2.lam_ref, ...), custom_call_target="tpu_custom_call" | custom-call | flops 40000000000 | bytes 10000000 | tf_op jit(solution)/shard_map/attention_forward/pallas_call | solution.py:927
  156.3 1.9 copy.49
  158.2 3.3 multiply_reduce_fusion.2
  161.6 0.9 multiply_convert_fusion.3.normed
  162.4 53.8 %second_exchange.1 = (bf16[128,1536]{1,0:T(8,128)(2,1)}, bf16[2048,1536]{1,0:T(8,128)(2,1)}, bf16[2048,1536]{1,0:T(8,128)(2,1)}) custom-call(bf16[128,1536]{1,0:T(8,128)(2,1)} %multiply_convert_fusion.3.normed, bf16[128,1536]{1,0:T(8,128)(2,1)} %fusion.1.given), custom_call_target="tpu_custom_call" | custom-call | flops 40000000000 | bytes 10000000 | tf_op jit(solution)/shard_map/second_exchange/pallas_call | solution.py:251
  216.2 0.0 copy-done.27
  216.3 0.0 copy-start.25
  216.3 0.0 copy-start.28
  216.3 0.0 slice-start.2
  216.3 5.6 %fusion.6 = f32[2048,512]{1,0:T(8,128)S(1)} fusion(bf16[2048,1536]{1,0:T(8,128)(2,1)} %get-tuple-element.68, bf16[1536,512]{1,0:T(8,128)(2,1)S(1)} %copy-done.27), kind=kOutput, calls=%fused_computation.65 | convolution fusion | flops 3221225472 | bytes 12058624 | tf_op jit(solution)/shard_map/dot_general | solution.py:32
  221.9 0.0 slice-start.3
  221.9 2.5 multiply_convert_fusion.2
  224.4 0.0 copy-start.26
  224.4 2.7 convolution_convert_fusion.2.refs_2_
  227.1 0.0 slice-done.2
  227.2 4.7 convolution_convert_fusion.given
  231.8 1.5 pad_maximum_fusion.lhs
  233.4 71.6 %scatter3.1 = (f32[128,1536]{1,0:T(8,128)}, f32[128,1536]{1,0:T(8,128)}, bf16[768,512]{1,0:T(8,128)(2,1)}) custom-call(bf16[2048,512]{1,0:T(8,128)(2,1)} %pad_maximum_fusion.lhs, bf16[1536,512]{1,0:T(8,128)(2,1)} %get-tuple-element.69.rhs, bf16[2048,256]{1,0:T(8,128)(2,1)} %copy-done.26, bf16[1536,256]{1,0:T(8,128)(2,1)} %get-tuple-element.67.rhs_two, ...), custom_call_target="tpu_custom_call" | custom-call | flops 40000000000 | bytes 10000000 | tf_op jit(solution)/shard_map/scatter3/pallas_call | solution.py:394
  305.0 2.4 add_convert_fusion.refs_4_
  307.4 0.9 multiply_reduce_fusion
  308.3 0.0 copy-done.8
  308.3 0.3 convert_bitcast_fusion
  308.6 2.4 convolution_convert_fusion.3.datt_ref
  311.0 0.9 copy.51.refs_1_
  312.0 69.9 %attention_backward.1 = (bf16[2048,384]{1,0:T(8,128)(2,1)}, f32[128,1]{1,0:T(8,128)}, f32[1,1]{1,0:T(1,128)}, bf16[96,1536]{1,0:T(8,128)(2,1)}, bf16[96,1536]{1,...) custom-call(f32[2]{0:T(128)} %pad_maximum_fusion.2.lam_ref, ...), custom_call_target="tpu_custom_call" | custom-call | flops 40000000000 | bytes 10000000 | tf_op jit(solution)/shard_map/attention_backward/pallas_call | solution.py:1143
  381.9 0.0 copy-start.13
  381.9 0.0 copy-start.15
  381.9 0.0 copy-start.24
  381.9 7.8 %convolution_convert_fusion.1.head = bf16[1536,384]{1,0:T(8,128)(2,1)} fusion(bf16[2048,1536]{1,0:T(8,128)(2,1)} %get-tuple-element.53, bf16[2048,384]{1,0:T(8,128)(2,1)} %get-tuple-element.74.dqkv), kind=kOutput, calls=%fused_computation.1 | convolution fusion | flops 2416508928 | bytes 9043968 | tf_op jit(solution)/shard_map/dot_general | solution.py:32
  389.8 0.7 broadcast_select_fusion
  390.5 0.1 add_convert_fusion.1.ffn_sum
  390.6 0.1 select_reduce_fusion
  390.8 0.1 pad_maximum_fusion.1
  390.9 0.1 add_convert_fusion.3.out_sum
  391.0 0.2 copy-done.3
  391.2 0.0 copy-start.18
  391.2 0.0 copy-start.19
  391.2 78.8 %last_exchange.1 = (bf16[1,96,4096]{2,1,0:T(8,128)(2,1)S(1)}, bf16[3,96,1536]{2,1,0:T(8,128)(2,1)S(1)}, bf16[96,1536]{1,0:T(8,128)(2,1)S(1)}, f32[32,128]{1,0:T(8,128)S(1)}, bf16[128,1536]{1,0:T(8,128)(2,1)S(1)}) custom-call(bf16[2048,384]{1,0:T(8,128)(2,1)} %get-tuple-element.74.dqkv, bf16[1536,384]{1,0:T(8,128)(2,1)S(1)} %copy-done.3, ...), custom_call_target="tpu_custom_call" | custom-call | flops 40000000000 | bytes 10000000 | tf_op jit(solution)/shard_map/last_exchange/pallas_call | solution.py:719
  470.1 0.5 slice_bitcast_fusion.2
  470.6 0.6 slice_bitcast_fusion
  471.2 1.3 multiply_reduce_fusion.3
  472.5 1.3 multiply_reduce_fusion.5
  476.4 0.9 select_convert_fusion
  477.2 1.0 bitcast_convert_fusion.3
  478.2 1.3 bitcast_convert_fusion
  479.5 1.3 bitcast_convert_fusion.4
  480.7 2.0 bitcast_convert_fusion.1
  482.8 0.7 copy.55
  (59 shorter events, 0.1 us)
Async XLA Ops:
  2.8 0.5 copy-start.20
  2.8 1.1 copy-start.22
  91.0 67.2 %copy-start = (bf16[128,1536]{1,0:T(8,128)(2,1)S(1)}, bf16[128,1536]{1,0:T(8,128)(2,1)}, u32[]{:S(2)}) copy-start(bf16[128,1536]{1,0:T(8,128)(2,1)} %get-tuple-element.62.tokens) | copy-start | bytes 1179652
  158.2 3.4 copy-start.14
  162.4 53.8 %copy-start.27 = (bf16[1536,512]{1,0:T(8,128)(2,1)S(1)}, bf16[1536,512]{1,0:T(8,128)(2,1)}, u32[]{:S(2)}) copy-start(bf16[1536,512]{1,0:T(8,128)(2,1)} %get-tuple-element.69.rhs) | copy-start | bytes 4718596
  216.3 5.7 %copy-start.25 = (bf16[2048,1536]{1,0:T(8,128)(2,1)S(1)}, bf16[2048,1536]{1,0:T(8,128)(2,1)}, u32[]{:S(2)}) copy-start(bf16[2048,1536]{1,0:T(8,128)(2,1)} %get-tuple-element.66) | copy-start | bytes 18874372
  216.3 5.7 %copy-start.28 = (bf16[1536,256]{1,0:T(8,128)(2,1)S(1)}, bf16[1536,256]{1,0:T(8,128)(2,1)}, u32[]{:S(2)}) copy-start(bf16[1536,256]{1,0:T(8,128)(2,1)} %get-tuple-element.67.rhs_two) | copy-start | bytes 2359300
  216.3 10.9 %slice-start.2 = ((s8[6291456]{0:T(1024)(128)(4,1)}), s8[4194304]{0:T(1024)(128)(4,1)S(1)}, s32[]{:S(2)}) async-start(s8[6291456]{0:T(1024)(128)(4,1)} %bitcast.75), calls=%async_computation.2 | async-start | bytes 8388608
  221.9 5.2 %slice-start.3 = ((s8[6291456]{0:T(1024)(128)(4,1)}), s8[2097152]{0:T(1024)(128)(4,1)S(1)}, s32[]{:S(2)}) async-start(s8[6291456]{0:T(1024)(128)(4,1)} %bitcast.75), calls=%async_computation.3 | async-start | bytes 4194304
  224.4 2.7 copy-start.26
  231.8 76.8 %slice-start = ((s8[4718592]{0:T(1024)(128)(4,1)}), s8[4194304]{0:T(1024)(128)(4,1)S(1)}, s32[]{:S(2)}) async-start(s8[4718592]{0:T(1024)(128)(4,1)} %bitcast.65), calls=%async_computation | async-start | bytes 8388608
  233.4 71.6 %copy-start.7 = (bf16[1536,512]{1,0:T(8,128)(2,1)S(1)}, bf16[1536,512]{1,0:T(8,128)(2,1)}, u32[]{:S(2)}) copy-start(bf16[1536,512]{1,0:T(8,128)(2,1)} %convolution_convert_fusion.given) | copy-start | bytes 4718596
  233.4 75.3 %slice-start.1 = ((s8[4718592]{0:T(1024)(128)(4,1)}), s8[524288]{0:T(1024)(128)(4,1)S(1)}, s32[]{:S(2)}) async-start(s8[4718592]{0:T(1024)(128)(4,1)} %bitcast.65), calls=%async_computation.1 | async-start | bytes 1048576
  305.0 2.4 copy-start.4
  305.0 2.4 copy-start.6
  305.0 3.3 copy-start.8
  381.9 8.6 %copy-start.10 = (bf16[768,256]{1,0:T(8,128)(2,1)S(1)}, bf16[768,256]{1,0:T(8,128)(2,1)}, u32[]{:S(2)}) copy-start(bf16[768,256]{1,0:T(8,128)(2,1)} %get-tuple-element.77) | copy-start | bytes 1179652
  381.9 8.6 %copy-start.13 = (bf16[1536,256]{1,0:T(8,128)(2,1)S(1)}, bf16[1536,256]{1,0:T(8,128)(2,1)}, u32[]{:S(2)}) copy-start(bf16[1536,256]{1,0:T(8,128)(2,1)} %convolution_convert_fusion.2.refs_2_) | copy-start | bytes 2359300
  381.9 8.8 %copy-start.15 = (f32[128,1]{1,0:T(8,128)S(1)}, f32[128,1]{1,0:T(8,128)}, u32[]{:S(2)}) copy-start(f32[128,1]{1,0:T(8,128)} %get-tuple-element.75) | copy-start | bytes 1540
  381.9 8.9 %copy-start.24 = (f32[26]{0:T(128)S(1)}, f32[26]{0:T(128)}, u32[]{:S(2)}) copy-start(f32[26]{0:T(128)} %pad.10.clone) | copy-start | bytes 316
  381.9 8.9 %copy-start.11 = (bf16[96,1536]{1,0:T(8,128)(2,1)S(1)}, bf16[96,1536]{1,0:T(8,128)(2,1)}, u32[]{:S(2)}) copy-start(bf16[96,1536]{1,0:T(8,128)(2,1)} %get-tuple-element.78) | copy-start | bytes 884740
  381.9 8.9 %copy-start.12 = (bf16[96,1536]{1,0:T(8,128)(2,1)S(1)}, bf16[96,1536]{1,0:T(8,128)(2,1)}, u32[]{:S(2)}) copy-start(bf16[96,1536]{1,0:T(8,128)(2,1)} %get-tuple-element.79) | copy-start | bytes 884740
  389.8 1.2 copy-start.1
  389.8 1.2 copy-start.2
  389.8 1.4 copy-start.3
  391.2 78.9 %copy-start.21 = (f32[12]{0:T(128)S(1)}, f32[12]{0:T(128)}, u32[]{:S(2)}) copy-start(f32[12]{0:T(128)} %copy-done.20) | copy-start | bytes 148
  391.2 78.9 %copy-start.23 = (f32[12]{0:T(128)S(1)}, f32[12]{0:T(128)}, u32[]{:S(2)}) copy-start(f32[12]{0:T(128)} %copy-done.22) | copy-start | bytes 148
  391.2 80.0 %copy-start.16 = (f32[12,64]{1,0:T(8,128)S(1)}, f32[12,64]{1,0:T(8,128)}, u32[]{:S(2)}) copy-start(f32[12,64]{1,0:T(8,128)} %param.28) | copy-start | bytes 9220
  391.2 80.0 %copy-start.17 = (f32[12,64]{1,0:T(8,128)S(1)}, f32[12,64]{1,0:T(8,128)}, u32[]{:S(2)}) copy-start(f32[12,64]{1,0:T(8,128)} %param.29) | copy-start | bytes 9220
  391.2 81.3 %copy-start.18 = (f32[12,64]{1,0:T(8,128)S(1)}, f32[12,64]{1,0:T(8,128)}, u32[]{:S(2)}) copy-start(f32[12,64]{1,0:T(8,128)} %param.26) | copy-start | bytes 9220
  391.2 81.3 %copy-start.19 = (f32[12,64]{1,0:T(8,128)S(1)}, f32[12,64]{1,0:T(8,128)}, u32[]{:S(2)}) copy-start(f32[12,64]{1,0:T(8,128)} %param.27) | copy-start | bytes 9220
  478.2 2.5 copy-start.5
  480.7 2.0 copy-start.9

commit v5 on v4

--- a/solution.py
+++ b/solution.py
@@ -300,13 +300,16 @@
             self.side_s.at[part, slot], self.side_r.at[part, slot], peer,
         )
 
-    def multiply(self, part, lhs, rhs):
+    def multiply(self, part, lhs, rhs, axis=1):
         c = self.cols(part)
         chunk = 4 * self.rows
 
         def quarter(q, carry):
-            left = lhs[pl.ds(pl.multiple_of(q * chunk, chunk), chunk), :]
-            p = dot(left, rhs[part * self.part : (part + 1) * self.part, :], 1, 1)
+            at = pl.ds(pl.multiple_of(q * chunk, chunk), chunk)
+            if axis:
+                p = dot(lhs[at, :], rhs[part * self.part : (part + 1) * self.part, :], 1, 1)
+            else:
+                p = dot(lhs[:, at], rhs[:, part * self.part : (part + 1) * self.part], 0, 0)
             p = p.astype(bf16).reshape(4, self.rows, self.part)
             for j in range(4):
                 self.own[j % 2, 2 * q + j // 2, :, c] = p[j]
@@ -331,10 +334,10 @@
             number = self.me ^ mask ^ self.order(part)[0]
             self.add(number, part, self.core_in[number // 2, :, c])
 
-    def begin(self, lhs, rhs):
-        self.multiply(0, lhs, rhs)
+    def begin(self, lhs, rhs, axis=1):
+        self.multiply(0, lhs, rhs, axis)
         for part in range(1, self.parts):
-            self.multiply(part, lhs, rhs)
+            self.multiply(part, lhs, rhs, axis)
             self.merge(part - 1)
         self.merge(self.parts - 1)
 
@@ -374,36 +377,61 @@
     return grads.at[pl.ds(pl.multiple_of((1 - place()[1]) * rows, rows), rows)]
 
 
-def scatter_kernel(lhs, rhs, lhs_two, rhs_two, given, out, out_two, taken, cargo_sem, *scratch):
+def weight_grads(left, right, out):
+    chunk = 512
+
+    def some(j, carry):
+        at = pl.ds(pl.multiple_of(j * chunk, chunk), chunk)
+        out[at, :] = dot(left[:, at], right[...], 0, 0).astype(bf16)
+        return carry
+
+    lax.fori_loop(0, left.shape[1] // chunk, some, 0)
+
+
+def scatter_kernel(
+    lhs, rhs, lhs_two, rhs_two, left, left_two, out, out_two, grads, grads_two, taken,
+    cargo_sem, copy_sem, held, held_two, *scratch,
+):
     greet(cross=True)
-    cargo = Cargo([(for_partner(given, taken.shape[0]), taken)], [], cargo_sem)
+    cargo = Cargo([(for_partner(grads, taken.shape[0]), taken)], [], cargo_sem)
+    copies = [pltpu.make_async_copy(a, b, copy_sem.at[i]) for i, (a, b) in enumerate(((left, held), (left_two, held_two)))]
+    for copy in copies:
+        copy.start()
     run, more = Scatter(sum_even, *scratch[:7]), Scatter(sum_even, *scratch[7:])
     run.begin(lhs, rhs)
     more.begin(lhs_two, rhs_two)
+    copies[0].wait()
+    weight_grads(held, lhs, grads)
     cargo.start()
     for step in range(3):
         run.halve_all(step, out)
         more.halve_all(step, out_two)
+        if step == 0:
+            copies[1].wait()
+            weight_grads(held_two, lhs_two, grads_two)
     run.finish()
     more.finish()
     cargo.finish()
 
 
-def scatter(lhs, rhs, lhs_two, rhs_two, given, collective_id):
+def scatter(lhs, rhs, lhs_two, rhs_two, left, left_two, collective_id):
     rows, width = lhs.shape[0] // group, rhs.shape[0]
     return pl.pallas_call(
         scatter_kernel,
-        in_specs=[VMEM] * 4 + [ANY],
-        out_specs=[VMEM, VMEM, ANY],
+        in_specs=[VMEM] * 4 + [ANY] * 2,
+        out_specs=[VMEM] * 4 + [ANY],
         out_shape=[jax.ShapeDtypeStruct((rows, width), f32)] * 2
-        + [jax.ShapeDtypeStruct((given.shape[0] // 2, given.shape[1]), bf16)],
-        scratch_shapes=[DMA((2, 1))] + Scatter.scratch(rows, width) + Scatter.scratch(rows, width),
+        + [
+            jax.ShapeDtypeStruct((width, lhs.shape[1]), bf16), jax.ShapeDtypeStruct((width, lhs_two.shape[1]), bf16),
+            jax.ShapeDtypeStruct((width // 2, lhs.shape[1]), bf16),
+        ],
+        scratch_shapes=[DMA((2, 1)), DMA((2,)), pltpu.VMEM(left.shape, bf16), pltpu.VMEM(left.shape, bf16)] + Scatter.scratch(rows, width) + Scatter.scratch(rows, width),
         compiler_params=pltpu.CompilerParams(
-            collective_id=collective_id, has_side_effects=True, vmem_limit_bytes=56 * 2**20
+            collective_id=collective_id, has_side_effects=True, vmem_limit_bytes=60 * 2**20
         ),
         cost_estimate=busy,
         name=f"scatter{collective_id}",
-    )(lhs, rhs, lhs_two, rhs_two, given)
+    )(lhs, rhs, lhs_two, rhs_two, left, left_two)
 
 
 def head_of(number, heads):
@@ -752,11 +780,12 @@
 ):
     step = pl.program_id(0)
     if share:
-        (w_one, w_two, w_rows), refs = refs[:3], refs[3:]
+        (w_one, w_two, w_rows, normed), refs = refs[:4], refs[4:]
     q_ref, k_ref, v_ref, kt_ref, o1_ref, o2_ref, lse_ref, *refs = refs
     if share:
         out_ref, both_ref, w_all = refs[:3]
-        qt_ref, vt_ref, att_ref, w_land, send_sem, recv_sem, local_sem, cargo_sem, *sems = refs[3:]
+        qt_ref, vt_ref, att_ref, w_land, held, send_sem, recv_sem, local_sem, cargo_sem, *sems = refs[3:]
+        copy = pltpu.make_async_copy(normed, held, local_sem.at[1])
         me, cube = place()
         deal = gate_deal(w_one, w_two, both_ref, sems[3:])
         sub = w_land.shape[0]
@@ -770,6 +799,7 @@
 
         @pl.when(step == 0)
         def _():
+            copy.start()
             greet_all()
             rows_cargo.start()
             run.start([0])
@@ -800,9 +830,10 @@
         def prepare(index, carry):
             cols = pl.ds(pl.multiple_of(index * block, block), block)
             cosine, sine = cos_ref[:, cols], sin_ref[:, cols]
-            query = rotated(qkv_ref[0:width, cols], cosine, sine)
-            key = rotated(qkv_ref[width : 2 * width, cols], cosine, sine)
-            value = qkv_ref[2 * width : 3 * width, cols]
+            qkv = dot(held[cols, :], qkv_ref[...]).T if share else qkv_ref[:, cols]
+            query = rotated(qkv[0:width], cosine, sine)
+            key = rotated(qkv[width : 2 * width], cosine, sine)
+            value = qkv[2 * width : 3 * width]
             qt_ref[:, cols] = query.astype(bf16)
             kt_ref[:, cols] = key.astype(bf16)
             vt_ref[:, cols] = value.astype(bf16)
@@ -811,6 +842,8 @@
             v_ref[cols, :] = value.T.astype(bf16)
             return carry
 
+        if share:
+            copy.wait()
         lax.fori_loop(0, length // block, prepare, 0)
 
     own = pl.ds(pl.multiple_of(step * block, block), block)
@@ -898,8 +931,7 @@
 
 
 def forward_attention(lam, qkv, cosine, sine, gain, block, weights=(), rows=0, heads=0, columns=0, collective_id=None):
-    width = qkv.shape[0] // 3
-    length = qkv.shape[1]
+    width, length = gain.shape[0], cosine.shape[1]
     full = lambda shape: pl.BlockSpec(shape, lambda i: (0,) * len(shape))
     outs = [
         ((length, width), bf16),
@@ -919,7 +951,7 @@
         outs, out_specs = outs + more, out_specs + [ANY] * 3
         scratch += [
             pltpu.VMEM((length, width), bf16), pltpu.VMEM((weights[2].shape[0] // 2, wide), bf16),
-            DMA((group,)), DMA((heads,)), DMA((1,)), DMA((2, 1)),
+            pltpu.VMEM(weights[3].shape, bf16), DMA((group,)), DMA((heads,)), DMA((2,)), DMA((2, 1)),
         ]
         scratch += Gather.scratch(2) + Deal.scratch(2)
     else:
@@ -945,13 +977,14 @@
     cos_ref, sin_ref, gain_ref, *refs,
 ):
     if share:
-        (left_ref, right_ref, cargo_in, given_ref, rows_ref), refs = refs[:5], refs[5:]
+        (left_ref, right_ref, cargo_in, given_ref, rows_ref, normed), refs = refs[:6], refs[6:]
     dqkv_ref, dgain_ref, dlam_ref, *refs = refs
     if share:
-        (part_ref, theirs_ref, cargo_out, taken_ref, back_ref), refs = refs[:5], refs[5:]
+        (part_ref, theirs_ref, cargo_out, taken_ref, back_ref, head_ref), refs = refs[:6], refs[6:]
     dmix_ref, dmixt_ref, delta_ref, dqt_ref, *refs = refs
     if share:
-        cargo_sem, part_sum, *refs = refs
+        cargo_sem, held_sem, held, part_sum, *refs = refs
+        copy = pltpu.make_async_copy(normed, held, held_sem.at[0])
         run, back_sems, refs = Scatter(sum_few_z, *refs[:7]), refs[7:10], refs[10:]
         back = Restore(rows_ref, back_ref, lambda n: n >= 0, natural(rows_ref.shape[1] // 2), *back_sems)
         part_cargo = Cargo([(part_ref, theirs_ref)], [], cargo_sem.at[1])
@@ -974,9 +1007,10 @@
 
 
             def meanwhile():
-                run.begin(left_ref, right_ref)
+                run.begin(left_ref, right_ref, 0)
                 cargo.start()
                 back.start()
+                copy.start()
 
             collect(meanwhile, datt_ref, *refs)
         source = refs[0] if share else datt_ref
@@ -1073,6 +1107,8 @@
 
         @pl.when(step == blocks - 1)
         def _():
+            copy.wait()
+            weight_grads(held, dqkv_ref, head_ref)
             run.finish()
             cargo.finish()
             part_cargo.finish()
@@ -1128,16 +1164,17 @@
     more, more_out, more_in, more_specs, out_specs = [], [], [], [], []
     if share:
         rows, wide = datt.shape
-        grads, part = extra[2], (extra[0].shape[0] // group, wide)
-        more_in, more_specs = list(extra), [full(a.shape) for a in extra[:2]] + [ANY] * 3
+        grads, part = extra[2], (wide // group, wide)
+        more_in, more_specs = list(extra), [full(a.shape) for a in extra[:2]] + [ANY] * 4
         more_out = [
             jax.ShapeDtypeStruct(part, bf16), jax.ShapeDtypeStruct(part, bf16),
             jax.ShapeDtypeStruct((grads.shape[0] // 2, grads.shape[1]), bf16),
             jax.ShapeDtypeStruct((rows, wide), bf16),
             jax.ShapeDtypeStruct((2, part[0], extra[4].shape[1] // 2 * group), bf16),
+            jax.ShapeDtypeStruct((wide, 3 * width), bf16),
         ]
-        out_specs = [full(part), ANY, ANY, ANY, ANY]
-        more = [DMA((2, 2, 2)), pltpu.VMEM(part, f32)] + Scatter.scratch(*part) + Restore.scratch(2) + [
+        out_specs = [full(part), ANY, ANY, ANY, ANY, full((wide, 3 * width))]
+        more = [DMA((2, 2, 2)), DMA((1,)), pltpu.VMEM(extra[5].shape, bf16), pltpu.VMEM(part, f32)] + Scatter.scratch(*part) + Restore.scratch(2) + [
             pltpu.VMEM((length, width), bf16), DMA((wide // width,)), DMA((group,)), DMA((1,)),
         ]
     return pl.pallas_call(
@@ -1206,10 +1243,9 @@
     gain_col = sub_gain[:, None]
     block = 4 * rows
 
-    qkv = dot(w_head, normed_all, 0, 1)
     q, k, v, kt, o1, o2, lse, attended, w_gates, w_o = forward_attention(
-        lam_mine, qkv, cosine, sine, gain_col, block,
-        (w_gate, w_up, w_out), rows, heads, columns, 1,
+        lam_mine, w_head, cosine, sine, gain_col, block,
+        (w_gate, w_up, w_out, normed_all), rows, heads, columns, 1,
     )
     resid = tokens + dot(attended, w_o)
     factor2 = rms_parts(resid)
@@ -1225,9 +1261,9 @@
     gate_low = (grad_inner * upper * sigma * (1.0 + gate * (1.0 - sigma))).astype(bf16)
     upper_low = (grad_inner * silu).astype(bf16)
     gates_low = jnp.concatenate([gate_low, upper_low], axis=1)
-    gate_grads = dot(two_all, gates_low, 0, 0).astype(bf16)
-    down_grads = dot(grad_all, inner, 0, 0).astype(bf16)
-    grad_two, ffn_out, gate_theirs = scatter(gates_low, w_gates, inner, w_d, gate_grads, 3)
+    grad_two, ffn_out, gate_grads, down_grads, gate_theirs = scatter(
+        gates_low, w_gates, inner, w_d, two_all, grad_all, 3
+    )
     output_low = (resid + ffn_out).astype(bf16)
 
     grad_resid_two, gain_two = rms_back(resid, factor2, norm_gain2, grad_two)
@@ -1240,12 +1276,10 @@
         mine = lax.dynamic_slice_in_dim(mine, cube * part, part, 0)
         return (mine.astype(f32) + theirs.astype(f32)).astype(bf16)
 
-    dqkv, dgain, dlam, out_part, out_theirs, down_theirs, output_back, gate_back = backward_attention(
+    dqkv, dgain, dlam, out_part, out_theirs, down_theirs, output_back, gate_back, head_grads = backward_attention(
         lam_mine, q, k, v, kt, o1, o2, lse, grad_att, cosine, sine, gain_col, block,
-        (attended.T, resid_low.T, down_grads, output_low, combine(gate_grads, gate_theirs)), 4,
-    )
-    head_grads = dot(normed_all, dqkv, 0, 0).astype(bf16)
-
+        (attended, resid_low, down_grads, output_low, combine(gate_grads, gate_theirs), normed_all), 4,
+    )
     hot = jax.nn.one_hot(my_head, heads, dtype=f32)
     lines = width // head_width
     small = jnp.concatenate([

time: 494 us -> 467 us (0.945); the launches traced: 486 us -> 466 us
  matrix products: 36.6 us -> 17.3 us
    dot_general x8 -> x4, matrix products: 36.6 us -> 17.3 us  [dot(): lax.dot_general(left, right, dims(left_axis, right_axis), preferred_eleme...]
where the time goes in v5:
time: 467 us; the launch traced here: 466 us
  Pallas kernels  408 us (87%)
  other arithmetic  26.2 us (6%)
  matrix products  17.3 us (4%)
  local copies, waits for them, and re-layouts  7.52 us (2%)
  between operations  6.67 us (1%)
    pallas_call x1, Pallas kernels, last_exchange(): pl.pallas_call(functools.partial(last_kernel, heads, head_width, columns)...  79.5 us
    pallas_call x1, Pallas kernels, scatter(): pl.pallas_call(scatter_kernel, in_specs=[VMEM] * 4 + [ANY] * 2, out_specs...  71.2 us
    pallas_call x1, Pallas kernels, backward_attention(): pl.pallas_call(functools.partial(backward_kernel, block, share), grid=(le...  70.5 us
    pallas_call x1, Pallas kernels, first_exchange(): pl.pallas_call(functools.partial(first_kernel, head_width, heads, columns...  68.7 us
    pallas_call x1, Pallas kernels, forward_attention(): pl.pallas_call(functools.partial(forward_kernel, block, share), grid=(len...  64.6 us
    pallas_call x1, Pallas kernels, second_exchange(): pl.pallas_call(second_kernel, in_specs=[ANY] * 2, out_specs=[ANY] * 3, ou...  53.9 us
    dot_general x4, matrix products, dot(): lax.dot_general(left, right, dims(left_axis, right_axis), preferred_eleme...  17.3 us

profile of v5, /device:TPU:0, one launch (start us, length us, event | category | flops | bytes accessed | tf_op | source)
XLA Modules:
  0.0 466.1 jit_solution(7453758164159570371)
XLA Ops:
  0.8 0.7 convert_bitcast_fusion
  1.4 0.5 pad.10.clone
  1.9 0.9 multiply_reduce_fusion.7
  2.8 0.0 copy-start.18
  2.8 0.5 copy-done.16
  3.3 0.6 fusion.3
  3.9 0.0 copy-done.18
  4.6 0.6 dynamic_slice.10
  5.2 1.2 pad_maximum_fusion.2.lam_ref
  6.4 1.2 broadcast_in_dim.47.places
  7.7 1.3 broadcast_in_dim.48.gain
  9.0 1.4 copy.42.gain_ref
  10.3 1.9 fusion.1.given
  12.2 68.7 %first_exchange.1 = (bf16[128,1536]{1,0:T(8,128)(2,1)}, bf16[2048,1536]{1,0:T(8,128)(2,1)}, s32[16,8,128]{2,1,0:T(8,128)}, bf16[1536,384]{1,0:T(8,128)(2,1)}, bf16[1536,256]{1,0:T(8,128)(2,1)}) custom-call(bf16[128,1536]{1,0:T(8,128)(2,1)} %bitcast.62, s32[1,8,128]{2,1,0:T(8,128)} %broadcast_in_dim.47.places, f32[1,1536]{1,0:T(1,128)} %broadcast_in_dim.48.gain, ...), custom_call_target="tpu_custom_call" | custom-call | flops 40000000000 | bytes 10000000 | tf_op jit(solution)/shard_map/first_exchange/pallas_call | solution.py:563
  80.9 0.8 slice_convert_fusion
  81.7 1.8 multiply_sine_fusion
  83.5 64.6 %attention_forward.1 = (bf16[2048,128]{1,0:T(8,128)(2,1)}, bf16[2048,128]{1,0:T(8,128)(2,1)}, bf16[2048,128]{1,0:T(8,128)(2,1)}, bf16[128,2048]{1,0:T(8,128)(2,1...) custom-call(f32[2]{0:T(128)} %pad_maximum_fusion.2.lam_ref, ...), custom_call_target="tpu_custom_call" | custom-call | flops 40000000000 | bytes 10000000 | tf_op jit(solution)/shard_map/attention_forward/pallas_call | solution.py:959
  148.2 0.0 copy-done
  148.2 0.0 copy-start.11
  148.2 3.3 multiply_reduce_fusion.2
  151.5 0.0 copy-done.11
  151.5 0.9 multiply_convert_fusion.3.normed
  152.4 53.9 %second_exchange.1 = (bf16[128,1536]{1,0:T(8,128)(2,1)}, bf16[2048,1536]{1,0:T(8,128)(2,1)}, bf16[2048,1536]{1,0:T(8,128)(2,1)}) custom-call(bf16[128,1536]{1,0:T(8,128)(2,1)} %multiply_convert_fusion.3.normed, bf16[128,1536]{1,0:T(8,128)(2,1)} %fusion.1.given), custom_call_target="tpu_custom_call" | custom-call | flops 40000000000 | bytes 10000000 | tf_op jit(solution)/shard_map/second_exchange/pallas_call | solution.py:251
  206.4 0.0 copy-done.22
  206.4 0.0 copy-start.21
  206.4 0.0 copy-start.23
  206.4 5.6 %fusion.5 = f32[2048,512]{1,0:T(8,128)S(1)} fusion(bf16[2048,1536]{1,0:T(8,128)(2,1)} %get-tuple-element.71.left, bf16[1536,512]{1,0:T(8,128)(2,1)S(1)} %copy-done.22), kind=kOutput, calls=%fused_computation.60 | convolution fusion | flops 3221225472 | bytes 12058624 | tf_op jit(solution)/shard_map/dot_general | solution.py:32
  212.0 0.0 copy-done.21
  212.0 0.0 copy-done.23
  212.1 3.4 multiply_convert_fusion.2
  215.5 1.6 pad_maximum_fusion.lhs
  217.0 71.2 %scatter3.1 = (f32[128,1536]{1,0:T(8,128)}, f32[128,1536]{1,0:T(8,128)}, bf16[1536,512]{1,0:T(8,128)(2,1)}, bf16[1536,256]{1,0:T(8,128)(2,1)}, bf16[768,512]{1,0:T(8,128)(2,1)}) custom-call(bf16[2048,512]{1,0:T(8,128)(2,1)} %pad_maximum_fusion.lhs, bf16[1536,512]{1,0:T(8,128)(2,1)} %get-tuple-element.72.rhs, bf16[2048,256]{1,0:T(8,128)(2,1)} %get-tuple-element.108.lhs_two, ...), custom_call_target="tpu_custom_call" | custom-call | flops 40000000000 | bytes 10000000 | tf_op jit(solution)/shard_map/scatter3/pallas_call | solution.py:419
  288.3 2.4 multiply_reduce_fusion
  290.7 0.0 copy-done.3
  290.7 0.3 fusion.4
  291.0 0.0 copy-start.5
  291.0 4.9 %convolution_convert_fusion.datt_ref = bf16[128,1536]{1,0:T(8,128)(2,1)} fusion(bf16[128,1536]{1,0:T(8,128)(2,1)S(1)} %get-tuple-element.104.refs_1_, bf16[1536,1536]{1,0:T(8,128)(2,1)} %get-tuple-element.67), kind=kOutput, calls=%fused_computation.1 | convolution fusion | flops 604176384 | bytes 5505024 | tf_op jit(solution)/shard_map/dot_general | solution.py:32
  295.9 0.0 copy-done.6
  295.9 1.1 add_convert_fusion.refs_4_
  297.0 70.5 %attention_backward.1 = (bf16[2048,384]{1,0:T(8,128)(2,1)}, f32[128,1]{1,0:T(8,128)}, f32[1,1]{1,0:T(1,128)}, bf16[96,1536]{1,0:T(8,128)(2,1)}, bf16[96,1536]{1,...) custom-call(f32[2]{0:T(128)} %pad_maximum_fusion.2.lam_ref, ...), custom_call_target="tpu_custom_call" | custom-call | flops 40000000000 | bytes 10000000 | tf_op jit(solution)/shard_map/attention_backward/pallas_call | solution.py:1180
  367.5 0.0 copy-start.1
  367.5 0.8 broadcast_select_fusion
  368.3 1.1 add_convert_fusion.1.ffn_sum
  369.4 0.1 select_reduce_fusion
  369.5 0.0 copy-done.20
  369.6 0.1 pad_maximum_fusion.1
  369.6 1.1 add_convert_fusion.3.out_sum
  370.8 0.0 copy-start.17
  370.8 0.0 copy-start.19
  370.8 0.0 copy-start.12
  370.8 0.0 copy-start.13
  370.8 0.0 copy-start.14
  370.8 0.0 copy-start.15
  370.9 79.5 %last_exchange.1 = (bf16[1,96,4096]{2,1,0:T(8,128)(2,1)S(1)}, bf16[3,96,1536]{2,1,0:T(8,128)(2,1)S(1)}, bf16[96,1536]{1,0:T(8,128)(2,1)S(1)}, f32[32,128]{1,0:T(8,128)S(1)}, bf16[128,1536]{1,0:T(8,128)(2,1)S(1)}) custom-call(bf16[2048,384]{1,0:T(8,128)(2,1)} %get-tuple-element.79.dqkv, bf16[1536,384]{1,0:T(8,128)(2,1)S(1)} %copy-done.2, ...), custom_call_target="tpu_custom_call" | custom-call | flops 40000000000 | bytes 10000000 | tf_op jit(solution)/shard_map/last_exchange/pallas_call | solution.py:747
  450.4 0.5 slice_bitcast_fusion.2
  450.9 0.6 slice_bitcast_fusion
  451.5 1.3 multiply_reduce_fusion.3
  452.8 1.3 multiply_reduce_fusion.5
  456.7 0.9 select_convert_fusion
  457.6 1.0 bitcast_convert_fusion.3
  458.5 1.3 bitcast_convert_fusion
  459.8 1.3 bitcast_convert_fusion.4
  461.1 2.0 bitcast_convert_fusion.1
  463.1 0.7 copy.51
  (33 shorter events, 0.1 us)
Async XLA Ops:
  2.8 0.5 copy-start.16
  2.8 1.1 copy-start.18
  83.5 64.6 %copy-start = (bf16[128,1536]{1,0:T(8,128)(2,1)S(1)}, bf16[128,1536]{1,0:T(8,128)(2,1)}, u32[]{:S(2)}) copy-start(bf16[128,1536]{1,0:T(8,128)(2,1)} %get-tuple-element.65.tokens) | copy-start | bytes 1179652
  148.2 3.4 copy-start.11
  152.4 54.0 %copy-start.22 = (bf16[1536,512]{1,0:T(8,128)(2,1)S(1)}, bf16[1536,512]{1,0:T(8,128)(2,1)}, u32[]{:S(2)}) copy-start(bf16[1536,512]{1,0:T(8,128)(2,1)} %get-tuple-element.72.rhs) | copy-start | bytes 4718596
  206.4 5.7 %copy-start.21 = (bf16[2048,1536]{1,0:T(8,128)(2,1)S(1)}, bf16[2048,1536]{1,0:T(8,128)(2,1)}, u32[]{:S(2)}) copy-start(bf16[2048,1536]{1,0:T(8,128)(2,1)} %get-tuple-element.69.left_two) | copy-start | bytes 18874372
  206.4 5.7 %copy-start.23 = (bf16[1536,256]{1,0:T(8,128)(2,1)S(1)}, bf16[1536,256]{1,0:T(8,128)(2,1)}, u32[]{:S(2)}) copy-start(bf16[1536,256]{1,0:T(8,128)(2,1)} %get-tuple-element.70.rhs_two) | copy-start | bytes 2359300
  288.3 2.4 copy-start.3
  288.3 2.4 copy-start.8
  291.0 4.9 %copy-start.5 = (bf16[128,1536]{1,0:T(8,128)(2,1)}, bf16[128,1536]{1,0:T(8,128)(2,1)S(1)}, u32[]{:S(2)}) copy-start(bf16[128,1536]{1,0:T(8,128)(2,1)S(1)} %get-tuple-element.104.refs_1_) | copy-start | bytes 1179652
  291.0 4.9 %copy-start.6 = (bf16[768,512]{1,0:T(8,128)(2,1)S(1)}, bf16[768,512]{1,0:T(8,128)(2,1)}, u32[]{:S(2)}) copy-start(bf16[768,512]{1,0:T(8,128)(2,1)} %get-tuple-element.77) | copy-start | bytes 2359300
  291.0 4.9 %copy-start.7 = (bf16[1536,512]{1,0:T(8,128)(2,1)S(1)}, bf16[1536,512]{1,0:T(8,128)(2,1)}, u32[]{:S(2)}) copy-start(bf16[1536,512]{1,0:T(8,128)(2,1)} %get-tuple-element.76) | copy-start | bytes 4718596
  297.0 71.3 %copy-start.10 = (bf16[1536,256]{1,0:T(8,128)(2,1)S(1)}, bf16[1536,256]{1,0:T(8,128)(2,1)}, u32[]{:S(2)}) copy-start(bf16[1536,256]{1,0:T(8,128)(2,1)} %get-tuple-element.74.refs_2_) | copy-start | bytes 2359300
  297.0 72.5 %copy-start.20 = (f32[26]{0:T(128)S(1)}, f32[26]{0:T(128)}, u32[]{:S(2)}) copy-start(f32[26]{0:T(128)} %pad.10.clone) | copy-start | bytes 316
  367.5 3.3 copy-start.1
  367.5 3.3 copy-start.2
  370.8 79.6 %copy-start.17 = (f32[12]{0:T(128)S(1)}, f32[12]{0:T(128)}, u32[]{:S(2)}) copy-start(f32[12]{0:T(128)} %copy-done.16) | copy-start | bytes 148
  370.8 79.6 %copy-start.19 = (f32[12]{0:T(128)S(1)}, f32[12]{0:T(128)}, u32[]{:S(2)}) copy-start(f32[12]{0:T(128)} %copy-done.18) | copy-start | bytes 148
  370.8 80.7 %copy-start.12 = (f32[12,64]{1,0:T(8,128)S(1)}, f32[12,64]{1,0:T(8,128)}, u32[]{:S(2)}) copy-start(f32[12,64]{1,0:T(8,128)} %param.28) | copy-start | bytes 9220
  370.8 80.7 %copy-start.13 = (f32[12,64]{1,0:T(8,128)S(1)}, f32[12,64]{1,0:T(8,128)}, u32[]{:S(2)}) copy-start(f32[12,64]{1,0:T(8,128)} %param.29) | copy-start | bytes 9220
  370.8 82.0 %copy-start.14 = (f32[12,64]{1,0:T(8,128)S(1)}, f32[12,64]{1,0:T(8,128)}, u32[]{:S(2)}) copy-start(f32[12,64]{1,0:T(8,128)} %param.26) | copy-start | bytes 9220
  370.8 82.0 %copy-start.15 = (f32[12,64]{1,0:T(8,128)S(1)}, f32[12,64]{1,0:T(8,128)}, u32[]{:S(2)}) copy-start(f32[12,64]{1,0:T(8,128)} %param.27) | copy-start | bytes 9220
  458.5 2.5 copy-start.4
  461.1 2.0 copy-start.9

commit v6 on v5

--- a/solution.py
+++ b/solution.py
@@ -306,7 +306,10 @@
 
         def quarter(q, carry):
             at = pl.ds(pl.multiple_of(q * chunk, chunk), chunk)
-            if axis:
+            if isinstance(lhs, tuple):
+                rows, k = slice(part * self.part, (part + 1) * self.part), lhs[0].shape[1]
+                p = dot(lhs[0][at, :], rhs[rows, :k], 1, 1) + dot(lhs[1][at, :], rhs[rows, k:], 1, 1)
+            elif axis:
                 p = dot(lhs[at, :], rhs[part * self.part : (part + 1) * self.part, :], 1, 1)
             else:
                 p = dot(lhs[:, at], rhs[:, part * self.part : (part + 1) * self.part], 0, 0)
@@ -377,19 +380,19 @@
     return grads.at[pl.ds(pl.multiple_of((1 - place()[1]) * rows, rows), rows)]
 
 
-def weight_grads(left, right, out):
-    chunk = 512
+def weight_grads(left, right, out, start=0):
+    chunk, width = 512, right.shape[1]
 
     def some(j, carry):
         at = pl.ds(pl.multiple_of(j * chunk, chunk), chunk)
-        out[at, :] = dot(left[:, at], right[...], 0, 0).astype(bf16)
+        out[at, start : start + width] = dot(left[:, at], right[...], 0, 0).astype(bf16)
         return carry
 
     lax.fori_loop(0, left.shape[1] // chunk, some, 0)
 
 
 def scatter_kernel(
-    lhs, rhs, lhs_two, rhs_two, left, left_two, out, out_two, grads, grads_two, taken,
+    gate, upper, rhs, lhs_two, rhs_two, left, left_two, out, out_two, grads, grads_two, taken,
     cargo_sem, copy_sem, held, held_two, *scratch,
 ):
     greet(cross=True)
@@ -398,10 +401,11 @@
     for copy in copies:
         copy.start()
     run, more = Scatter(sum_even, *scratch[:7]), Scatter(sum_even, *scratch[7:])
-    run.begin(lhs, rhs)
+    run.begin((gate, upper), rhs)
     more.begin(lhs_two, rhs_two)
     copies[0].wait()
-    weight_grads(held, lhs, grads)
+    weight_grads(held, gate, grads)
+    weight_grads(held, upper, grads, gate.shape[1])
     cargo.start()
     for step in range(3):
         run.halve_all(step, out)
@@ -414,16 +418,16 @@
     cargo.finish()
 
 
-def scatter(lhs, rhs, lhs_two, rhs_two, left, left_two, collective_id):
-    rows, width = lhs.shape[0] // group, rhs.shape[0]
+def scatter(gate, upper, rhs, lhs_two, rhs_two, left, left_two, collective_id):
+    rows, width = gate.shape[0] // group, rhs.shape[0]
     return pl.pallas_call(
         scatter_kernel,
-        in_specs=[VMEM] * 4 + [ANY] * 2,
+        in_specs=[VMEM] * 5 + [ANY] * 2,
         out_specs=[VMEM] * 4 + [ANY],
         out_shape=[jax.ShapeDtypeStruct((rows, width), f32)] * 2
         + [
-            jax.ShapeDtypeStruct((width, lhs.shape[1]), bf16), jax.ShapeDtypeStruct((width, lhs_two.shape[1]), bf16),
-            jax.ShapeDtypeStruct((width // 2, lhs.shape[1]), bf16),
+            jax.ShapeDtypeStruct(rhs.shape, bf16), jax.ShapeDtypeStruct((width, lhs_two.shape[1]), bf16),
+            jax.ShapeDtypeStruct((width // 2, rhs.shape[1]), bf16),
         ],
         scratch_shapes=[DMA((2, 1)), DMA((2,)), pltpu.VMEM(left.shape, bf16), pltpu.VMEM(left.shape, bf16)] + Scatter.scratch(rows, width) + Scatter.scratch(rows, width),
         compiler_params=pltpu.CompilerParams(
@@ -431,7 +435,7 @@
         ),
         cost_estimate=busy,
         name=f"scatter{collective_id}",
-    )(lhs, rhs, lhs_two, rhs_two, left, left_two)
+    )(gate, upper, rhs, lhs_two, rhs_two, left, left_two)
 
 
 def head_of(number, heads):
@@ -1260,9 +1264,8 @@
     inner = (silu * upper).astype(bf16)
     gate_low = (grad_inner * upper * sigma * (1.0 + gate * (1.0 - sigma))).astype(bf16)
     upper_low = (grad_inner * silu).astype(bf16)
-    gates_low = jnp.concatenate([gate_low, upper_low], axis=1)
     grad_two, ffn_out, gate_grads, down_grads, gate_theirs = scatter(
-        gates_low, w_gates, inner, w_d, two_all, grad_all, 3
+        gate_low, upper_low, w_gates, inner, w_d, two_all, grad_all, 3
     )
     output_low = (resid + ffn_out).astype(bf16)
 

time: 467 us -> 466 us (level)
  no operation moved by 1% of the time
where the time goes in v6:
time: 466 us; the launch traced here: 465 us
  Pallas kernels  408 us (88%)
  other arithmetic  24.6 us (5%)
  matrix products  18 us (4%)
  local copies, waits for them, and re-layouts  7.51 us (2%)
  between operations  6.67 us (1%)
    pallas_call x1, Pallas kernels, last_exchange(): pl.pallas_call(functools.partial(last_kernel, heads, head_width, columns)...  79.4 us
    pallas_call x1, Pallas kernels, scatter(): pl.pallas_call(scatter_kernel, in_specs=[VMEM] * 5 + [ANY] * 2, out_specs...  71.3 us
    pallas_call x1, Pallas kernels, backward_attention(): pl.pallas_call(functools.partial(backward_kernel, block, share), grid=(le...  70.5 us
    pallas_call x1, Pallas kernels, first_exchange(): pl.pallas_call(functools.partial(first_kernel, head_width, heads, columns...  68.7 us
    pallas_call x1, Pallas kernels, forward_attention(): pl.pallas_call(functools.partial(forward_kernel, block, share), grid=(len...  64.7 us
    pallas_call x1, Pallas kernels, second_exchange(): pl.pallas_call(second_kernel, in_specs=[ANY] * 2, out_specs=[ANY] * 3, ou...  53.9 us
    dot_general x4, matrix products, dot(): lax.dot_general(left, right, dims(left_axis, right_axis), preferred_eleme...  18 us

profile of v6, /device:TPU:0, one launch (start us, length us, event | category | flops | bytes accessed | tf_op | source)
XLA Modules:
  0.0 465.2 jit_solution(17038652884632909723)
XLA Ops:
  0.8 0.7 convert_bitcast_fusion
  1.4 0.5 pad.10.clone
  1.9 0.9 multiply_reduce_fusion.7
  2.8 0.0 copy-start.18
  2.8 0.5 copy-done.16
  3.3 0.6 fusion.3
  3.9 0.0 copy-done.18
  4.6 0.6 dynamic_slice.10
  5.2 1.2 pad_maximum_fusion.1.lam_ref
  6.4 1.2 broadcast_in_dim.47.places
  7.7 1.3 broadcast_in_dim.48.gain
  9.0 1.4 copy.38.gain_ref
  10.3 1.9 fusion.1.given
  12.2 68.7 %first_exchange.1 = (bf16[128,1536]{1,0:T(8,128)(2,1)}, bf16[2048,1536]{1,0:T(8,128)(2,1)}, s32[16,8,128]{2,1,0:T(8,128)}, bf16[1536,384]{1,0:T(8,128)(2,1)}, bf16[1536,256]{1,0:T(8,128)(2,1)}) custom-call(bf16[128,1536]{1,0:T(8,128)(2,1)} %bitcast.62, s32[1,8,128]{2,1,0:T(8,128)} %broadcast_in_dim.47.places, f32[1,1536]{1,0:T(1,128)} %broadcast_in_dim.48.gain, ...), custom_call_target="tpu_custom_call" | custom-call | flops 40000000000 | bytes 10000000 | tf_op jit(solution)/shard_map/first_exchange/pallas_call | solution.py:567
  80.9 0.8 slice_convert_fusion
  81.7 1.8 multiply_sine_fusion
  83.5 64.7 %attention_forward.1 = (bf16[2048,128]{1,0:T(8,128)(2,1)}, bf16[2048,128]{1,0:T(8,128)(2,1)}, bf16[2048,128]{1,0:T(8,128)(2,1)}, bf16[128,2048]{1,0:T(8,128)(2,1...) custom-call(f32[2]{0:T(128)} %pad_maximum_fusion.1.lam_ref, ...), custom_call_target="tpu_custom_call" | custom-call | flops 40000000000 | bytes 10000000 | tf_op jit(solution)/shard_map/attention_forward/pallas_call | solution.py:963
  148.2 0.0 copy-done
  148.2 0.0 copy-start.11
  148.2 3.3 multiply_reduce_fusion.2
  151.6 0.0 copy-done.11
  151.6 0.9 multiply_convert_fusion.3.normed
  152.5 53.9 %second_exchange.1 = (bf16[128,1536]{1,0:T(8,128)(2,1)}, bf16[2048,1536]{1,0:T(8,128)(2,1)}, bf16[2048,1536]{1,0:T(8,128)(2,1)}) custom-call(bf16[128,1536]{1,0:T(8,128)(2,1)} %multiply_convert_fusion.3.normed, bf16[128,1536]{1,0:T(8,128)(2,1)} %fusion.1.given), custom_call_target="tpu_custom_call" | custom-call | flops 40000000000 | bytes 10000000 | tf_op jit(solution)/shard_map/second_exchange/pallas_call | solution.py:251
  206.4 0.0 copy-done.22
  206.4 0.0 copy-start.21
  206.4 0.0 copy-start.23
  206.4 5.6 %fusion.5 = f32[2048,512]{1,0:T(8,128)S(1)} fusion(bf16[2048,1536]{1,0:T(8,128)(2,1)} %get-tuple-element.71.left, bf16[1536,512]{1,0:T(8,128)(2,1)S(1)} %copy-done.22), kind=kOutput, calls=%fused_computation.59 | convolution fusion | flops 3221225472 | bytes 12058624 | tf_op jit(solution)/shard_map/dot_general | solution.py:32
  212.1 4.1 multiply_convert_fusion.1
  216.2 71.3 %scatter3.1 = (f32[128,1536]{1,0:T(8,128)}, f32[128,1536]{1,0:T(8,128)}, bf16[1536,512]{1,0:T(8,128)(2,1)}, bf16[1536,256]{1,0:T(8,128)(2,1)}, bf16[768,512]{1,0:T(8,128)(2,1)}) custom-call(bf16[2048,256]{1,0:T(8,128)(2,1)} %get-tuple-element.107.gate, bf16[2048,256]{1,0:T(8,128)(2,1)} %get-tuple-element.106.upper, bf16[1536,512]{1,0:T(8,128)(2,1)} %get-tuple-element.72.rhs, ...), custom_call_target="tpu_custom_call" | custom-call | flops 40000000000 | bytes 10000000 | tf_op jit(solution)/shard_map/scatter3/pallas_call | solution.py:423
  287.5 0.0 copy-start.3
  287.5 0.0 copy-start.8
  287.5 2.4 multiply_reduce_fusion
  289.9 0.0 copy-done.3
  289.9 0.3 fusion.4
  290.2 0.0 copy-start.5
  290.2 4.9 %convolution_convert_fusion.datt_ref = bf16[128,1536]{1,0:T(8,128)(2,1)} fusion(bf16[128,1536]{1,0:T(8,128)(2,1)S(1)} %get-tuple-element.104.refs_1_, bf16[1536,1536]{1,0:T(8,128)(2,1)} %get-tuple-element.67), kind=kOutput, calls=%fused_computation.1 | convolution fusion | flops 604176384 | bytes 5505024 | tf_op jit(solution)/shard_map/dot_general | solution.py:32
  295.1 1.1 add_convert_fusion.refs_4_
  296.2 70.5 %attention_backward.1 = (bf16[2048,384]{1,0:T(8,128)(2,1)}, f32[128,1]{1,0:T(8,128)}, f32[1,1]{1,0:T(1,128)}, bf16[96,1536]{1,0:T(8,128)(2,1)}, bf16[96,1536]{1,...) custom-call(f32[2]{0:T(128)} %pad_maximum_fusion.1.lam_ref, ...), custom_call_target="tpu_custom_call" | custom-call | flops 40000000000 | bytes 10000000 | tf_op jit(solution)/shard_map/attention_backward/pallas_call | solution.py:1184
  366.7 0.0 copy-start.1
  366.7 0.7 broadcast_select_fusion
  367.5 1.1 add_convert_fusion.1.ffn_sum
  368.6 0.1 select_reduce_fusion
  368.7 0.1 pad_maximum_fusion
  368.8 1.1 add_convert_fusion.3.out_sum
  370.0 0.0 copy-start.17
  370.0 0.0 copy-start.19
  370.0 0.0 copy-start.12
  370.0 0.0 copy-start.13
  370.0 0.0 copy-start.14
  370.0 0.0 copy-start.15
  370.0 79.4 %last_exchange.1 = (bf16[1,96,4096]{2,1,0:T(8,128)(2,1)S(1)}, bf16[3,96,1536]{2,1,0:T(8,128)(2,1)S(1)}, bf16[96,1536]{1,0:T(8,128)(2,1)S(1)}, f32[32,128]{1,0:T(8,128)S(1)}, bf16[128,1536]{1,0:T(8,128)(2,1)S(1)}) custom-call(bf16[2048,384]{1,0:T(8,128)(2,1)} %get-tuple-element.79.dqkv, bf16[1536,384]{1,0:T(8,128)(2,1)S(1)} %copy-done.2, ...), custom_call_target="tpu_custom_call" | custom-call | flops 40000000000 | bytes 10000000 | tf_op jit(solution)/shard_map/last_exchange/pallas_call | solution.py:751
  449.5 0.5 slice_bitcast_fusion.2
  450.0 0.6 slice_bitcast_fusion
  450.6 0.0 copy-done.13
  450.6 1.3 multiply_reduce_fusion.3
  451.9 0.0 copy-done.15
  451.9 1.3 multiply_reduce_fusion.5
  455.8 0.9 select_convert_fusion
  456.7 1.0 bitcast_convert_fusion.3
  457.7 1.3 bitcast_convert_fusion
  458.9 1.3 bitcast_convert_fusion.4
  460.2 2.0 bitcast_convert_fusion.1
  462.2 0.0 copy-done.9
  462.2 0.7 copy.41
  (32 shorter events, 0.1 us)
Async XLA Ops:
  2.8 0.5 copy-start.16
  2.8 1.1 copy-start.18
  83.5 64.7 %copy-start = (bf16[128,1536]{1,0:T(8,128)(2,1)S(1)}, bf16[128,1536]{1,0:T(8,128)(2,1)}, u32[]{:S(2)}) copy-start(bf16[128,1536]{1,0:T(8,128)(2,1)} %get-tuple-element.65.tokens) | copy-start | bytes 1179652
  148.2 3.4 copy-start.11
  152.5 54.0 %copy-start.22 = (bf16[1536,512]{1,0:T(8,128)(2,1)S(1)}, bf16[1536,512]{1,0:T(8,128)(2,1)}, u32[]{:S(2)}) copy-start(bf16[1536,512]{1,0:T(8,128)(2,1)} %get-tuple-element.72.rhs) | copy-start | bytes 4718596
  206.4 5.7 %copy-start.21 = (bf16[2048,1536]{1,0:T(8,128)(2,1)S(1)}, bf16[2048,1536]{1,0:T(8,128)(2,1)}, u32[]{:S(2)}) copy-start(bf16[2048,1536]{1,0:T(8,128)(2,1)} %get-tuple-element.69.left_two) | copy-start | bytes 18874372
  206.4 5.7 %copy-start.23 = (bf16[1536,256]{1,0:T(8,128)(2,1)S(1)}, bf16[1536,256]{1,0:T(8,128)(2,1)}, u32[]{:S(2)}) copy-start(bf16[1536,256]{1,0:T(8,128)(2,1)} %get-tuple-element.70.rhs_two) | copy-start | bytes 2359300
  287.5 2.4 copy-start.3
  287.5 2.4 copy-start.8
  290.2 4.9 %copy-start.5 = (bf16[128,1536]{1,0:T(8,128)(2,1)}, bf16[128,1536]{1,0:T(8,128)(2,1)S(1)}, u32[]{:S(2)}) copy-start(bf16[128,1536]{1,0:T(8,128)(2,1)S(1)} %get-tuple-element.104.refs_1_) | copy-start | bytes 1179652
  290.2 4.9 %copy-start.6 = (bf16[768,512]{1,0:T(8,128)(2,1)S(1)}, bf16[768,512]{1,0:T(8,128)(2,1)}, u32[]{:S(2)}) copy-start(bf16[768,512]{1,0:T(8,128)(2,1)} %get-tuple-element.77) | copy-start | bytes 2359300
  290.2 4.9 %copy-start.7 = (bf16[1536,512]{1,0:T(8,128)(2,1)S(1)}, bf16[1536,512]{1,0:T(8,128)(2,1)}, u32[]{:S(2)}) copy-start(bf16[1536,512]{1,0:T(8,128)(2,1)} %get-tuple-element.76) | copy-start | bytes 4718596
  296.2 71.2 %copy-start.10 = (bf16[1536,256]{1,0:T(8,128)(2,1)S(1)}, bf16[1536,256]{1,0:T(8,128)(2,1)}, u32[]{:S(2)}) copy-start(bf16[1536,256]{1,0:T(8,128)(2,1)} %get-tuple-element.74.refs_2_) | copy-start | bytes 2359300
  296.2 72.5 %copy-start.20 = (f32[26]{0:T(128)S(1)}, f32[26]{0:T(128)}, u32[]{:S(2)}) copy-start(f32[26]{0:T(128)} %pad.10.clone) | copy-start | bytes 316
  366.7 3.2 copy-start.1
  366.7 3.2 copy-start.2
  370.0 79.5 %copy-start.17 = (f32[12]{0:T(128)S(1)}, f32[12]{0:T(128)}, u32[]{:S(2)}) copy-start(f32[12]{0:T(128)} %copy-done.16) | copy-start | bytes 148
  370.0 79.5 %copy-start.19 = (f32[12]{0:T(128)S(1)}, f32[12]{0:T(128)}, u32[]{:S(2)}) copy-start(f32[12]{0:T(128)} %copy-done.18) | copy-start | bytes 148
  370.0 80.7 %copy-start.12 = (f32[12,64]{1,0:T(8,128)S(1)}, f32[12,64]{1,0:T(8,128)}, u32[]{:S(2)}) copy-start(f32[12,64]{1,0:T(8,128)} %param.28) | copy-start | bytes 9220
  370.0 80.7 %copy-start.13 = (f32[12,64]{1,0:T(8,128)S(1)}, f32[12,64]{1,0:T(8,128)}, u32[]{:S(2)}) copy-start(f32[12,64]{1,0:T(8,128)} %param.29) | copy-start | bytes 9220
  370.0 81.9 %copy-start.14 = (f32[12,64]{1,0:T(8,128)S(1)}, f32[12,64]{1,0:T(8,128)}, u32[]{:S(2)}) copy-start(f32[12,64]{1,0:T(8,128)} %param.26) | copy-start | bytes 9220
  370.0 81.9 %copy-start.15 = (f32[12,64]{1,0:T(8,128)S(1)}, f32[12,64]{1,0:T(8,128)}, u32[]{:S(2)}) copy-start(f32[12,64]{1,0:T(8,128)} %param.27) | copy-start | bytes 9220
  457.7 2.5 copy-start.4
  460.2 2.0 copy-start.9
